TPU v7x, 32 devices: a whole 2x2x4 slice. The times are simulated.
32 devices in a mesh: wide: 16 (over z, x, core), grp: 2 (over y).
Axes of the slice: x: 2, y: 2, z: 4, core: 2. Of those that a mesh axis runs over, the one named last changes fastest.
Arguments:
- tokens: bfloat16 [2, 32, 196, 768], P(None, ('wide', 'grp')), may hold values from -6 to 6
- cotangent: bfloat16 [2, 32, 196, 768], P(None, ('wide', 'grp')), may hold values from -6 to 6
- window_place: int32 [2, 32], P(None, ('wide', 'grp')), may hold values from 0 to 25
- master: float32 [55424, 128], P('grp'), may hold values from -2 to 2
- first_moment: float32 [55424, 128], P('grp'), may hold values from -3 to 3
- second_moment: float32 [55424, 128], P('grp'), may hold values from 0.05 to 1
Outputs:
- block_out: bfloat16 [2, 32, 196, 768], P(None, ('wide', 'grp'))
- input_grad: bfloat16 [2, 32, 196, 768], P(None, ('wide', 'grp'))
- grads: float32 [55424, 128], P('grp')
- master_next: float32 [55424, 128], P('grp')
- moment_next: float32 [55424, 128], P('grp')
- second_next: float32 [55424, 128], P('grp')
- weights_next: bfloat16 [55424, 128], replicated
- proj_bias_grad: float32 [768], replicated
Inputs may be any that keep to these rules, and one draw needn't show every extreme that they name: `window_place`: place of a slot's window in its image's grid of 5 x 5 windows of 14 x 14 tokens, row by row, over the 64 x 64 token grid zero-padded at its ends; 25 marks an empty slot.
All inputs are finite; a program needn't handle non-finite values.
Results may differ from a plain program's by a relative error of at most 0.018.
Values may be sent and summed in bfloat16 or wider, within the bound.
No kernel may reach another device: no remote copies, remote signals or barrier semaphores. Data moves between devices by JAX's collectives and lax.ppermute only.
A program may use at most 320 MiB of HBM per device.

v0:
```python
import math

import jax
import jax.numpy as jnp
from jax import lax
from jax.sharding import PartitionSpec as P

FF = 3072
HD = 64
WS = 14
GRID = 64
ADAM_STEP = 10


HIGHEST = lax.Precision.HIGHEST
EPS_NORM = 1e-06
BETA_ONE = 0.9
BETA_TWO = 0.95
ADAM_EPS = 1e-08
LEARN_RATE = 0.02
DECAY_RATE = 0.1


def layout(feature):
    rel_span = 2 * WS - 1
    return [
        (feature, 3 * feature),
        (2 * feature,),
        (feature, feature),
        (feature,),
        (feature, FF),
        (FF,),
        (FF, feature),
        (feature,),
        (feature,),
        (feature,),
        (feature,),
        (feature,),
        (rel_span, HD),
        (rel_span, HD),
    ]


def unpack(flat_vec, feature):
    members = []
    offset = 0
    for dims_of in layout(feature):
        length = math.prod(dims_of)
        members.append(flat_vec[offset : offset + length].reshape(dims_of))
        offset = offset + length
    return tuple(members)


def pack_flat(members, row_count):
    flat_parts = [member.reshape(-1) for member in members]
    filled = sum((part_vec.shape[0] for part_vec in flat_parts))
    flat_parts.append(jnp.zeros((row_count * 128 - filled,), jnp.float32))
    return jnp.concatenate(flat_parts).reshape(row_count, 128)


def token_mask(window_place):
    cells = jnp.arange(WS * WS, dtype=jnp.int32)
    inner_row = cells // WS
    inner_col = cells % WS
    places = window_place[..., None]
    live_slot = places < 25
    row_real = WS * (places // 5) + inner_row < GRID
    col_real = WS * (places % 5) + inner_col < GRID
    return jnp.where(live_slot & row_real & col_real, 1.0, 0.0).astype(jnp.float32)


def rel_index():
    rel_span = 2 * WS - 1
    query_pos = jnp.arange(WS, dtype=jnp.int32)[:, None, None]
    key_pos = jnp.arange(WS, dtype=jnp.int32)[None, :, None]
    offsets = jnp.arange(rel_span, dtype=jnp.int32)[None, None, :]
    return jnp.where(offsets == query_pos - key_pos + WS - 1, 1.0, 0.0).astype(jnp.float32)


def normalize(inputs):
    row_mean = jnp.mean(inputs, -1, keepdims=True)
    centred = inputs - row_mean
    inv_scale = lax.rsqrt(jnp.mean(centred * centred, -1, keepdims=True) + EPS_NORM)
    return (centred * inv_scale, inv_scale)


def norm_back(grad_hat, normed_hat, inv_scale):
    first_mean = jnp.mean(grad_hat, -1, keepdims=True)
    second_mean = jnp.mean(grad_hat * normed_hat, -1, keepdims=True)
    return inv_scale * (grad_hat - first_mean - normed_hat * second_mean)


def score_block(queries, key_rows, table_h, table_w, onehot):
    win_count, tok_count, head_count, head_size = queries.shape
    rel_span = table_h.shape[0]
    score_scale = 1.0 / math.sqrt(head_size)
    direct = (
        jnp.einsum("sqhc,skhc->shqk", queries, key_rows, preferred_element_type=jnp.float32)
        * score_scale
    )
    along_h = jnp.einsum("sqhc,rc->shqr", queries, table_h, preferred_element_type=jnp.float32)
    along_w = jnp.einsum("sqhc,rc->shqr", queries, table_w, preferred_element_type=jnp.float32)
    rel_rows = jnp.einsum(
        "shabr,akr->shabk",
        along_h.reshape(win_count, head_count, WS, WS, rel_span),
        onehot,
        precision=HIGHEST,
    )
    rel_cols = jnp.einsum(
        "shabr,bkr->shabk",
        along_w.reshape(win_count, head_count, WS, WS, rel_span),
        onehot,
        precision=HIGHEST,
    )
    scores = (
        direct.reshape(win_count, head_count, WS, WS, WS, WS)
        + rel_rows[:, :, :, :, :, None]
        + rel_cols[:, :, :, :, None, :]
    )
    return scores.reshape(win_count, head_count, tok_count, tok_count)


def gelu_slope(pre_act):
    normal_cdf = 0.5 * (1.0 + jax.scipy.special.erf(pre_act / math.sqrt(2.0)))
    return normal_cdf + pre_act * jnp.exp(-0.5 * pre_act * pre_act) / math.sqrt(2.0 * math.pi)


def window_pass(tokens, cotangent, keep_mask, weights, onehot):
    (
        qkv_w,
        qv_b,
        proj_w,
        proj_b,
        fc1_w,
        fc1_b,
        fc2_w,
        fc2_b,
        ln1_g,
        ln1_b,
        ln2_g,
        ln2_b,
        table_h,
        table_w,
    ) = weights
    win_count, tok_count, feature = tokens.shape
    head_count = feature // HD
    row_count = win_count * tok_count
    score_scale = 1.0 / math.sqrt(HD)
    inputs = tokens.reshape(row_count, feature).astype(jnp.float32)
    keep_rows = keep_mask.reshape(row_count, 1)
    hat_one, scale_one = normalize(inputs)
    normed_one = (
        (hat_one * ln1_g.astype(jnp.float32) + ln1_b.astype(jnp.float32)) * keep_rows
    ).astype(jnp.bfloat16)
    bias_full = jnp.concatenate(
        [qv_b[:feature], jnp.zeros((feature,), jnp.bfloat16), qv_b[feature:]]
    ).astype(jnp.float32)
    mixed = (jnp.dot(normed_one, qkv_w, preferred_element_type=jnp.float32) + bias_full).astype(
        jnp.bfloat16
    )
    queries = mixed[:, :feature].reshape(win_count, tok_count, head_count, HD)
    key_rows = mixed[:, feature : 2 * feature].reshape(win_count, tok_count, head_count, HD)
    values = mixed[:, 2 * feature :].reshape(win_count, tok_count, head_count, HD)
    scores = score_block(queries, key_rows, table_h, table_w, onehot)
    peak = jnp.max(scores, -1, keepdims=True)
    log_total = peak + jnp.log(jnp.sum(jnp.exp(scores - peak), -1, keepdims=True))
    attn_probs = jnp.exp(scores - log_total).astype(jnp.bfloat16)
    attended = jnp.einsum("shqk,skhc->sqhc", attn_probs, values, preferred_element_type=jnp.float32)
    attended = attended.reshape(row_count, feature).astype(jnp.bfloat16)
    resid = keep_rows * (
        inputs
        + jnp.dot(attended, proj_w, preferred_element_type=jnp.float32)
        + proj_b.astype(jnp.float32)
    )
    hat_two, scale_two = normalize(resid)
    normed_two = (hat_two * ln2_g.astype(jnp.float32) + ln2_b.astype(jnp.float32)).astype(
        jnp.bfloat16
    )
    pre_act = jnp.dot(normed_two, fc1_w, preferred_element_type=jnp.float32) + fc1_b.astype(
        jnp.float32
    )
    activation = jax.nn.gelu(pre_act, approximate=False).astype(jnp.bfloat16)
    result = keep_rows * (
        resid
        + jnp.dot(activation, fc2_w, preferred_element_type=jnp.float32)
        + fc2_b.astype(jnp.float32)
    )
    cot_rows = cotangent.reshape(row_count, feature).astype(jnp.float32) * keep_rows
    grad_out = cot_rows.astype(jnp.bfloat16)
    grad_fc2_w = jnp.einsum("nf,nd->fd", activation, grad_out, preferred_element_type=jnp.float32)
    grad_fc2_b = jnp.sum(grad_out.astype(jnp.float32), 0)
    grad_act = jnp.einsum("nd,fd->nf", grad_out, fc2_w, preferred_element_type=jnp.float32)
    grad_pre = (grad_act * gelu_slope(pre_act)).astype(jnp.bfloat16)
    grad_fc1_w = jnp.einsum("nd,nf->df", normed_two, grad_pre, preferred_element_type=jnp.float32)
    grad_fc1_b = jnp.sum(grad_pre.astype(jnp.float32), 0)
    grad_norm_two = jnp.einsum("nf,df->nd", grad_pre, fc1_w, preferred_element_type=jnp.float32)
    grad_ln2_g = jnp.sum(grad_norm_two * hat_two, 0)
    grad_ln2_b = jnp.sum(grad_norm_two, 0)
    grad_resid = cot_rows + norm_back(grad_norm_two * ln2_g.astype(jnp.float32), hat_two, scale_two)
    grad_branch = keep_rows * grad_resid
    grad_proj = grad_branch.astype(jnp.bfloat16)
    grad_proj_w = jnp.einsum("nd,ne->de", attended, grad_proj, preferred_element_type=jnp.float32)
    grad_proj_b = jnp.sum(grad_proj.astype(jnp.float32), 0)
    grad_att = jnp.einsum(
        "ne,de->nd", grad_proj, proj_w, preferred_element_type=jnp.float32
    ).astype(jnp.bfloat16)
    grad_att = grad_att.reshape(win_count, tok_count, head_count, HD)
    scores_again = score_block(queries, key_rows, table_h, table_w, onehot)
    probs_full = jnp.exp(scores_again - log_total)
    probs_low = probs_full.astype(jnp.bfloat16)
    grad_values = jnp.einsum(
        "shqk,sqhc->skhc", probs_low, grad_att, preferred_element_type=jnp.float32
    )
    grad_probs = jnp.einsum("sqhc,skhc->shqk", grad_att, values, preferred_element_type=jnp.float32)
    grad_scores = probs_full * (grad_probs - jnp.sum(probs_full * grad_probs, -1, keepdims=True))
    grad_scores = grad_scores.astype(jnp.bfloat16)
    grad_query = (
        jnp.einsum("shqk,skhc->sqhc", grad_scores, key_rows, preferred_element_type=jnp.float32)
        * score_scale
    )
    grad_keys = (
        jnp.einsum("shqk,sqhc->skhc", grad_scores, queries, preferred_element_type=jnp.float32)
        * score_scale
    )
    rel_span = table_h.shape[0]
    grad_six = grad_scores.astype(jnp.float32).reshape(win_count, head_count, WS, WS, WS, WS)
    grad_rel_rows = jnp.sum(grad_six, -1)
    grad_rel_cols = jnp.sum(grad_six, -2)
    grad_along_h = jnp.einsum("shabk,akr->shabr", grad_rel_rows, onehot, precision=HIGHEST).reshape(
        win_count, head_count, tok_count, rel_span
    )
    grad_along_w = jnp.einsum("shabk,bkr->shabr", grad_rel_cols, onehot, precision=HIGHEST).reshape(
        win_count, head_count, tok_count, rel_span
    )
    query_wide = queries.astype(jnp.float32)
    grad_query = grad_query + jnp.einsum(
        "shqr,rc->sqhc", grad_along_h, table_h.astype(jnp.float32), precision=HIGHEST
    )
    grad_query = grad_query + jnp.einsum(
        "shqr,rc->sqhc", grad_along_w, table_w.astype(jnp.float32), precision=HIGHEST
    )
    grad_table_h = jnp.einsum("shqr,sqhc->rc", grad_along_h, query_wide, precision=HIGHEST)
    grad_table_w = jnp.einsum("shqr,sqhc->rc", grad_along_w, query_wide, precision=HIGHEST)
    grad_mixed = jnp.concatenate(
        [
            grad_query.reshape(row_count, feature),
            grad_keys.reshape(row_count, feature),
            grad_values.reshape(row_count, feature),
        ],
        -1,
    ).astype(jnp.bfloat16)
    grad_qkv_w = jnp.einsum("nd,nf->df", normed_one, grad_mixed, preferred_element_type=jnp.float32)
    column_sums = jnp.sum(grad_mixed.astype(jnp.float32), 0)
    grad_qv_b = jnp.concatenate([column_sums[:feature], column_sums[2 * feature :]])
    grad_norm_one = keep_rows * jnp.einsum(
        "nf,df->nd", grad_mixed, qkv_w, preferred_element_type=jnp.float32
    )
    grad_ln1_g = jnp.sum(grad_norm_one * hat_one, 0)
    grad_ln1_b = jnp.sum(grad_norm_one, 0)
    grad_input = grad_branch + norm_back(
        grad_norm_one * ln1_g.astype(jnp.float32), hat_one, scale_one
    )
    grad_list = (
        grad_qkv_w,
        grad_qv_b,
        grad_proj_w,
        grad_proj_b,
        grad_fc1_w,
        grad_fc1_b,
        grad_fc2_w,
        grad_fc2_b,
        grad_ln1_g,
        grad_ln1_b,
        grad_ln2_g,
        grad_ln2_b,
        grad_table_h,
        grad_table_w,
    )
    block_part = result.reshape(win_count, tok_count, feature).astype(jnp.bfloat16)
    input_part = grad_input.reshape(win_count, tok_count, feature).astype(jnp.bfloat16)
    return (block_part, input_part, grad_list)


def reduce_grads(local_grads, group_size, part_rows):
    blocks = local_grads.reshape(group_size, part_rows, 128)
    spread = lax.psum_scatter(blocks.astype(jnp.bfloat16), "wide", scatter_dimension=1, tiled=True)
    owned = lax.psum_scatter(spread, "grp", scatter_dimension=0, tiled=True).astype(jnp.float32)
    return owned


def body(tokens, cotangent, window_place, master, first_moment, second_moment):
    part_rows = master.shape[0]
    wide_size = lax.axis_size("wide")
    group_size = lax.axis_size("grp")
    rows_all = part_rows * group_size
    feature = tokens.shape[-1]
    micro_count = tokens.shape[0]
    onehot = rel_index()
    masks = token_mask(window_place)
    block_parts = []
    input_parts = []
    reduced = None
    bias_local = jnp.zeros((feature,), jnp.float32)
    for micro in range(micro_count):
        gathered = lax.all_gather(master.astype(jnp.bfloat16), "grp", axis=0, tiled=True)
        weights = unpack(gathered.reshape(-1), feature)
        block_part, input_part, grad_list = window_pass(
            tokens[micro], cotangent[micro], masks[micro], weights, onehot
        )
        block_parts.append(block_part)
        input_parts.append(input_part)
        bias_local = bias_local + grad_list[3]
        local_grads = pack_flat(grad_list, rows_all)
        owned = reduce_grads(local_grads, group_size, part_rows)
        reduced = owned if reduced is None else reduced + owned
    totals = (
        lax.all_gather(reduced.astype(jnp.bfloat16), "wide", axis=1, tiled=True)
        .astype(reduced.dtype)
        .reshape(part_rows, 128)
    )
    factor = 1.0 / (micro_count * wide_size * group_size)
    grads = totals * factor
    proj_bias_grad = lax.psum(bias_local, ("wide", "grp")) * factor
    moment_next = BETA_ONE * first_moment + (1.0 - BETA_ONE) * grads
    second_next = BETA_TWO * second_moment + (1.0 - BETA_TWO) * grads * grads
    fix_one = 1.0 - BETA_ONE**ADAM_STEP
    fix_two = 1.0 - BETA_TWO**ADAM_STEP
    update = (
        moment_next / fix_one / (jnp.sqrt(second_next / fix_two) + ADAM_EPS) + DECAY_RATE * master
    )
    master_next = master - LEARN_RATE * update
    weights_next = lax.all_gather(master_next.astype(jnp.bfloat16), "grp", axis=0, tiled=True)
    block_out = jnp.stack(block_parts)
    input_grad = jnp.stack(input_parts)
    return (
        block_out,
        input_grad,
        grads,
        master_next,
        moment_next,
        second_next,
        weights_next,
        proj_bias_grad,
    )


def solution(mesh):
    return jax.shard_map(
        body,
        mesh=mesh,
        in_specs=(
            P(None, ("wide", "grp"), None, None),
            P(None, ("wide", "grp"), None, None),
            P(None, ("wide", "grp")),
            P("grp", None),
            P("grp", None),
            P("grp", None),
        ),
        out_specs=(
            P(None, ("wide", "grp"), None, None),
            P(None, ("wide", "grp"), None, None),
            P("grp", None),
            P("grp", None),
            P("grp", None),
            P("grp", None),
            P(),
            P(),
        ),
        check_vma=False,
    )
```

profile of v0, /device:TPU:0, one launch (start us, length us, event | category | flops | bytes accessed | tf_op | source)
XLA Modules:
  0.0 2166.7 jit_solution(6872942744403854429)
XLA Ops:
  7.2 7.9 convert_element_type.324
  23.6 164.5 %all-gather.4.cloned.1.call-done = bf16[55424,128]{1,0:T(8,128)(2,1)} async-done(((bf16[27712,128]{1,0:T(8,128)(2,1)}), bf16[55424,128]{1,0:T(8,128)(2,1)}) %all-gather.4.cloned.1.call-update) | async-done | bytes 14188560 | tf_op jit(solution)/shard_map/all_gather | solution.py:305
  190.1 5.6 reshape.1002
  197.2 3.1 fusion.9
  200.6 35.0 %slice.144 = bf16[110848,64]{1,0:T(8,128)(2,1)} reshape(bf16[55424,128]{1,0:T(8,128)(2,1)} %all-gather.4.cloned.1.call-done) | data formatting | bytes 28377088 | tf_op jit(solution)/shard_map/slice | solution.py:49
  248.6 3.1 copy.243
  251.8 10.8 convolution_bitcast_fusion.4
  265.1 9.0 add.458
  274.1 12.8 add.459
  289.8 4.1 fusion.49
  294.7 8.1 add.454
  302.8 12.7 add.455
  316.4 3.2 fusion.271
  323.2 3.3 reshape.1008
  326.5 9.3 fusion.260
  335.9 8.4 reshape.1009
  348.2 9.2 reshape.1010
  359.3 3.5 reshape.1065
  362.8 3.9 copy.232
  366.7 12.1 convolution_bitcast_fusion.5
  378.9 3.5 copy.233
  382.4 10.3 add.435
  392.8 12.7 add.436
  405.4 3.9 reshape.1064
  409.3 4.2 fusion.46
  414.2 8.1 add.431
  422.3 12.7 add.432
  436.9 3.2 fusion.269
  444.7 9.0 fusion.19
  453.7 7.2 fusion.16
  469.0 3.5 convert_reduce_fusion.3
  499.7 12.8 reshape.1053
  512.6 12.8 reshape.1056
  525.3 18.9 fusion.252
  564.6 3.1 convolution_convert_fusion.4
  570.3 3.8 fusion.43
  597.1 3.1 convolution_convert_fusion.5
  602.8 3.8 fusion.42
  611.2 6.4 reshape.1038
  618.9 3.7 reshape.1039
  622.7 6.0 copy.312
  628.7 3.7 convolution_convert_fusion
  632.5 9.2 reshape.1041
  645.1 3.4 fusion.114
  648.5 203.4 %concatenate.37 = bf16[7094272]{0:T(1024)(128)(2,1)} concatenate(bf16[1769472]{0:T(1024)(128)(2,1)S(1)} %reshape.1038, bf16[768]{0:T(1024)(128)(2,1)} %get-tuple-element.110, bf16[768]{0:T(1024)(128)(2,1)} %get-tuple-element.109, bf16[589824]{0:T(1024)(128)(2,1)} %reshape.1039, bf16[768]{0:T(1024)(128)(2,1)} %get-tuple-element.112, bf16[2359296]{0:T(1024)(128)(2,1)} %bitcast.508, ...), dimensions={0} | concatenate | bytes 28377088 | tf_op jit(solution)/shard_map/concatenate | solution.py:58
  852.0 97.8 %copy.276 = bf16[2,27712,128]{2,0,1:T(2,128)(2,1)} copy(bf16[2,27712,128]{2,1,0:T(8,128)(2,1)} %bitcast.495) | data formatting | bytes 28377088 | tf_op jit(solution)/shard_map/convert_element_type | solution.py:286
  949.8 6.4 reshape.1032
  957.5 3.5 reshape.1033
  961.0 6.0 copy.311
  967.1 3.7 convolution_convert_fusion.2
  970.8 9.2 reshape.1035
  982.7 203.5 %concatenate.36 = bf16[7094272]{0:T(1024)(128)(2,1)} concatenate(bf16[1769472]{0:T(1024)(128)(2,1)S(1)} %reshape.1032, bf16[768]{0:T(1024)(128)(2,1)} %get-tuple-element.108, bf16[768]{0:T(1024)(128)(2,1)} %get-tuple-element.107, bf16[589824]{0:T(1024)(128)(2,1)} %reshape.1033, bf16[768]{0:T(1024)(128)(2,1)} %get-tuple-element.113, bf16[2359296]{0:T(1024)(128)(2,1)} %bitcast.509, ...), dimensions={0} | concatenate | bytes 28377088 | tf_op jit(solution)/shard_map/concatenate | solution.py:58
  1186.2 97.8 %copy.272 = bf16[2,27712,128]{2,0,1:T(2,128)(2,1)} copy(bf16[2,27712,128]{2,1,0:T(8,128)(2,1)} %bitcast.494) | data formatting | bytes 28377088 | tf_op jit(solution)/shard_map/convert_element_type | solution.py:286
  1285.9 486.3 %all-reduce.7.cloned.1.call-done = (bf16[2,27712,128]{2,0,1:T(2,128)(2,1)}, bf16[2,27712,128]{2,0,1:T(2,128)(2,1)}) async-done(((bf16[2,27712,128]{2,0,1:T(2,128)(2,1)}, bf16[2,27712,128]{2,0,1:T(2,128)(2,1)}), (bf16[2,27712,128]{2,0,1:T(2,128)(2,1)}, bf16[2,27712,128]{2,0,1:T(2,128)(2,1)})) %all-reduce.7.cloned.1.call-update) | async-done | bytes 28377104
  1777.8 15.8 reduce-scatter.9.cloned.1.call-done
  1793.6 21.6 reduce-scatter.7.cloned.1.call-done
  1816.5 7.9 copy.278
  1824.4 110.4 %all-gather.6.cloned.1.call-done = bf16[1,27712,128]{2,0,1:T(2,128)(2,1)} async-done(((bf16[1,1732,128]{2,0,1:T(2,128)(2,1)}), bf16[1,27712,128]{2,0,1:T(2,128)(2,1)}) %all-gather.6.cloned.1.call-update) | async-done | bytes 7094288 | tf_op jit(solution)/shard_map/all_gather | solution.py:317
  1934.8 42.2 %fusion.254 = (bf16[27712,128]{1,0:T(8,128)(2,1)}, f32[27712,128]{1,0:T(8,128)}, f32[27712,128]{1,0:T(8,128)}, f32[27712,128]{1,0:T(8,128)}, f32[27712,128]{1,0:T(8,128)}) fusion(f32[27712,128]{1,0:T(8,128)} %param.9, bf16[1,27712,128]{2,0,1:T(2,128)(2,1)} %all-gather.6.cloned.1.call-done, f32[27712,128]{1,0:T(8,128)} %param.10, f32[27712,128]{1,0:T(8,128)} %param.11), kind=kLoop, calls=%fused_computation.395 | loop fusion | flops 63848448 | bytes 113508352 | tf_op jit(solution)/shard_map/convert_element_type | solution.py:332
  1978.5 3.7 fusion.77
  1982.2 4.8 fusion.76
  1990.5 39.3 %psum.7 = f32[768]{0:T(1024)S(1)} all-reduce(f32[768]{0:T(1024)S(1)} %copy-done.91), channel_id=1, replica_groups=mesh['wide'=16,'grp'=2] {'wide','grp'}, use_global_device_ids=true, to_apply=%region_46.47 | all-reduce | flops 768 | bytes 6144 | tf_op jit(solution)/shard_map/psum | solution.py:323
  2030.5 116.4 %all-gather.8.cloned.1.call-done = bf16[55424,128]{1,0:T(8,128)(2,1)} async-done(((bf16[27712,128]{1,0:T(8,128)(2,1)}), bf16[55424,128]{1,0:T(8,128)(2,1)}) %all-gather.8.cloned.1.call-update) | async-done | bytes 14188560 | tf_op jit(solution)/shard_map/all_gather | solution.py:332
  2146.9 12.8 copy.342
  (386 shorter events, 158.6 us)
Async XLA Ops:
  7.2 180.9 %all-gather.4.cloned.1.call-start = ((), (), s32[]{:S(2)}) async-start(), calls=%async_computation.2 | async-start | bytes 21282816 | tf_op jit(solution)/shard_map/all_gather | solution.py:305
  15.1 4.1 copy-start.114
  15.1 4.2 copy-start.51
  15.1 1757.1 %all-reduce.7.cloned.1.call-start = ((), (), s32[]{:S(2)}) async-start(), calls=%async_computation.7 | async-start | bytes 56754176
  17.1 180.0 %copy-start.84 = (f32[196]{0:T(256)}, f32[196]{0:T(256)S(1)}, u32[]{:S(2)}) copy-start(f32[196]{0:T(256)S(1)} %broadcast_multiply_fusion.10) | copy-start | bytes 2356
  19.3 4.2 copy-start.92
  19.3 177.8 %copy-start.79 = (f32[1,1,196]{2,1,0:T(1,128)}, f32[1,1,196]{2,1,0:T(1,128)S(1)}, u32[]{:S(2)}) copy-start(f32[1,1,196]{2,1,0:T(1,128)S(1)} %get-tuple-element.120) | copy-start | bytes 2356
  23.0 174.2 %copy-start.98 = (f32[196]{0:T(256)}, f32[196]{0:T(256)S(1)}, u32[]{:S(2)}) copy-start(f32[196]{0:T(256)S(1)} %add_rsqrt_fusion.1) | copy-start | bytes 2356
  197.1 40.2 %copy-start.71 = (f32[768]{0:T(1024)}, f32[768]{0:T(1024)S(1)}, u32[]{:S(2)}) copy-start(f32[768]{0:T(1024)S(1)} %get-tuple-element.94) | copy-start | bytes 9220
  197.1 40.2 %copy-start.111 = (f32[768]{0:T(1024)}, f32[768]{0:T(1024)S(1)}, u32[]{:S(2)}) copy-start(f32[768]{0:T(1024)S(1)} %get-tuple-element.93) | copy-start | bytes 9220
  200.6 36.8 %copy-start.29 = (bf16[1,1,196,768]{3,2,1,0:T(8,128)(2,1)S(1)}, bf16[1,1,196,768]{3,2,1,0:T(8,128)(2,1)}, u32[]{:S(2)}) copy-start(bf16[1,1,196,768]{3,2,1,0:T(8,128)(2,1)} %copy-done.28) | copy-start | bytes 903172
  200.6 36.8 %copy-start.93 = (f32[1,1,196]{2,1,0:T(1,128)S(1)}, f32[1,1,196]{2,1,0:T(1,128)}, u32[]{:S(2)}) copy-start(f32[1,1,196]{2,1,0:T(1,128)} %copy-done.92) | copy-start | bytes 2356
  200.6 36.8 %copy-start.102 = (f32[196]{0:T(256)S(1)}, f32[196]{0:T(256)}, u32[]{:S(2)}) copy-start(f32[196]{0:T(256)} %copy-done.101) | copy-start | bytes 2356
  200.6 36.8 %copy-start.106 = (f32[196]{0:T(256)S(1)}, f32[196]{0:T(256)}, u32[]{:S(2)}) copy-start(f32[196]{0:T(256)} %add_rsqrt_fusion.3) | copy-start | bytes 2356
  442.4 11.3 slice-start.3
  443.0 25.9 %copy-start.21 = (f32[196,768]{1,0:T(8,128)}, f32[196,768]{1,0:T(8,128)S(1)}, u32[]{:S(2)}) copy-start(f32[196,768]{1,0:T(8,128)S(1)} %get-tuple-element.126) | copy-start | bytes 1806340
  443.0 25.9 %copy-start.89 = (f32[196]{0:T(256)}, f32[196]{0:T(256)S(1)}, u32[]{:S(2)}) copy-start(f32[196]{0:T(256)S(1)} %broadcast_multiply_fusion.11) | copy-start | bytes 2356
  443.3 25.7 %copy-start.104 = (f32[196]{0:T(256)}, f32[196]{0:T(256)S(1)}, u32[]{:S(2)}) copy-start(f32[196]{0:T(256)S(1)} %add_rsqrt_fusion.2) | copy-start | bytes 2356
  444.6 9.1 slice-start.4
  444.7 16.3 slice-start.1
  453.7 7.2 slice-start.2
  453.7 7.2 copy-start.61
  468.9 3.5 copy-start.58
  483.3 7.6 copy-start.1
  525.3 18.9 copy-start.64
  549.0 5.1 copy-start.11
  555.3 5.4 copy-start.6
  557.9 4.4 copy-start.33
  557.9 4.4 copy-start.53
  557.9 4.4 copy-start.55
  557.9 4.4 copy-start.82
  564.5 4.2 copy-start.16
  564.6 4.2 copy-start.40
  570.2 3.8 copy-start.14
  570.3 4.9 copy-start.12
  587.4 5.3 copy-start.32
  589.9 4.3 copy-start.31
  589.9 4.3 copy-start.34
  589.9 4.3 copy-start.52
  589.9 4.3 copy-start.54
  589.9 4.3 copy-start.73
  590.0 4.3 copy-start.95
  590.0 4.3 copy-start.103
  590.0 4.3 copy-start.107
  597.1 4.1 copy-start.24
  597.1 4.1 copy-start.42
  602.8 3.8 copy-start.13
  622.7 6.1 copy-start.45
  622.7 6.1 copy-start.48
  622.7 6.1 copy-start.83
  961.0 6.1 copy-start.43
  961.0 6.1 copy-start.62
  961.0 6.1 copy-start.96
  1284.1 509.5 %reduce-scatter.9.cloned.1.call-start = ((), (), s32[]{:S(2)}) async-start(), calls=%async_computation.6 | async-start | bytes 1333248
  1774.9 40.3 %reduce-scatter.7.cloned.1.call-start = ((), (), s32[]{:S(2)}) async-start(), calls=%async_computation.5 | async-start | bytes 1333248
  1777.7 157.1 %all-gather.6.cloned.1.call-start = ((), (), s32[]{:S(2)}) async-start(), calls=%async_computation.3 | async-start | bytes 15075328 | tf_op jit(solution)/shard_map/all_gather | solution.py:317
  1824.3 322.5 %all-gather.8.cloned.1.call-start = ((), (), s32[]{:S(2)}) async-start(), calls=%async_computation.4 | async-start | bytes 21282816 | tf_op jit(solution)/shard_map/all_gather | solution.py:332
  1978.4 3.7 copy-start.23
  1978.4 3.7 copy-start.44
  1978.4 3.7 copy-start.97
  1982.1 6.3 copy-start.109
  1982.2 6.3 copy-start.108
  1982.2 6.3 copy-start.86
  1982.2 6.3 copy-start.100
  (63 other events, 132.5 us)
Sparse Core Ops, SparseCore 0:
  15.2 172.8 all-gather.3
  1284.2 487.9 all-reduce.6
  1775.1 18.4 reduce-scatter.8
  1796.3 18.8 reduce-scatter.6
  1824.4 110.2 all-gather.5
  1977.1 169.6 all-gather.7
where the time goes:
time: 2210 us; the launch traced here: 2170 us
  local copies, waits for them, and re-layouts  946 us (43%)
  waiting for transfers between devices  915 us (41%)
  matrix products  158 us (7%)
  other arithmetic  92 us (4%)
  blocking collectives  39.3 us (2%)
    unnamed x9, waiting for transfers between devices  524 us
    concatenate x2, local copies, waits for them, and re-layouts, pack_flat(): return jnp.concatenate(flat_parts).reshape(row_count, 128)  407 us
    convert_element_type x2, local copies, waits for them, and re-layouts, reduce_grads(): blocks.astype(jnp.bfloat16)  196 us
    all_gather x1, waiting for transfers between devices, body(): lax.all_gather(master.astype(jnp.bfloat16), 'grp', axis=0, tiled=True)  165 us
    all_gather x1, waiting for transfers between devices, body(): lax.all_gather(master_next.astype(jnp.bfloat16), 'grp', axis=0, tiled=True)  116 us
    all_gather x1, waiting for transfers between devices, body(): lax.all_gather(reduced.astype(jnp.bfloat16), 'wide', axis=1, tiled=True)  110 us
    add x12, local copies, waits for them, and re-layouts, score_block(): direct.reshape(win_count, head_count, WS, WS, WS, WS)  93.8 us
    slice x5, local copies, waits for them, and re-layouts, unpack(): members.append(flat_vec[offset:offset + length].reshape(dims_of))  48.9 us
  transfers between devices with their start and end apart: 6, of which 6 were waited for; matrix products, arithmetic and copies ran while one was open for 1% of the time, Pallas kernels for 0%

commit v1 on v0

v1 whole, which is shorter than its diff:
```python
import functools
import math

import jax
import jax.numpy as jnp
from jax import lax
from jax.experimental import pallas as pl
from jax.experimental.pallas import tpu as pltpu
from jax.sharding import PartitionSpec as P

FF = 3072
HD = 64
WS = 14
GRID = 64
ADAM_STEP = 10


EPS_NORM = 1e-06
BETA_ONE = 0.9
BETA_TWO = 0.95
ADAM_EPS = 1e-08
LEARN_RATE = 0.02
DECAY_RATE = 0.1


def layout(feature):
    rel_span = 2 * WS - 1
    return [
        (feature, 3 * feature),
        (2 * feature,),
        (feature, feature),
        (feature,),
        (feature, FF),
        (FF,),
        (FF, feature),
        (feature,),
        (feature,),
        (feature,),
        (feature,),
        (feature,),
        (rel_span, HD),
        (rel_span, HD),
    ]


def unpack(rows, feature):
    members = []
    row = 0
    dims = layout(feature)
    for dims_of in dims[:8]:
        length = math.prod(dims_of) // 128
        members.append(rows[row : row + length].reshape(dims_of))
        row = row + length
    tail_size = sum(math.prod(dims_of) for dims_of in dims[8:])
    tail = rows[row : row - (-tail_size // 128)].reshape(-1)
    offset = 0
    for dims_of in dims[8:]:
        length = math.prod(dims_of)
        members.append(tail[offset : offset + length].reshape(dims_of))
        offset = offset + length
    return tuple(members)


def token_mask(window_place):
    cells = jnp.arange(WS * WS, dtype=jnp.int32)
    inner_row = cells // WS
    inner_col = cells % WS
    places = window_place[..., None]
    live_slot = places < 25
    row_real = WS * (places // 5) + inner_row < GRID
    col_real = WS * (places % 5) + inner_col < GRID
    return jnp.where(live_slot & row_real & col_real, 1.0, 0.0).astype(jnp.float32)


def normalize(inputs):
    row_mean = jnp.mean(inputs, -1, keepdims=True)
    centred = inputs - row_mean
    inv_scale = lax.rsqrt(jnp.mean(centred * centred, -1, keepdims=True) + EPS_NORM)
    return (centred * inv_scale, inv_scale)


def norm_back(grad_hat, normed_hat, inv_scale):
    first_mean = jnp.mean(grad_hat, -1, keepdims=True)
    second_mean = jnp.mean(grad_hat * normed_hat, -1, keepdims=True)
    return inv_scale * (grad_hat - first_mean - normed_hat * second_mean)


def attend_kernel(q_ref, k_ref, v_ref, table_ref, shift_ref, key_ref, probs_ref, out_ref):
    shift = shift_ref[...]
    key_cells = key_ref[...]
    row_count = shift.shape[0]
    real_key = lax.broadcasted_iota(jnp.int32, (row_count, row_count), 1) < WS * WS
    for part in range(2):
        cut = slice(part * HD, (part + 1) * HD)
        queries = q_ref[:, cut]
        along = jnp.dot(queries, table_ref[...], preferred_element_type=jnp.float32)
        for bit in (1, 2, 4, 8):
            along = jnp.where((shift & bit) != 0, pltpu.roll(along, 128 - bit, 1), along)
        high = along.astype(jnp.bfloat16)
        low = (along - high.astype(jnp.float32)).astype(jnp.bfloat16)
        scores = dot_last(queries, k_ref[:, cut]) * (1.0 / math.sqrt(HD))
        scores = scores + dot_last(high, key_cells) + dot_last(low, key_cells)
        scores = jnp.where(real_key, scores, -1e30)
        powers = jnp.exp(scores - jnp.max(scores, -1, keepdims=True))
        probs = (powers / jnp.sum(powers, -1, keepdims=True)).astype(jnp.bfloat16)
        probs_ref[0, part] = probs
        out_ref[:, cut] = jnp.dot(
            probs, v_ref[:, cut], preferred_element_type=jnp.float32
        ).astype(jnp.bfloat16)


def attend_back_kernel(
    q_ref, k_ref, v_ref, probs_ref, grad_ref, table_ref, shift_ref, key_ref,
    dq_ref, dk_ref, dv_ref, dtable_ref,
):
    shift = shift_ref[...]
    key_cells = key_ref[...]
    scale = 1.0 / math.sqrt(HD)

    @pl.when((pl.program_id(0) == 0) & (pl.program_id(1) == 0))
    def _():
        dtable_ref[...] = jnp.zeros(dtable_ref.shape, jnp.float32)

    for part in range(2):
        cut = slice(part * HD, (part + 1) * HD)
        queries = q_ref[:, cut]
        grad = grad_ref[:, cut]
        probs = probs_ref[0, part]
        dv_ref[:, cut] = dot_first(probs, grad).astype(jnp.bfloat16)
        grad_probs = dot_last(grad, v_ref[:, cut])
        wide_probs = probs.astype(jnp.float32)
        inner = jnp.sum(wide_probs * grad_probs, -1, keepdims=True)
        grad_scores = (wide_probs * (grad_probs - inner)).astype(jnp.bfloat16)
        dk_ref[:, cut] = (dot_first(grad_scores, queries) * scale).astype(jnp.bfloat16)
        along = jnp.dot(grad_scores, key_cells, preferred_element_type=jnp.float32)
        for bit in (1, 2, 4, 8):
            along = jnp.where((shift & bit) != 0, pltpu.roll(along, bit, 1), along)
        high = along.astype(jnp.bfloat16)
        low = (along - high.astype(jnp.float32)).astype(jnp.bfloat16)
        grad_query = jnp.dot(grad_scores, k_ref[:, cut], preferred_element_type=jnp.float32) * scale
        grad_query = grad_query + dot_last(high, table_ref[...]) + dot_last(low, table_ref[...])
        dq_ref[:, cut] = grad_query.astype(jnp.bfloat16)
        dtable_ref[...] += dot_first(queries, high) + dot_first(queries, low)


def window_constants(row_count):
    cells = jnp.arange(row_count, dtype=jnp.int32)[:, None]
    lanes = jnp.arange(128, dtype=jnp.int32)[None, :]
    first = lanes < 64
    shift = jnp.where(first, WS - 1 - cells // WS, WS - 1 - cells % WS)
    live = cells < WS * WS
    shift = jnp.where(live, shift, 0)
    offset = jnp.where(first, lanes, lanes - 64)
    place = jnp.where(first, cells // WS, cells % WS)
    key_cells = jnp.where(live & (offset == place), 1.0, 0.0).astype(jnp.bfloat16)
    return shift, key_cells


def wide_table(table_h, table_w):
    pad = jnp.zeros((HD, 64 - table_h.shape[0]), table_h.dtype)
    return jnp.concatenate([table_h[::-1].T, pad, table_w[::-1].T, pad], 1)


def attend(mixed, table, shift, key_cells, feature):
    rows, pairs = shift.shape[0], feature // 128
    wins = mixed.shape[0] // rows
    whole = lambda shape: pl.BlockSpec(shape, lambda w, h: (0,) * len(shape))
    column = lambda base: pl.BlockSpec((rows, 128), lambda w, h: (w, base * pairs + h))
    return pl.pallas_call(
        attend_kernel,
        grid=(wins, pairs),
        in_specs=[column(0), column(1), column(2), whole((HD, 128)), whole((rows, 128)), whole((rows, 128))],
        out_specs=[
            pl.BlockSpec((1, 2, rows, rows), lambda w, h: (w, h, 0, 0)),
            pl.BlockSpec((rows, 128), lambda w, h: (w, h)),
        ],
        out_shape=[
            jax.ShapeDtypeStruct((wins, 2 * pairs, rows, rows), jnp.bfloat16),
            jax.ShapeDtypeStruct((wins * rows, feature), jnp.bfloat16),
        ],
        name="attend",
    )(mixed, mixed, mixed, table, shift, key_cells)


def attend_back(mixed, probs, grad_att, table, shift, key_cells, feature):
    rows, pairs = shift.shape[0], feature // 128
    wins = mixed.shape[0] // rows
    whole = lambda shape: pl.BlockSpec(shape, lambda w, h: (0,) * len(shape))
    column = lambda base: pl.BlockSpec((rows, 128), lambda w, h: (w, base * pairs + h))
    flat = jax.ShapeDtypeStruct((wins * rows, feature), jnp.bfloat16)
    return pl.pallas_call(
        attend_back_kernel,
        grid=(wins, pairs),
        in_specs=[
            column(0), column(1), column(2),
            pl.BlockSpec((1, 2, rows, rows), lambda w, h: (w, h, 0, 0)),
            column(0),
            whole((HD, 128)), whole((rows, 128)), whole((rows, 128)),
        ],
        out_specs=[column(0), column(0), column(0), whole((HD, 128))],
        out_shape=[flat, flat, flat, jax.ShapeDtypeStruct((HD, 128), jnp.float32)],
        name="attend_back",
    )(mixed, mixed, mixed, probs, grad_att, table, shift, key_cells)


def dot_last(left, right):
    return lax.dot_general(left, right, (((1,), (1,)), ((), ())), preferred_element_type=jnp.float32)


def dot_first(left, right):
    return lax.dot_general(left, right, (((0,), (0,)), ((), ())), preferred_element_type=jnp.float32)


def pack_kernel(
    n1_ref, dq_ref, dk_ref, dv_ref, att_ref, dproj_ref, n2_ref, dpre_ref, act_ref, dout_ref, tail_ref,
    out_ref, rows_ref, stage_ref, bias_ref, stage_sems, bias_sems,
    *, part_rows, share_rows, group_size,
):
    count = n1_ref.shape[0]
    ones = jnp.ones((16, count), jnp.bfloat16)

    def weight(base, left_ref, right_refs):
        width = sum(ref.shape[1] for ref in right_refs) // 128

        def block(f, carry):
            left = left_ref[:, pl.ds(pl.multiple_of(f * 128, 128), 128)]
            column = 0
            for ref in right_refs:
                product = dot_first(left, ref[...])
                for j in range(ref.shape[1] // 128):
                    rows_ref[pl.ds(base + f * 128 * width + column, 128, stride=width), :] = product[
                        :, j * 128 : (j + 1) * 128
                    ]
                    column += 1
            return carry

        lax.fori_loop(0, left_ref.shape[1] // 128, block, 0)
        return base + left_ref.shape[1] * width

    def bias(base, ref):
        total = jnp.dot(ones, ref[...], preferred_element_type=jnp.float32)
        for j in range(ref.shape[1] // 128):
            rows_ref[base + j : base + j + 1, :] = total[0:1, j * 128 : (j + 1) * 128]
        return base + ref.shape[1] // 128

    limit = stage_ref.shape[1]
    chunks = []
    for owner in range(group_size):
        low = 0
        while low < part_rows:
            size = min(limit, part_rows - low)
            chunks.append((owner * part_rows + low, owner * share_rows + low, size))
            low += size
    flying = {}
    sent = 0

    def emit(upto):
        nonlocal sent
        while sent < len(chunks) and chunks[sent][0] + chunks[sent][2] <= upto:
            source, target, size = chunks[sent]
            slot = sent % 2
            if slot in flying:
                flying.pop(slot).wait()
            step = next(s for s in (128, 64, 32, 16) if size % s == 0)

            def convert(i, carry, source=source, slot=slot, step=step):
                at = pl.multiple_of(i * step, step)
                stage_ref[slot, pl.ds(at, step), :] = rows_ref[
                    pl.ds(pl.multiple_of(source + at, 16), step), :
                ].astype(jnp.bfloat16)
                return carry

            lax.fori_loop(0, size // step, convert, 0)
            copy = pltpu.make_async_copy(
                stage_ref.at[slot, pl.ds(0, size), :],
                out_ref.at[pl.ds(target, size), :],
                stage_sems.at[slot],
            )
            copy.start()
            flying[slot] = copy
            sent += 1

    row = weight(0, n1_ref, [dq_ref, dk_ref, dv_ref])
    row = bias(row, dq_ref)
    row = bias(row, dv_ref)
    emit(row)
    row = weight(row, att_ref, [dproj_ref])
    proj_bias = row
    row = bias(row, dproj_ref)
    emit(row)
    bias_size = dproj_ref.shape[1] // 128
    spare = share_rows - part_rows
    bias_ref[...] = jnp.concatenate(
        [
            rows_ref[proj_bias : proj_bias + bias_size, :],
            jnp.zeros((spare - bias_size, 128), jnp.float32),
        ],
        0,
    ).astype(jnp.bfloat16)
    bias_copies = [
        pltpu.make_async_copy(
            bias_ref, out_ref.at[pl.ds(owner * share_rows + part_rows, spare), :], bias_sems.at[owner]
        )
        for owner in range(group_size)
    ]
    for copy in bias_copies:
        copy.start()
    row = weight(row, n2_ref, [dpre_ref])
    row = bias(row, dpre_ref)
    emit(row)
    row = weight(row, act_ref, [dout_ref])
    row = bias(row, dout_ref)
    emit(row)
    rows_ref[row : row + tail_ref.shape[0], :] = tail_ref[...]
    emit(group_size * part_rows)
    for slot in list(flying):
        flying.pop(slot).wait()
    for copy in bias_copies:
        copy.wait()


def pack_shares(factors, tail, part_rows, group_size, wide_size):
    feature = factors[0].shape[1]
    grain = 16 * wide_size
    share_rows = -(-(part_rows + feature // 128) // grain) * grain
    spare = share_rows - part_rows
    whole = pl.BlockSpec(memory_space=pltpu.VMEM)
    packed = pl.pallas_call(
        functools.partial(
            pack_kernel, part_rows=part_rows, share_rows=share_rows, group_size=group_size
        ),
        in_specs=[whole] * (len(factors) + 1),
        out_specs=pl.BlockSpec(memory_space=pl.ANY),
        out_shape=jax.ShapeDtypeStruct((group_size * share_rows, 128), jnp.bfloat16),
        scratch_shapes=[
            pltpu.VMEM((group_size * part_rows, 128), jnp.float32),
            pltpu.VMEM((2, 2048, 128), jnp.bfloat16),
            pltpu.VMEM((spare, 128), jnp.bfloat16),
            pltpu.SemaphoreType.DMA((2,)),
            pltpu.SemaphoreType.DMA((group_size,)),
        ],
        compiler_params=pltpu.CompilerParams(vmem_limit_bytes=60 * 1024 * 1024),
        name="pack_grads",
    )(*factors, tail)
    return packed, share_rows


def gelu_slope(pre_act):
    normal_cdf = 0.5 * (1.0 + jax.scipy.special.erf(pre_act / math.sqrt(2.0)))
    return normal_cdf + pre_act * jnp.exp(-0.5 * pre_act * pre_act) / math.sqrt(2.0 * math.pi)


def window_pass(tokens, cotangent, keep_mask, weights):
    (
        qkv_w,
        qv_b,
        proj_w,
        proj_b,
        fc1_w,
        fc1_b,
        fc2_w,
        fc2_b,
        ln1_g,
        ln1_b,
        ln2_g,
        ln2_b,
        table_h,
        table_w,
    ) = weights
    win_count, tok_count, feature = tokens.shape
    row_count = win_count * tok_count
    inputs = tokens.reshape(row_count, feature).astype(jnp.float32)
    keep_rows = keep_mask.reshape(row_count, 1)
    hat_one, scale_one = normalize(inputs)
    normed_one = (
        (hat_one * ln1_g.astype(jnp.float32) + ln1_b.astype(jnp.float32)) * keep_rows
    ).astype(jnp.bfloat16)
    bias_full = jnp.concatenate(
        [qv_b[:feature], jnp.zeros((feature,), jnp.bfloat16), qv_b[feature:]]
    ).astype(jnp.float32)
    mixed = (jnp.dot(normed_one, qkv_w, preferred_element_type=jnp.float32) + bias_full).astype(
        jnp.bfloat16
    )
    shift, key_cells = window_constants(tok_count)
    table = wide_table(table_h, table_w)
    probs, attended = attend(mixed, table, shift, key_cells, feature)
    resid = keep_rows * (
        inputs
        + jnp.dot(attended, proj_w, preferred_element_type=jnp.float32)
        + proj_b.astype(jnp.float32)
    )
    hat_two, scale_two = normalize(resid)
    normed_two = (hat_two * ln2_g.astype(jnp.float32) + ln2_b.astype(jnp.float32)).astype(
        jnp.bfloat16
    )
    pre_act = jnp.dot(normed_two, fc1_w, preferred_element_type=jnp.float32) + fc1_b.astype(
        jnp.float32
    )
    activation = jax.nn.gelu(pre_act, approximate=False).astype(jnp.bfloat16)
    result = keep_rows * (
        resid
        + jnp.dot(activation, fc2_w, preferred_element_type=jnp.float32)
        + fc2_b.astype(jnp.float32)
    )
    cot_rows = cotangent.reshape(row_count, feature).astype(jnp.float32) * keep_rows
    grad_out = cot_rows.astype(jnp.bfloat16)
    grad_act = jnp.einsum("nd,fd->nf", grad_out, fc2_w, preferred_element_type=jnp.float32)
    grad_pre = (grad_act * gelu_slope(pre_act)).astype(jnp.bfloat16)
    grad_norm_two = jnp.einsum("nf,df->nd", grad_pre, fc1_w, preferred_element_type=jnp.float32)
    grad_ln2_g = jnp.sum(grad_norm_two * hat_two, 0)
    grad_ln2_b = jnp.sum(grad_norm_two, 0)
    grad_resid = cot_rows + norm_back(grad_norm_two * ln2_g.astype(jnp.float32), hat_two, scale_two)
    grad_branch = keep_rows * grad_resid
    grad_proj = grad_branch.astype(jnp.bfloat16)
    grad_att = jnp.einsum(
        "ne,de->nd", grad_proj, proj_w, preferred_element_type=jnp.float32
    ).astype(jnp.bfloat16)
    grad_query, grad_keys, grad_values, grad_table = attend_back(
        mixed, probs, grad_att, table, shift, key_cells, feature
    )
    rel_span = table_h.shape[0]
    grad_table_h = grad_table[:, :rel_span].T[::-1]
    grad_table_w = grad_table[:, 64 : 64 + rel_span].T[::-1]
    grad_mixed = jnp.concatenate([grad_query, grad_keys, grad_values], -1)
    grad_norm_one = keep_rows * jnp.einsum(
        "nf,df->nd", grad_mixed, qkv_w, preferred_element_type=jnp.float32
    )
    grad_ln1_g = jnp.sum(grad_norm_one * hat_one, 0)
    grad_ln1_b = jnp.sum(grad_norm_one, 0)
    grad_input = grad_branch + norm_back(
        grad_norm_one * ln1_g.astype(jnp.float32), hat_one, scale_one
    )
    factors = (
        normed_one,
        grad_query,
        grad_keys,
        grad_values,
        attended,
        grad_proj,
        normed_two,
        grad_pre,
        activation,
        grad_out,
    )
    tail = (grad_ln1_g, grad_ln1_b, grad_ln2_g, grad_ln2_b, grad_table_h, grad_table_w)
    block_part = result.reshape(win_count, tok_count, feature).astype(jnp.bfloat16)
    input_part = grad_input.reshape(win_count, tok_count, feature).astype(jnp.bfloat16)
    return (block_part, input_part, factors, tail)


def body(tokens, cotangent, window_place, master, first_moment, second_moment):
    part_rows = master.shape[0]
    wide_size = lax.axis_size("wide")
    group_size = lax.axis_size("grp")
    feature = tokens.shape[-1]
    micro_count, slots, tok_count, _ = tokens.shape
    masks = token_mask(window_place)
    gathered = lax.all_gather(master.astype(jnp.bfloat16), "grp", axis=0, tiled=True)
    weights = unpack(gathered, feature)
    wins = micro_count * slots
    extra = -tok_count % 16

    def padded(values):
        values = values.reshape((wins,) + values.shape[2:])
        return jnp.pad(values, ((0, 0), (0, extra)) + ((0, 0),) * (values.ndim - 2))

    block_part, input_part, factors, tail = window_pass(
        padded(tokens), padded(cotangent), padded(masks), weights
    )
    filled = sum(math.prod(dims_of) for dims_of in layout(feature)[:8]) // 128
    tail = jnp.concatenate([member.reshape(-1) for member in tail])
    tail_rows = part_rows * group_size - filled
    tail = jnp.pad(tail, (0, tail_rows * 128 - tail.shape[0])).reshape(tail_rows, 128)
    packed, share_rows = pack_shares(factors, tail, part_rows, group_size, wide_size)
    owned = lax.psum_scatter(packed, ("grp", "wide"), scatter_dimension=0, tiled=True)
    totals = lax.all_gather(owned, "wide", axis=0, tiled=True).astype(jnp.float32)
    factor = 1.0 / (micro_count * wide_size * group_size)
    grads = totals[:part_rows] * factor
    proj_bias_grad = totals[part_rows : part_rows + feature // 128].reshape(-1) * factor
    moment_next = BETA_ONE * first_moment + (1.0 - BETA_ONE) * grads
    second_next = BETA_TWO * second_moment + (1.0 - BETA_TWO) * grads * grads
    fix_one = 1.0 - BETA_ONE**ADAM_STEP
    fix_two = 1.0 - BETA_TWO**ADAM_STEP
    update = (
        moment_next / fix_one / (jnp.sqrt(second_next / fix_two) + ADAM_EPS) + DECAY_RATE * master
    )
    master_next = master - LEARN_RATE * update
    weights_next = lax.all_gather(master_next.astype(jnp.bfloat16), "grp", axis=0, tiled=True)
    block_out = block_part[:, :tok_count].reshape(tokens.shape)
    input_grad = input_part[:, :tok_count].reshape(tokens.shape)
    return (
        block_out,
        input_grad,
        grads,
        master_next,
        moment_next,
        second_next,
        weights_next,
        proj_bias_grad,
    )


def solution(mesh):
    return jax.shard_map(
        body,
        mesh=mesh,
        in_specs=(
            P(None, ("wide", "grp"), None, None),
            P(None, ("wide", "grp"), None, None),
            P(None, ("wide", "grp")),
            P("grp", None),
            P("grp", None),
            P("grp", None),
        ),
        out_specs=(
            P(None, ("wide", "grp"), None, None),
            P(None, ("wide", "grp"), None, None),
            P("grp", None),
            P("grp", None),
            P("grp", None),
            P("grp", None),
            P(),
            P(),
        ),
        check_vma=False,
    )
```

time: 2210 us -> 831 us (0.38); the launches traced: 2170 us -> 830 us
  local copies, waits for them, and re-layouts: 946 us -> 60.6 us
  waiting for transfers between devices: 915 us -> 557 us
  matrix products: 158 us -> 42.2 us
  Pallas kernels: 0 us -> 83 us
  blocking collectives: 39.3 us -> 0 us
    unnamed x9 -> x4, waiting for transfers between devices: 524 us -> 0.07 us
    concatenate x3 -> x1, local copies, waits for them, and re-layouts: 407 us -> 0.09 us  [body(): tail = jnp.concatenate([member.reshape(-1) for member in tail])]
    convert_element_type x5 -> x0, local copies, waits for them, and re-layouts: 207 us -> none  [the longest x2 196 us: reduce_grads(): blocks.astype(jnp.bfloat16)]
    reduce_scatter x0 -> x1, waiting for transfers between devices: none -> 162 us  [body(): lax.psum_scatter(packed, ('grp', 'wide'), scatter_dimension=0, tiled=True)]
    dot_general x40 -> x0, matrix products: 105 us -> none  [the longest x2 22.9 us: score_block(): jnp.einsum('shabr,bkr->shabk', along_w.reshape(win_count, head_count, WS,...]
    add x12 -> x0, local copies, waits for them, and re-layouts: 93.8 us -> none  [score_block(): direct.reshape(win_count, head_count, WS, WS, WS, WS)]
    pallas_call x0 -> x3, Pallas kernels: none -> 83 us  [the longest x1 33.1 us: pack_shares(): pl.pallas_call(functools.partial(pack_kernel, part_rows=part_rows, share_...]
    reshape x18 -> x8, local copies, waits for them, and re-layouts: 101 us -> 27.8 us  [the longest x4 26.9 us: unpack(): members.append(rows[row:row + length].reshape(dims_of))]
  transfers between devices with their start and end apart: 6 -> 4, of which waited for: 6 -> 4; matrix products, arithmetic and copies ran while one was open for 1% -> 2% of each run, Pallas kernels for 0% -> 0%
where the time goes in v1:
time: 831 us; the launch traced here: 830 us
  waiting for transfers between devices  557 us (67%)
  Pallas kernels  83 us (10%)
  other arithmetic  72.9 us (9%)
  local copies, waits for them, and re-layouts  60.6 us (7%)
  matrix products  42.2 us (5%)
  between operations  14 us (2%)
    all_gather x1, waiting for transfers between devices, body(): lax.all_gather(master.astype(jnp.bfloat16), 'grp', axis=0, tiled=True)  167 us
    reduce_scatter x1, waiting for transfers between devices, body(): lax.psum_scatter(packed, ('grp', 'wide'), scatter_dimension=0, tiled=True)  162 us
    all_gather x1, waiting for transfers between devices, body(): lax.all_gather(master_next.astype(jnp.bfloat16), 'grp', axis=0, tiled=True)  160 us
    all_gather x1, waiting for transfers between devices, body(): lax.all_gather(owned, 'wide', axis=0, tiled=True).astype(jnp.float32)  68.2 us
    convert_element_type x1, other arithmetic, body(): master_next.astype(jnp.bfloat16)  42.1 us
    pallas_call x1, Pallas kernels, pack_shares(): pl.pallas_call(functools.partial(pack_kernel, part_rows=part_rows, share_...  33.1 us
    reshape x4, local copies, waits for them, and re-layouts, unpack(): members.append(rows[row:row + length].reshape(dims_of))  26.9 us
    pallas_call x1, Pallas kernels, attend(): pl.pallas_call(attend_kernel, grid=(wins, pairs), in_specs=[column(0), co...  25.3 us
  transfers between devices with their start and end apart: 4, of which 4 were waited for; matrix products, arithmetic and copies ran while one was open for 2% of the time, Pallas kernels for 0%

profile of v1, /device:TPU:0, one launch (start us, length us, event | category | flops | bytes accessed | tf_op | source)
XLA Modules:
  0.0 829.9 jit_solution(3695255650764342317)
XLA Ops:
  7.2 7.9 convert_element_type.167
  15.2 0.6 copy-done.9
  15.8 0.1 and_select_fusion
  15.8 0.1 mul.247
  15.9 0.2 copy-done.6
  16.2 0.2 copy-done.7
  16.3 0.1 copy_bitcast_fusion
  16.5 0.2 convert_reduce_fusion
  16.7 0.1 div.111
  16.7 0.3 multiply_reduce_fusion.5
  17.1 0.1 rsqrt.22
  17.2 1.1 pad_convert_fusion
  18.4 0.8 select_convert_fusion.key_ref
  19.1 0.8 select_select_fusion.shift_ref
  19.9 1.3 fusion.31
  21.2 166.9 %all-gather.4.cloned.1.call-done = bf16[55424,128]{1,0:T(8,128)(2,1)} async-done(((bf16[27712,128]{1,0:T(8,128)(2,1)}), bf16[55424,128]{1,0:T(8,128)(2,1)}) %all-gather.4.cloned.1.call-update) | async-done | bytes 14188560 | tf_op jit(solution)/shard_map/all_gather | solution.py:458
  188.1 0.7 slice.111
  188.8 0.1 slice.89
  188.9 0.1 copy.26
  189.0 0.1 rev.12
  189.1 0.1 copy.27
  189.2 0.1 rev.13
  189.3 1.6 slice.114
  190.9 1.9 reshape.437
  192.8 3.4 slice.108
  196.2 7.6 reshape.436
  203.7 9.3 %fusion.53 = (bf16[18432,128]{1,0:T(8,128)(2,1)}, bf16[18432,128]{1,0:T(8,128)(2,1)}) fusion(bf16[55424,128]{1,0:T(8,128)(2,1)} %all-gather.4.cloned.1.call-done), kind=kLoop, calls=%fused_computation.137 | loop fusion | bytes 18874368 | tf_op jit(solution)/shard_map/slice | solution.py:52
  213.1 9.2 %reshape.439 = bf16[3072,768]{1,0:T(8,128)(2,1)} reshape(bf16[18432,128]{1,0:T(8,128)(2,1)} %get-tuple-element.45) | data formatting | bytes 9437184 | tf_op jit(solution)/shard_map/reshape | solution.py:52
  222.3 0.7 pad_maximum_fusion.table_ref
  223.0 0.8 fusion.36
  223.8 0.5 multiply_convert_fusion.1
  224.3 4.9 fusion.16.q_ref.k_ref.v_ref
  229.2 25.3 %attend.1 = (bf16[2,12,208,208]{3,2,1,0:T(8,128)(2,1)}, bf16[416,768]{1,0:T(8,128)(2,1)}) custom-call(bf16[416,2304]{1,0:T(8,128)(2,1)} %fusion.16.q_ref.k_ref.v_ref, bf16[416,2304]{1,0:T(8,128)(2,1)} %fusion.16.q_ref.k_ref.v_ref, bf16[416,2304]{1,0:T(8,128)(2,1)} %fusion.16.q_ref.k_ref.v_ref, bf16[64,128]{1,0:T(8,128)(2,1)} %pad_maximum_fusion.table_ref, ...), custom_call_target="tpu_custom_call" | custom-call | tf_op jit(solution)/shard_map/attend/pallas_call | solution.py:169
  254.5 2.7 fusion.55
  257.2 0.3 multiply_reduce_fusion.4
  257.5 8.2 reshape.438
  265.7 0.3 add_convert_fusion.1.n2_ref
  266.0 1.1 fusion.34
  267.0 15.5 %fusion.2 = (bf16[416,3072]{1,0:T(8,128)(2,1)}, f32[416,3072]{1,0:T(8,128)S(1)}) fusion(f32[3072]{0:T(1024)S(1)} %fusion.34, bf16[416,768]{1,0:T(8,128)(2,1)S(1)} %add_convert_fusion.1.n2_ref, bf16[768,3072]{1,0:T(8,128)(2,1)} %reshape.438), kind=kOutput, calls=%fused_computation.8 | convolution fusion | flops 2047279104 | bytes 13037568 | tf_op jit(solution)/shard_map/dot_general | solution.py:396
  282.6 3.8 fusion.8.dpre_ref
  286.4 2.6 multiply_reduce_fusion
  289.0 1.9 fusion.52
  290.9 1.5 convolution_convert_fusion.grad_ref
  292.4 24.6 %attend_back.1 = (bf16[416,768]{1,0:T(8,128)(2,1)}, bf16[416,768]{1,0:T(8,128)(2,1)}, bf16[416,768]{1,0:T(8,128)(2,1)}, f32[64,128]{1,0:T(8,128)}) custom-call(bf16[416,2304]{1,0:T(8,128)(2,1)} %fusion.16.q_ref.k_ref.v_ref, bf16[416,2304]{1,0:T(8,128)(2,1)} %fusion.16.q_ref.k_ref.v_ref, bf16[416,2304]{1,0:T(8,128)(2,1)} %fusion.16.q_ref.k_ref.v_ref, ...), custom_call_target="tpu_custom_call" | custom-call | tf_op jit(solution)/shard_map/attend_back/pallas_call | solution.py:191
  317.0 5.9 fusion.50
  323.0 0.1 slice_bitcast_fusion
  323.0 0.1 rev.15
  323.1 0.1 copy.25
  323.2 0.1 reshape.444
  323.3 0.1 copy.24
  323.5 0.1 concatenate.25
  323.6 0.6 pad_bitcast_fusion.tail_ref
  324.2 3.0 multiply_convert_fusion
  327.2 33.1 %pack_grads.1 = bf16[55808,128]{1,0:T(8,128)(2,1)} custom-call(bf16[416,768]{1,0:T(8,128)(2,1)} %get-tuple-element.47.n1_ref, bf16[416,768]{1,0:T(8,128)(2,1)} %get-tuple-element.16.dq_ref, bf16[416,768]{1,0:T(8,128)(2,1)} %get-tuple-element.17.dk_ref, bf16[416,768]{1,0:T(8,128)(2,1)} %get-tuple-element.18.dv_ref, ...), custom_call_target="tpu_custom_call" | custom-call | tf_op jit(solution)/shard_map/pack_grads/pallas_call | solution.py:328
  360.3 162.2 %reduce-scatter.2.cloned.1.call-done = bf16[1744,128]{1,0:T(8,128)(2,1)} async-done(((bf16[55808,128]{1,0:T(8,128)(2,1)}), bf16[1744,128]{1,0:T(8,128)(2,1)}) %reduce-scatter.2.cloned.1.call-update) | async-done | bytes 446480 | tf_op jit(solution)/shard_map/reduce_scatter | solution.py:475
  522.6 68.2 %all-gather.6.cloned.1.call-done = bf16[27904,128]{1,0:T(8,128)(2,1)} async-done(((bf16[1744,128]{1,0:T(8,128)(2,1)}), bf16[27904,128]{1,0:T(8,128)(2,1)}) %all-gather.6.cloned.1.call-update) | async-done | bytes 7143440 | tf_op jit(solution)/shard_map/all_gather | solution.py:476
  590.8 8.6 %convert_element_type.203 = f32[27904,128]{1,0:T(8,128)} convert(bf16[27904,128]{1,0:T(8,128)(2,1)} %all-gather.6.cloned.1.call-done) | non-fusion elementwise | flops 3571712 | bytes 21430272 | tf_op jit(solution)/shard_map/convert_element_type | solution.py:476
  599.4 42.1 %fusion.51 = (bf16[27712,128]{1,0:T(8,128)(2,1)}, f32[27712,128]{1,0:T(8,128)}, f32[27712,128]{1,0:T(8,128)}, f32[27712,128]{1,0:T(8,128)}, f32[27712,128]{1,0:T(8,128)}) fusion(f32[27712,128]{1,0:T(8,128)} %param.9, f32[27904,128]{1,0:T(8,128)} %convert_element_type.203, f32[27712,128]{1,0:T(8,128)} %param.10, f32[27712,128]{1,0:T(8,128)} %param.11), kind=kLoop, calls=%fused_computation.135 | loop fusion | flops 60301312 | bytes 120602624 | tf_op jit(solution)/shard_map/convert_element_type | solution.py:488
  641.5 5.3 fusion.30
  646.9 1.3 copy.35
  648.2 1.3 copy.34
  649.5 1.3 fusion.35
  650.8 159.8 %all-gather.8.cloned.1.call-done = bf16[55424,128]{1,0:T(8,128)(2,1)} async-done(((bf16[27712,128]{1,0:T(8,128)(2,1)}), bf16[55424,128]{1,0:T(8,128)(2,1)}) %all-gather.8.cloned.1.call-update) | async-done | bytes 14188560 | tf_op jit(solution)/shard_map/all_gather | solution.py:488
  810.6 12.8 %copy.37 = bf16[55424,128]{1,0:T(8,128)(2,1)} copy(bf16[55424,128]{1,0:T(8,128)(2,1)} %all-gather.8.cloned.1.call-done) | data formatting | bytes 28377088
  (60 shorter events, 0.7 us)
Async XLA Ops:
  7.2 180.9 %all-gather.4.cloned.1.call-start = ((), (), s32[]{:S(2)}) async-start(), calls=%async_computation.1 | async-start | bytes 21282816 | tf_op jit(solution)/shard_map/all_gather | solution.py:458
  15.1 0.7 copy-start.9
  15.1 1.1 copy-start.6
  15.1 1.3 copy-start.7
  15.1 507.4 %reduce-scatter.2.cloned.1.call-start = ((), (), s32[]{:S(2)}) async-start(), calls=%async_computation.2 | async-start | bytes 14733312 | tf_op jit(solution)/shard_map/reduce_scatter | solution.py:475
  265.7 16.9 %slice-start = ((s8[4718592]{0:T(1024)(128)(4,1)}), s8[4194304]{0:T(1024)(128)(4,1)S(1)}, s32[]{:S(2)}) async-start(s8[4718592]{0:T(1024)(128)(4,1)} %bitcast.113), calls=%async_computation.5 | async-start | bytes 8388608
  265.7 20.7 %slice-start.2 = ((s8[4718592]{0:T(1024)(128)(4,1)}), s8[4194304]{0:T(1024)(128)(4,1)S(1)}, s32[]{:S(2)}) async-start(s8[4718592]{0:T(1024)(128)(4,1)} %bitcast.115), calls=%async_computation.7 | async-start | bytes 8388608
  266.0 16.6 %copy-start.4 = (bf16[416,768]{1,0:T(8,128)(2,1)}, bf16[416,768]{1,0:T(8,128)(2,1)S(1)}, u32[]{:S(2)}) copy-start(bf16[416,768]{1,0:T(8,128)(2,1)S(1)} %add_convert_fusion.1.n2_ref) | copy-start | bytes 1916932
  267.0 15.5 %slice-start.1 = ((s8[4718592]{0:T(1024)(128)(4,1)}), s8[524288]{0:T(1024)(128)(4,1)S(1)}, s32[]{:S(2)}) async-start(s8[4718592]{0:T(1024)(128)(4,1)} %bitcast.113), calls=%async_computation.6 | async-start | bytes 1048576
  267.0 19.3 %slice-start.3 = ((s8[4718592]{0:T(1024)(128)(4,1)}), s8[524288]{0:T(1024)(128)(4,1)S(1)}, s32[]{:S(2)}) async-start(s8[4718592]{0:T(1024)(128)(4,1)} %bitcast.115), calls=%async_computation.8 | async-start | bytes 1048576
  286.4 2.6 copy-start.2
  289.0 1.9 copy-start.1
  290.9 1.5 copy-start.3
  317.0 5.9 copy-start.8
  317.0 7.2 copy-start
  360.3 230.5 %all-gather.6.cloned.1.call-start = ((), (), s32[]{:S(2)}) async-start(), calls=%async_computation.3 | async-start | bytes 7589888 | tf_op jit(solution)/shard_map/all_gather | solution.py:476
  522.6 288.0 %all-gather.8.cloned.1.call-start = ((), (), s32[]{:S(2)}) async-start(), calls=%async_computation.4 | async-start | bytes 21282816 | tf_op jit(solution)/shard_map/all_gather | solution.py:488
  641.5 6.7 copy-start.5
Sparse Core Ops, SparseCore 0:
  15.2 172.8 all-gather.3
  360.4 162.0 reduce-scatter.1
  524.7 66.0 all-gather.5
  641.6 168.8 all-gather.7

commit v2 on v1

--- a/solution.py
+++ b/solution.py
@@ -448,6 +448,59 @@
     return (block_part, input_part, factors, tail)
 
 
+def swap(values, axis, bit):
+    return lax.ppermute(values, axis, [(i, i ^ bit) for i in range(lax.axis_size(axis))])
+
+
+def wide_bits(count):
+    place = lax.axis_index("wide")
+    return [(place >> bit) & 1 for bit in range(count)]
+
+
+def splits(part_rows):
+    return lax.axis_size("grp") == 2 and lax.axis_size("wide") % 8 == 0 and part_rows % 64 == 0
+
+
+def eighth_index(core, cross, deep):
+    return (core * 2 + cross) * 2 + deep
+
+
+def gather_groups(mine, diagonal, own):
+    core, cross, deep = wide_bits(3)
+    first = swap(mine, "grp", 1)
+    last = swap(diagonal, "grp", 1)
+    side = swap(first, "wide", 2)
+    back = swap(first, "wide", 4)
+    near = (first, side, back, last)
+    far = [swap(part, "wide", 1) for part in near]
+    group = lax.axis_index("grp")
+    out = jnp.zeros((2, 8) + mine.shape, mine.dtype)
+    out = lax.dynamic_update_slice(out, own.reshape((1, 8) + mine.shape), (group, 0, 0, 0))
+    for parts, which in ((near, core), (far, 1 - core)):
+        for part, flip_cross, flip_deep in zip(parts, (0, 1, 0, 1), (0, 0, 1, 1)):
+            at = eighth_index(which, cross ^ flip_cross, deep ^ flip_deep)
+            out = lax.dynamic_update_slice(out, part[None, None], (1 - group, at, 0, 0))
+    return out.reshape(2 * own.shape[0], 128)
+
+
+def own_eighths(rows):
+    core, cross, deep = wide_bits(3)
+    parts = rows.reshape(8, -1, 128)
+    spots = (eighth_index(core, cross, deep), eighth_index(core, 1 - cross, 1 - deep))
+    return [lax.dynamic_index_in_dim(parts, spot, keepdims=False) for spot in spots]
+
+
+def adam(grads, master, first_moment, second_moment):
+    moment_next = BETA_ONE * first_moment + (1.0 - BETA_ONE) * grads
+    second_next = BETA_TWO * second_moment + (1.0 - BETA_TWO) * grads * grads
+    fix_one = 1.0 - BETA_ONE**ADAM_STEP
+    fix_two = 1.0 - BETA_TWO**ADAM_STEP
+    update = (
+        moment_next / fix_one / (jnp.sqrt(second_next / fix_two) + ADAM_EPS) + DECAY_RATE * master
+    )
+    return (master - LEARN_RATE * update, moment_next, second_next)
+
+
 def body(tokens, cotangent, window_place, master, first_moment, second_moment):
     part_rows = master.shape[0]
     wide_size = lax.axis_size("wide")
@@ -455,7 +508,11 @@
     feature = tokens.shape[-1]
     micro_count, slots, tok_count, _ = tokens.shape
     masks = token_mask(window_place)
-    gathered = lax.all_gather(master.astype(jnp.bfloat16), "grp", axis=0, tiled=True)
+    if splits(part_rows):
+        mine, diagonal = (part.astype(jnp.bfloat16) for part in own_eighths(master))
+        gathered = gather_groups(mine, diagonal, master.astype(jnp.bfloat16))
+    else:
+        gathered = lax.all_gather(master.astype(jnp.bfloat16), "grp", axis=0, tiled=True)
     weights = unpack(gathered, feature)
     wins = micro_count * slots
     extra = -tok_count % 16
@@ -473,19 +530,25 @@
     tail = jnp.pad(tail, (0, tail_rows * 128 - tail.shape[0])).reshape(tail_rows, 128)
     packed, share_rows = pack_shares(factors, tail, part_rows, group_size, wide_size)
     owned = lax.psum_scatter(packed, ("grp", "wide"), scatter_dimension=0, tiled=True)
-    totals = lax.all_gather(owned, "wide", axis=0, tiled=True).astype(jnp.float32)
+    totals = lax.all_gather(owned, "wide", axis=0, tiled=True)
     factor = 1.0 / (micro_count * wide_size * group_size)
-    grads = totals[:part_rows] * factor
-    proj_bias_grad = totals[part_rows : part_rows + feature // 128].reshape(-1) * factor
-    moment_next = BETA_ONE * first_moment + (1.0 - BETA_ONE) * grads
-    second_next = BETA_TWO * second_moment + (1.0 - BETA_TWO) * grads * grads
-    fix_one = 1.0 - BETA_ONE**ADAM_STEP
-    fix_two = 1.0 - BETA_TWO**ADAM_STEP
-    update = (
-        moment_next / fix_one / (jnp.sqrt(second_next / fix_two) + ADAM_EPS) + DECAY_RATE * master
-    )
-    master_next = master - LEARN_RATE * update
-    weights_next = lax.all_gather(master_next.astype(jnp.bfloat16), "grp", axis=0, tiled=True)
+    bias_total = totals[part_rows : part_rows + feature // 128]
+    proj_bias_grad = bias_total.astype(jnp.float32).reshape(-1) * factor
+    totals = totals[:part_rows]
+
+    def step(total_rows, *state):
+        grads = total_rows.astype(jnp.float32) * factor
+        return (grads,) + adam(grads, *state)
+
+    state = (master, first_moment, second_moment)
+    grads, master_next, moment_next, second_next = step(totals, *state)
+    own_weights = master_next.astype(jnp.bfloat16)
+    if splits(part_rows):
+        pieces = zip(*(own_eighths(rows) for rows in (totals,) + state))
+        mine, diagonal = (step(*piece)[1].astype(jnp.bfloat16) for piece in pieces)
+        weights_next = gather_groups(mine, diagonal, own_weights)
+    else:
+        weights_next = lax.all_gather(own_weights, "grp", axis=0, tiled=True)
     block_out = block_part[:, :tok_count].reshape(tokens.shape)
     input_grad = input_part[:, :tok_count].reshape(tokens.shape)
     return (

time: 831 us -> 597 us (0.72); the launches traced: 830 us -> 587 us
  waiting for transfers between devices: 557 us -> 272 us
  local copies, waits for them, and re-layouts: 60.6 us -> 97.5 us
  starting transfers between devices: 0.16 us -> 10.6 us
    all_gather x3 -> x1, waiting for transfers between devices: 395 us -> 61.2 us  [body(): totals = lax.all_gather(owned, 'wide', axis=0, tiled=True)]
    ppermute x0 -> x16, waiting for transfers between devices: none -> 49.5 us  [swap(): lax.ppermute(values, axis, [(i, i ^ bit) for i in range(lax.axis_size(axi...]
    dynamic_update_slice x0 -> x18, local copies, waits for them, and re-layouts: none -> 28.4 us  [the longest x16 15.5 us: gather_groups(): out = lax.dynamic_update_slice(out, part[None, None], (1 - group, at, 0, 0))]
    another operation x0 -> x2, local copies, waits for them, and re-layouts: none -> 14.3 us
    unnamed x33 -> x26, local copies, waits for them, and re-layouts: 16.6 us -> 2.83 us
    ppermute x0 -> x16, starting transfers between devices: none -> 10.5 us  [swap(): lax.ppermute(values, axis, [(i, i ^ bit) for i in range(lax.axis_size(axi...]
  transfers between devices with their start and end apart: 4 -> 18, of which waited for: 4 -> 7; matrix products, arithmetic and copies ran while one was open for 2% -> 18% of each run, Pallas kernels for 0% -> 0%
where the time goes in v2:
time: 597 us; the launch traced here: 587 us
  waiting for transfers between devices  272 us (46%)
  local copies, waits for them, and re-layouts  97.5 us (16%)
  Pallas kernels  83.1 us (14%)
  other arithmetic  67.2 us (11%)
  matrix products  41.7 us (7%)
  between operations  14.5 us (2%)
  starting transfers between devices  10.6 us (2%)
    reduce_scatter x1, waiting for transfers between devices, body(): lax.psum_scatter(packed, ('grp', 'wide'), scatter_dimension=0, tiled=True)  162 us
    all_gather x1, waiting for transfers between devices, body(): totals = lax.all_gather(owned, 'wide', axis=0, tiled=True)  61.2 us
    ppermute x16, waiting for transfers between devices, swap(): lax.ppermute(values, axis, [(i, i ^ bit) for i in range(lax.axis_size(axi...  49.5 us
    convert_element_type x1, other arithmetic, body(): own_weights = master_next.astype(jnp.bfloat16)  38.4 us
    pallas_call x1, Pallas kernels, pack_shares(): pl.pallas_call(functools.partial(pack_kernel, part_rows=part_rows, share_...  33.2 us
    reshape x4, local copies, waits for them, and re-layouts, unpack(): members.append(rows[row:row + length].reshape(dims_of))  27.3 us
    pallas_call x1, Pallas kernels, attend(): pl.pallas_call(attend_kernel, grid=(wins, pairs), in_specs=[column(0), co...  25.3 us
    pallas_call x1, Pallas kernels, attend_back(): pl.pallas_call(attend_back_kernel, grid=(wins, pairs), in_specs=[column(0...  24.6 us
  transfers between devices with their start and end apart: 18, of which 7 were waited for; matrix products, arithmetic and copies ran while one was open for 18% of the time, Pallas kernels for 0%

profile of v2, /device:TPU:0, one launch (start us, length us, event | category | flops | bytes accessed | tf_op | source)
XLA Modules:
  0.0 587.0 jit_solution(11804785342532968172)
XLA Ops:
  7.2 3.5 bitcast_convert_fusion
  10.7 3.0 collective-permute-start.3
  15.1 1.4 copy_bitcast_fusion
  17.1 1.1 pad_convert_fusion
  18.2 7.9 %convert_element_type.190 = bf16[27712,128]{1,0:T(8,128)(2,1)} convert(f32[27712,128]{1,0:T(8,128)} %param.9) | non-fusion elementwise | flops 3547136 | bytes 21282816 | tf_op jit(solution)/shard_map/convert_element_type | solution.py:513
  26.3 1.3 fusion.60
  29.2 7.1 %broadcast.453.clone = bf16[2,8,3464,128]{3,2,1,0:T(8,128)(2,1)} broadcast(bf16[]{:T(256)} %constant.103.clone.1), dimensions={} | broadcast | bytes 14188546 | tf_op jit(solution)/shard_map/broadcast.45
  36.3 6.4 %constant_dynamic-update-slice_fusion.1 = bf16[2,8,3464,128]{3,2,1,0:T(8,128)(2,1)} fusion(bf16[2,8,3464,128]{3,2,1,0:T(8,128)(2,1)} %broadcast.453.clone, bf16[1,8,3464,128]{3,2,1,0:T(8,128)(2,1)} %bitcast.197, s32[]{:T(128)S(6)} %select_n.197), kind=kLoop, calls=%fused_computation.136 | loop fusion | bytes 14188548 | tf_op jit(solution)/shard_map/dynamic_update_slice | solution.py:478
  42.8 9.8 %collective-permute-done = bf16[3464,128]{1,0:T(8,128)(2,1)S(1)} collective-permute-done((bf16[3464,128]{1,0:T(8,128)(2,1)}, bf16[3464,128]{1,0:T(8,128)(2,1)S(1)}, u32[]{:S(2)}, u32[]{:S(2)}) %collective-permute-start) | collective-permute-done | bytes 886816 | tf_op jit(solution)/shard_map/ppermute | solution.py:452
  52.6 1.8 collective-permute-start.2
  54.4 1.5 collective-permute-start.1
  55.9 1.0 bitcast_dynamic-update-slice_fusion.15
  56.9 17.9 %collective-permute-done.2 = bf16[3464,128]{1,0:T(8,128)(2,1)S(1)} collective-permute-done((bf16[3464,128]{1,0:T(8,128)(2,1)S(1)}, bf16[3464,128]{1,0:T(8,128)(2,1)S(1)}, u32[]{:S(2)}, u32[]{:S(2)}) %collective-permute-start.2) | collective-permute-done | bytes 886816 | tf_op jit(solution)/shard_map/ppermute | solution.py:452
  74.8 1.5 collective-permute-done.1
  76.2 1.0 bitcast_dynamic-update-slice_fusion.14
  77.2 1.0 bitcast_dynamic-update-slice_fusion.13
  78.2 1.0 bitcast_dynamic-update-slice_fusion.12
  79.1 1.0 bitcast_dynamic-update-slice_fusion.11
  80.1 1.0 bitcast_dynamic-update-slice_fusion.10
  81.1 1.0 bitcast_dynamic-update-slice_fusion.9
  82.1 1.0 bitcast_dynamic-update-slice_fusion.8
  84.4 0.8 fusion.64
  85.2 1.6 slice.114
  86.8 3.4 slice.108
  90.2 9.3 %fusion.83 = (bf16[18432,128]{1,0:T(8,128)(2,1)}, bf16[18432,128]{1,0:T(8,128)(2,1)}) fusion(bf16[55424,128]{1,0:T(8,128)(2,1)} %bitcast.195), kind=kLoop, calls=%fused_computation.193 | loop fusion | bytes 18874368 | tf_op jit(solution)/shard_map/slice | solution.py:52
  100.0 1.9 reshape.497
  101.9 7.6 %reshape.496 = bf16[768,2304]{1,0:T(8,128)(2,1)} reshape(bf16[13824,128]{1,0:T(8,128)(2,1)} %slice.108) | data formatting | bytes 7077888 | tf_op jit(solution)/shard_map/reshape | solution.py:52
  109.5 9.2 %reshape.499 = bf16[3072,768]{1,0:T(8,128)(2,1)} reshape(bf16[18432,128]{1,0:T(8,128)(2,1)} %get-tuple-element.47) | data formatting | bytes 9437184 | tf_op jit(solution)/shard_map/reshape | solution.py:52
  119.9 5.0 fusion.19.q_ref.k_ref.v_ref
  124.9 25.3 %attend.1 = (bf16[2,12,208,208]{3,2,1,0:T(8,128)(2,1)}, bf16[416,768]{1,0:T(8,128)(2,1)}) custom-call(bf16[416,2304]{1,0:T(8,128)(2,1)} %fusion.19.q_ref.k_ref.v_ref, bf16[416,2304]{1,0:T(8,128)(2,1)} %fusion.19.q_ref.k_ref.v_ref, bf16[416,2304]{1,0:T(8,128)(2,1)} %fusion.19.q_ref.k_ref.v_ref, bf16[64,128]{1,0:T(8,128)(2,1)} %pad_maximum_fusion.table_ref, ...), custom_call_target="tpu_custom_call" | custom-call | tf_op jit(solution)/shard_map/attend/pallas_call | solution.py:169
  150.2 2.7 fusion.85
  153.2 8.6 %reshape.498 = bf16[768,3072]{1,0:T(8,128)(2,1)} reshape(bf16[18432,128]{1,0:T(8,128)(2,1)} %get-tuple-element.48) | data formatting | bytes 9437184 | tf_op jit(solution)/shard_map/reshape | solution.py:52
  162.0 15.1 %fusion.5 = (bf16[416,3072]{1,0:T(8,128)(2,1)}, f32[416,3072]{1,0:T(8,128)S(1)}) fusion(f32[3072]{0:T(1024)S(1)} %fusion.63, bf16[416,768]{1,0:T(8,128)(2,1)S(1)} %add_convert_fusion.1.n2_ref, bf16[768,3072]{1,0:T(8,128)(2,1)} %reshape.498), kind=kOutput, calls=%fused_computation.11 | convolution fusion | flops 2047279104 | bytes 13037568 | tf_op jit(solution)/shard_map/dot_general | solution.py:396
  177.2 3.6 fusion.11.dpre_ref
  180.8 2.6 multiply_reduce_fusion
  183.5 2.0 fusion.82
  185.4 1.5 convolution_convert_fusion.grad_ref
  187.0 24.6 %attend_back.1 = (bf16[416,768]{1,0:T(8,128)(2,1)}, bf16[416,768]{1,0:T(8,128)(2,1)}, bf16[416,768]{1,0:T(8,128)(2,1)}, f32[64,128]{1,0:T(8,128)}) custom-call(bf16[416,2304]{1,0:T(8,128)(2,1)} %fusion.19.q_ref.k_ref.v_ref, bf16[416,2304]{1,0:T(8,128)(2,1)} %fusion.19.q_ref.k_ref.v_ref, bf16[416,2304]{1,0:T(8,128)(2,1)} %fusion.19.q_ref.k_ref.v_ref, ...), custom_call_target="tpu_custom_call" | custom-call | tf_op jit(solution)/shard_map/attend_back/pallas_call | solution.py:191
  211.6 5.9 %fusion.78 = (f32[768]{0:T(1024)S(1)}, f32[768]{0:T(1024)S(1)}, f32[416]{0:T(512)S(1)}, f32[416]{0:T(512)S(1)}, f32[416,768]{1,0:T(8,128)}) fusion(f32[416]{0:T(512)S(1)} %rsqrt.22, f32[416]{0:T(512)S(1)} %div.133, bf16[2,196,768]{2,1,0:T(8,128)(2,1)S(1)} %get-tuple-element.75, f32[416,768]{1,0:T(8,128)} %fusion.60, f32[768]{0:T(1024)S(1)} %get-tuple-element.46, ...), kind=kOutput, calls=%fused_computation.190 | convolution fusion | flops 1481463552 | bytes 8631424 | tf_op jit(solution)/shard_map/nf,df->nd/dot_general | solution.py:425
  218.7 3.0 multiply_convert_fusion
  221.7 33.2 %pack_grads.1 = bf16[55808,128]{1,0:T(8,128)(2,1)} custom-call(bf16[416,768]{1,0:T(8,128)(2,1)} %get-tuple-element.51.n1_ref, bf16[416,768]{1,0:T(8,128)(2,1)} %get-tuple-element.16.dq_ref, bf16[416,768]{1,0:T(8,128)(2,1)} %get-tuple-element.17.dk_ref, bf16[416,768]{1,0:T(8,128)(2,1)} %get-tuple-element.18.dv_ref, ...), custom_call_target="tpu_custom_call" | custom-call | tf_op jit(solution)/shard_map/pack_grads/pallas_call | solution.py:328
  255.0 161.6 %reduce-scatter.2.cloned.1.call-done = bf16[1744,128]{1,0:T(8,128)(2,1)} async-done(((bf16[55808,128]{1,0:T(8,128)(2,1)}), bf16[1744,128]{1,0:T(8,128)(2,1)}) %reduce-scatter.2.cloned.1.call-update) | async-done | bytes 446480 | tf_op jit(solution)/shard_map/reduce_scatter | solution.py:532
  416.6 5.3 fusion.59
  422.0 1.3 copy.35
  423.3 1.3 copy.34
  424.6 61.2 %all-gather.2.cloned.1.call-done = bf16[27904,128]{1,0:T(8,128)(2,1)} async-done(((bf16[1744,128]{1,0:T(8,128)(2,1)}), bf16[27904,128]{1,0:T(8,128)(2,1)}) %all-gather.2.cloned.1.call-update) | async-done | bytes 7143440 | tf_op jit(solution)/shard_map/all_gather | solution.py:533
  485.8 3.0 slice-done
  488.8 5.6 fusion.50
  494.4 1.5 collective-permute-start.11
  496.5 38.4 %fusion.79 = (bf16[27712,128]{1,0:T(8,128)(2,1)}, f32[27712,128]{1,0:T(8,128)}, f32[27712,128]{1,0:T(8,128)}, f32[27712,128]{1,0:T(8,128)}, f32[27712,128]{1,0:T(8,128)}) fusion(f32[27712,128]{1,0:T(8,128)} %param.9, bf16[27904,128]{1,0:T(8,128)(2,1)} %all-gather.2.cloned.1.call-done, f32[27712,128]{1,0:T(8,128)} %param.10, f32[27712,128]{1,0:T(8,128)} %param.11), kind=kLoop, calls=%fused_computation.191 | loop fusion | flops 63848448 | bytes 113508352 | tf_op jit(solution)/shard_map/convert_element_type | solution.py:545
  535.0 1.3 multiply_bitcast_fusion
  536.2 7.1 %broadcast.453 = bf16[2,8,3464,128]{3,2,1,0:T(8,128)(2,1)} broadcast(bf16[]{:T(256)} %constant.103.clone.1), dimensions={} | broadcast | bytes 14188546 | tf_op jit(solution)/shard_map/broadcast.45
  543.3 6.4 %constant_dynamic-update-slice_fusion = bf16[2,8,3464,128]{3,2,1,0:T(8,128)(2,1)} fusion(bf16[2,8,3464,128]{3,2,1,0:T(8,128)(2,1)} %broadcast.453, bf16[1,8,3464,128]{3,2,1,0:T(8,128)(2,1)} %bitcast.196, s32[]{:T(128)S(6)} %select_n.197), kind=kLoop, calls=%fused_computation.135 | loop fusion | bytes 14188548 | tf_op jit(solution)/shard_map/dynamic_update_slice | solution.py:478
  549.8 1.6 collective-permute-start.10
  551.9 1.0 bitcast_dynamic-update-slice_fusion.7
  552.9 19.0 %collective-permute-done.10 = bf16[3464,128]{1,0:T(8,128)(2,1)S(1)} collective-permute-done((bf16[3464,128]{1,0:T(8,128)(2,1)S(1)}, bf16[3464,128]{1,0:T(8,128)(2,1)S(1)}, u32[]{:S(2)}, u32[]{:S(2)}) %collective-permute-start.10) | collective-permute-done | bytes 886816 | tf_op jit(solution)/shard_map/ppermute | solution.py:452
  571.9 1.3 collective-permute-done.9
  573.2 1.0 bitcast_dynamic-update-slice_fusion.6
  574.2 1.0 bitcast_dynamic-update-slice_fusion.5
  575.1 1.0 bitcast_dynamic-update-slice_fusion.4
  576.1 1.0 bitcast_dynamic-update-slice_fusion.3
  577.1 1.0 bitcast_dynamic-update-slice_fusion.2
  578.1 1.0 bitcast_dynamic-update-slice_fusion.1
  579.0 1.0 bitcast_dynamic-update-slice_fusion
  (102 shorter events, 10.1 us)
Async XLA Ops:
  7.2 409.4 %reduce-scatter.2.cloned.1.call-start = ((), (), s32[]{:S(2)}) async-start(), calls=%async_computation.1 | async-start | bytes 14733312 | tf_op jit(solution)/shard_map/reduce_scatter | solution.py:532
  10.7 45.2 %collective-permute-start.3 = (bf16[3464,128]{1,0:T(8,128)(2,1)}, bf16[3464,128]{1,0:T(8,128)(2,1)S(1)}, u32[]{:S(2)}, u32[]{:S(2)}) collective-permute-start(bf16[3464,128]{1,0:T(8,128)(2,1)} %get-tuple-element.49), channel_id=1, source_target_pairs={{0,1},{1,0},{2,3},{3,2},{4,5},{5,4},{6,7},{7,6},{8,9},{9,8},{10,11... | collective-permute-start | bytes 2660360 | tf_op jit(solution)/shard_map/ppermute | solution.py:452
  13.7 38.9 %collective-permute-start = (bf16[3464,128]{1,0:T(8,128)(2,1)}, bf16[3464,128]{1,0:T(8,128)(2,1)S(1)}, u32[]{:S(2)}, u32[]{:S(2)}) collective-permute-start(bf16[3464,128]{1,0:T(8,128)(2,1)} %get-tuple-element.50), channel_id=1, source_target_pairs={{0,1},{1,0},{2,3},{3,2},{4,5},{5,4},{6,7},{7,6},{8,9},{9,8},{10,11... | collective-permute-start | bytes 2660360 | tf_op jit(solution)/shard_map/ppermute | solution.py:452
  52.6 26.5 %collective-permute-start.4 = (bf16[3464,128]{1,0:T(8,128)(2,1)S(1)}, bf16[3464,128]{1,0:T(8,128)(2,1)S(1)}, u32[]{:S(2)}, u32[]{:S(2)}) collective-permute-start(bf16[3464,128]{1,0:T(8,128)(2,1)S(1)} %collective-permute-done), channel_id=1, source_target_pairs={{0,2},{2,0},{4,6},{6,4},{8,10},{10,8},{12,14},{14,12},{16,18},{18,... | collective-permute-start | bytes 2660360 | tf_op jit(solution)/shard_map/ppermute | solution.py:452
  52.6 22.2 %collective-permute-start.2 = (bf16[3464,128]{1,0:T(8,128)(2,1)S(1)}, bf16[3464,128]{1,0:T(8,128)(2,1)S(1)}, u32[]{:S(2)}, u32[]{:S(2)}) collective-permute-start(bf16[3464,128]{1,0:T(8,128)(2,1)S(1)} %collective-permute-done), channel_id=1, source_target_pairs={{0,8},{2,10},{4,12},{6,14},{8,0},{10,2},{12,4},{14,6},{16,24},{18,... | collective-permute-start | bytes 2660360 | tf_op jit(solution)/shard_map/ppermute | solution.py:452
  54.4 21.8 %collective-permute-start.1 = (bf16[3464,128]{1,0:T(8,128)(2,1)S(1)}, bf16[3464,128]{1,0:T(8,128)(2,1)S(1)}, u32[]{:S(2)}, u32[]{:S(2)}) collective-permute-start(bf16[3464,128]{1,0:T(8,128)(2,1)S(1)} %collective-permute-done), channel_id=1, source_target_pairs={{0,4},{2,6},{4,0},{6,2},{8,12},{10,14},{12,8},{14,10},{16,20},{18,... | collective-permute-start | bytes 2660360 | tf_op jit(solution)/shard_map/ppermute | solution.py:452
  55.9 26.2 %collective-permute-start.7 = (bf16[3464,128]{1,0:T(8,128)(2,1)S(1)}, bf16[3464,128]{1,0:T(8,128)(2,1)S(1)}, u32[]{:S(2)}, u32[]{:S(2)}) collective-permute-start(bf16[3464,128]{1,0:T(8,128)(2,1)S(1)} %collective-permute-done.3), channel_id=1, source_target_pairs={{0,2},{2,0},{4,6},{6,4},{8,10},{10,8},{12,14},{14,12},{16,18},{18,... | collective-permute-start | bytes 2660360 | tf_op jit(solution)/shard_map/ppermute | solution.py:452
  74.7 6.3 %collective-permute-start.6 = (bf16[3464,128]{1,0:T(8,128)(2,1)S(1)}, bf16[3464,128]{1,0:T(8,128)(2,1)S(1)}, u32[]{:S(2)}, u32[]{:S(2)}) collective-permute-start(bf16[3464,128]{1,0:T(8,128)(2,1)S(1)} %collective-permute-done.2), channel_id=1, source_target_pairs={{0,2},{2,0},{4,6},{6,4},{8,10},{10,8},{12,14},{14,12},{16,18},{18,... | collective-permute-start | bytes 2660360 | tf_op jit(solution)/shard_map/ppermute | solution.py:452
  76.2 3.9 collective-permute-start.5
  161.7 15.4 %slice-start.1 = ((s8[4718592]{0:T(1024)(128)(4,1)}), s8[4194304]{0:T(1024)(128)(4,1)S(1)}, s32[]{:S(2)}) async-start(s8[4718592]{0:T(1024)(128)(4,1)} %bitcast.203), calls=%async_computation.4 | async-start | bytes 8388608
  161.7 19.0 %slice-start.3 = ((s8[4718592]{0:T(1024)(128)(4,1)}), s8[4194304]{0:T(1024)(128)(4,1)S(1)}, s32[]{:S(2)}) async-start(s8[4718592]{0:T(1024)(128)(4,1)} %bitcast.205), calls=%async_computation.6 | async-start | bytes 8388608
  162.0 15.1 %copy-start.4 = (bf16[416,768]{1,0:T(8,128)(2,1)}, bf16[416,768]{1,0:T(8,128)(2,1)S(1)}, u32[]{:S(2)}) copy-start(bf16[416,768]{1,0:T(8,128)(2,1)S(1)} %add_convert_fusion.1.n2_ref) | copy-start | bytes 1916932
  162.0 15.1 %slice-start.2 = ((s8[4718592]{0:T(1024)(128)(4,1)}), s8[524288]{0:T(1024)(128)(4,1)S(1)}, s32[]{:S(2)}) async-start(s8[4718592]{0:T(1024)(128)(4,1)} %bitcast.203), calls=%async_computation.5 | async-start | bytes 1048576
  162.0 18.8 %slice-start.4 = ((s8[4718592]{0:T(1024)(128)(4,1)}), s8[524288]{0:T(1024)(128)(4,1)S(1)}, s32[]{:S(2)}) async-start(s8[4718592]{0:T(1024)(128)(4,1)} %bitcast.205), calls=%async_computation.7 | async-start | bytes 1048576
  180.8 2.6 copy-start.2
  183.4 2.0 copy-start.1
  185.4 1.6 copy-start.3
  211.5 5.9 %copy-start.6 = (f32[64,128]{1,0:T(8,128)S(1)}, f32[64,128]{1,0:T(8,128)}, u32[]{:S(2)}) copy-start(f32[64,128]{1,0:T(8,128)} %get-tuple-element.19) | copy-start | bytes 98308
  211.5 7.2 %copy-start = (f32[416,768]{1,0:T(8,128)S(1)}, f32[416,768]{1,0:T(8,128)}, u32[]{:S(2)}) copy-start(f32[416,768]{1,0:T(8,128)} %get-tuple-element.36) | copy-start | bytes 3833860
  254.9 230.9 %all-gather.2.cloned.1.call-start = ((), (), s32[]{:S(2)}) async-start(), calls=%async_computation.2 | async-start | bytes 7589888 | tf_op jit(solution)/shard_map/all_gather | solution.py:533
  416.6 6.7 %copy-start.5 = (bf16[416,768]{1,0:T(8,128)(2,1)S(1)}, bf16[416,768]{1,0:T(8,128)(2,1)}, u32[]{:S(2)}) copy-start(bf16[416,768]{1,0:T(8,128)(2,1)} %get-tuple-element.52) | copy-start | bytes 1916932
  485.8 3.0 slice-start
  494.4 57.5 %collective-permute-start.11 = (bf16[3464,128]{1,0:T(8,128)(2,1)S(1)}, bf16[3464,128]{1,0:T(8,128)(2,1)S(1)}, u32[]{:S(2)}, u32[]{:S(2)}) collective-permute-start(bf16[3464,128]{1,0:T(8,128)(2,1)S(1)} %get-tuple-element.37), channel_id=1, source_target_pairs={{0,1},{1,0},{2,3},{3,2},{4,5},{5,4},{6,7},{7,6},{8,9},{9,8},{10,11... | collective-permute-start | bytes 2660360 | tf_op jit(solution)/shard_map/ppermute | solution.py:452
  496.0 53.8 %collective-permute-start.8 = (bf16[3464,128]{1,0:T(8,128)(2,1)S(1)}, bf16[3464,128]{1,0:T(8,128)(2,1)S(1)}, u32[]{:S(2)}, u32[]{:S(2)}) collective-permute-start(bf16[3464,128]{1,0:T(8,128)(2,1)S(1)} %get-tuple-element.38), channel_id=1, source_target_pairs={{0,1},{1,0},{2,3},{3,2},{4,5},{5,4},{6,7},{7,6},{8,9},{9,8},{10,11... | collective-permute-start | bytes 2660360 | tf_op jit(solution)/shard_map/ppermute | solution.py:452
  549.8 26.3 %collective-permute-start.12 = (bf16[3464,128]{1,0:T(8,128)(2,1)S(1)}, bf16[3464,128]{1,0:T(8,128)(2,1)S(1)}, u32[]{:S(2)}, u32[]{:S(2)}) collective-permute-start(bf16[3464,128]{1,0:T(8,128)(2,1)S(1)} %collective-permute-done.8), channel_id=1, source_target_pairs={{0,2},{2,0},{4,6},{6,4},{8,10},{10,8},{12,14},{14,12},{16,18},{18,... | collective-permute-start | bytes 2660360 | tf_op jit(solution)/shard_map/ppermute | solution.py:452
  549.8 22.1 %collective-permute-start.10 = (bf16[3464,128]{1,0:T(8,128)(2,1)S(1)}, bf16[3464,128]{1,0:T(8,128)(2,1)S(1)}, u32[]{:S(2)}, u32[]{:S(2)}) collective-permute-start(bf16[3464,128]{1,0:T(8,128)(2,1)S(1)} %collective-permute-done.8), channel_id=1, source_target_pairs={{0,8},{2,10},{4,12},{6,14},{8,0},{10,2},{12,4},{14,6},{16,24},{18,... | collective-permute-start | bytes 2660360 | tf_op jit(solution)/shard_map/ppermute | solution.py:452
  551.4 21.8 %collective-permute-start.9 = (bf16[3464,128]{1,0:T(8,128)(2,1)S(1)}, bf16[3464,128]{1,0:T(8,128)(2,1)S(1)}, u32[]{:S(2)}, u32[]{:S(2)}) collective-permute-start(bf16[3464,128]{1,0:T(8,128)(2,1)S(1)} %collective-permute-done.8), channel_id=1, source_target_pairs={{0,4},{2,6},{4,0},{6,2},{8,12},{10,14},{12,8},{14,10},{16,20},{18,... | collective-permute-start | bytes 2660360 | tf_op jit(solution)/shard_map/ppermute | solution.py:452
  551.9 27.2 %collective-permute-start.15 = (bf16[3464,128]{1,0:T(8,128)(2,1)S(1)}, bf16[3464,128]{1,0:T(8,128)(2,1)S(1)}, u32[]{:S(2)}, u32[]{:S(2)}) collective-permute-start(bf16[3464,128]{1,0:T(8,128)(2,1)S(1)} %collective-permute-done.11), channel_id=1, source_target_pairs={{0,2},{2,0},{4,6},{6,4},{8,10},{10,8},{12,14},{14,12},{16,18},{18,... | collective-permute-start | bytes 2660360 | tf_op jit(solution)/shard_map/ppermute | solution.py:452
  571.9 6.2 %collective-permute-start.14 = (bf16[3464,128]{1,0:T(8,128)(2,1)S(1)}, bf16[3464,128]{1,0:T(8,128)(2,1)S(1)}, u32[]{:S(2)}, u32[]{:S(2)}) collective-permute-start(bf16[3464,128]{1,0:T(8,128)(2,1)S(1)} %collective-permute-done.10), channel_id=1, source_target_pairs={{0,2},{2,0},{4,6},{6,4},{8,10},{10,8},{12,14},{14,12},{16,18},{18,... | collective-permute-start | bytes 2660360 | tf_op jit(solution)/shard_map/ppermute | solution.py:452
  573.2 3.9 collective-permute-start.13
Sparse Core Ops, SparseCore 0:
  255.0 161.4 reduce-scatter.1
  418.7 67.0 all-gather.1

commit v3 on v2

--- a/solution.py
+++ b/solution.py
@@ -465,7 +465,7 @@
     return (core * 2 + cross) * 2 + deep
 
 
-def gather_groups(mine, diagonal, own):
+def gather_groups(mine, diagonal, finish, base):
     core, cross, deep = wide_bits(3)
     first = swap(mine, "grp", 1)
     last = swap(diagonal, "grp", 1)
@@ -474,7 +474,8 @@
     near = (first, side, back, last)
     far = [swap(part, "wide", 1) for part in near]
     group = lax.axis_index("grp")
-    out = jnp.zeros((2, 8) + mine.shape, mine.dtype)
+    own = finish(first)
+    out = base.reshape((2, 8) + mine.shape)
     out = lax.dynamic_update_slice(out, own.reshape((1, 8) + mine.shape), (group, 0, 0, 0))
     for parts, which in ((near, core), (far, 1 - core)):
         for part, flip_cross, flip_deep in zip(parts, (0, 1, 0, 1), (0, 0, 1, 1)):
@@ -490,15 +491,18 @@
     return [lax.dynamic_index_in_dim(parts, spot, keepdims=False) for spot in spots]
 
 
-def adam(grads, master, first_moment, second_moment):
-    moment_next = BETA_ONE * first_moment + (1.0 - BETA_ONE) * grads
+def first_step(grads, first_moment):
+    return BETA_ONE * first_moment + (1.0 - BETA_ONE) * grads
+
+
+def second_step(grads, master, moment_next, second_moment):
     second_next = BETA_TWO * second_moment + (1.0 - BETA_TWO) * grads * grads
     fix_one = 1.0 - BETA_ONE**ADAM_STEP
     fix_two = 1.0 - BETA_TWO**ADAM_STEP
     update = (
         moment_next / fix_one / (jnp.sqrt(second_next / fix_two) + ADAM_EPS) + DECAY_RATE * master
     )
-    return (master - LEARN_RATE * update, moment_next, second_next)
+    return (master - LEARN_RATE * update, second_next)
 
 
 def body(tokens, cotangent, window_place, master, first_moment, second_moment):
@@ -510,7 +514,12 @@
     masks = token_mask(window_place)
     if splits(part_rows):
         mine, diagonal = (part.astype(jnp.bfloat16) for part in own_eighths(master))
-        gathered = gather_groups(mine, diagonal, master.astype(jnp.bfloat16))
+        gathered = gather_groups(
+            mine,
+            diagonal,
+            lambda first: master.astype(jnp.bfloat16),
+            jnp.zeros((part_rows * group_size, 128), jnp.bfloat16),
+        )
     else:
         gathered = lax.all_gather(master.astype(jnp.bfloat16), "grp", axis=0, tiled=True)
     weights = unpack(gathered, feature)
@@ -536,19 +545,32 @@
     proj_bias_grad = bias_total.astype(jnp.float32).reshape(-1) * factor
     totals = totals[:part_rows]
 
-    def step(total_rows, *state):
-        grads = total_rows.astype(jnp.float32) * factor
-        return (grads,) + adam(grads, *state)
-
-    state = (master, first_moment, second_moment)
-    grads, master_next, moment_next, second_next = step(totals, *state)
-    own_weights = master_next.astype(jnp.bfloat16)
+    def scaled(total_rows):
+        return total_rows.astype(jnp.float32) * factor
+
+    grads = scaled(totals)
+    moment_next = first_step(grads, first_moment)
+    later = []
+
+    def finish(arrived):
+        held, moment, _ = lax.optimization_barrier((totals, first_moment, arrived))
+        held = scaled(held)
+        later.extend(second_step(held, master, first_step(held, moment), second_moment))
+        return later[0].astype(jnp.bfloat16)
+
     if splits(part_rows):
-        pieces = zip(*(own_eighths(rows) for rows in (totals,) + state))
-        mine, diagonal = (step(*piece)[1].astype(jnp.bfloat16) for piece in pieces)
-        weights_next = gather_groups(mine, diagonal, own_weights)
+        mine, diagonal = (
+            second_step(scaled(total), old, first_step(scaled(total), moment), second)[0].astype(
+                jnp.bfloat16
+            )
+            for total, old, moment, second in zip(
+                *(own_eighths(rows) for rows in (totals, master, first_moment, second_moment))
+            )
+        )
+        weights_next = gather_groups(mine, diagonal, finish, gathered)
     else:
-        weights_next = lax.all_gather(own_weights, "grp", axis=0, tiled=True)
+        weights_next = lax.all_gather(finish(totals), "grp", axis=0, tiled=True)
+    master_next, second_next = later
     block_out = block_part[:, :tok_count].reshape(tokens.shape)
     input_grad = input_part[:, :tok_count].reshape(tokens.shape)
     return (

time: 597 us -> 588 us (0.985)
  waiting for transfers between devices: 272 us -> 254 us
  other arithmetic: 67.2 us -> 76.6 us
    ppermute x16, waiting for transfers between devices: 49.5 us -> 31.3 us  [swap(): lax.ppermute(values, axis, [(i, i ^ bit) for i in range(lax.axis_size(axi...]
    add x0 -> x1, other arithmetic: none -> 16 us  [first_step(): return BETA_ONE * first_moment + (1.0 - BETA_ONE) * grads]
    another operation x2 -> x0, local copies, waits for them, and re-layouts: 14.3 us -> none
    reshape x0 -> x1, local copies, waits for them, and re-layouts: none -> 7.13 us  [gather_groups(): out = base.reshape((2, 8) + mine.shape)]
where the time goes in v3:
time: 588 us; the launch traced here: 577 us
  waiting for transfers between devices  254 us (43%)
  local copies, waits for them, and re-layouts  94.8 us (16%)
  Pallas kernels  83 us (14%)
  other arithmetic  76.6 us (13%)
  matrix products  41.7 us (7%)
  between operations  14.9 us (3%)
  starting transfers between devices  11.8 us (2%)
    reduce_scatter x1, waiting for transfers between devices, body(): lax.psum_scatter(packed, ('grp', 'wide'), scatter_dimension=0, tiled=True)  162 us
    all_gather x1, waiting for transfers between devices, body(): totals = lax.all_gather(owned, 'wide', axis=0, tiled=True)  61.3 us
    pallas_call x1, Pallas kernels, pack_shares(): pl.pallas_call(functools.partial(pack_kernel, part_rows=part_rows, share_...  32.9 us
    ppermute x16, waiting for transfers between devices, swap(): lax.ppermute(values, axis, [(i, i ^ bit) for i in range(lax.axis_size(axi...  31.3 us
    convert_element_type x1, other arithmetic, finish(): return later[0].astype(jnp.bfloat16)  30.3 us
    reshape x4, local copies, waits for them, and re-layouts, unpack(): members.append(rows[row:row + length].reshape(dims_of))  27.1 us
    pallas_call x1, Pallas kernels, attend(): pl.pallas_call(attend_kernel, grid=(wins, pairs), in_specs=[column(0), co...  25.3 us
    pallas_call x1, Pallas kernels, attend_back(): pl.pallas_call(attend_back_kernel, grid=(wins, pairs), in_specs=[column(0...  24.8 us
  transfers between devices with their start and end apart: 18, of which 7 were waited for; matrix products, arithmetic and copies ran while one was open for 18% of the time, Pallas kernels for 0%

profile of v3, /device:TPU:0, one launch (start us, length us, event | category | flops | bytes accessed | tf_op | source)
XLA Modules:
  0.0 577.0 jit_solution(3698968637788329422)
XLA Ops:
  7.2 3.5 bitcast_convert_fusion
  10.7 3.0 collective-permute-start
  13.7 7.9 %convert_element_type.195 = bf16[27712,128]{1,0:T(8,128)(2,1)} convert(f32[27712,128]{1,0:T(8,128)} %param.9) | non-fusion elementwise | flops 3547136 | bytes 21282816 | tf_op jit(solution)/shard_map/convert_element_type | solution.py:520
  21.7 1.4 copy_bitcast_fusion
  23.3 1.2 pad_convert_fusion
  25.0 1.3 fusion.66
  28.0 7.1 %reshape.496 = bf16[2,8,3464,128]{3,2,1,0:T(8,128)(2,1)} broadcast(bf16[]{:T(256)} %constant.104.clone.1), dimensions={} | broadcast | bytes 14188546 | tf_op jit(solution)/shard_map/reshape | solution.py:478
  35.1 6.4 %constant_dynamic-update-slice_fusion.1 = bf16[2,8,3464,128]{3,2,1,0:T(8,128)(2,1)} fusion(bf16[2,8,3464,128]{3,2,1,0:T(8,128)(2,1)} %reshape.496, bf16[1,8,3464,128]{3,2,1,0:T(8,128)(2,1)} %bitcast.201, s32[]{:T(128)S(6)} %select_n.197), kind=kLoop, calls=%fused_computation.143 | loop fusion | bytes 14188548 | tf_op jit(solution)/shard_map/dynamic_update_slice | solution.py:479
  41.6 2.0 collective-permute-start.1
  43.5 1.6 collective-permute-start.2
  45.1 7.5 %collective-permute-done.3 = bf16[3464,128]{1,0:T(8,128)(2,1)S(1)} collective-permute-done((bf16[3464,128]{1,0:T(8,128)(2,1)}, bf16[3464,128]{1,0:T(8,128)(2,1)S(1)}, u32[]{:S(2)}, u32[]{:S(2)}) %collective-permute-start.3) | collective-permute-done | bytes 886816 | tf_op jit(solution)/shard_map/ppermute | solution.py:452
  52.6 1.0 bitcast_dynamic-update-slice_fusion.15
  53.6 9.1 %collective-permute-done.1 = bf16[3464,128]{1,0:T(8,128)(2,1)S(1)} collective-permute-done((bf16[3464,128]{1,0:T(8,128)(2,1)S(1)}, bf16[3464,128]{1,0:T(8,128)(2,1)S(1)}, u32[]{:S(2)}, u32[]{:S(2)}) %collective-permute-start.1) | collective-permute-done | bytes 886816 | tf_op jit(solution)/shard_map/ppermute | solution.py:452
  62.7 1.4 collective-permute-done.2
  64.1 1.0 bitcast_dynamic-update-slice_fusion.14
  65.1 1.0 bitcast_dynamic-update-slice_fusion.13
  66.1 1.0 bitcast_dynamic-update-slice_fusion.12
  67.0 1.0 bitcast_dynamic-update-slice_fusion.11
  68.0 1.0 bitcast_dynamic-update-slice_fusion.10
  69.0 1.0 bitcast_dynamic-update-slice_fusion.9
  70.0 1.0 bitcast_dynamic-update-slice_fusion.8
  71.6 0.8 fusion.70
  72.5 3.4 slice.108
  75.8 1.6 slice.114
  77.4 9.3 %fusion.89 = (bf16[18432,128]{1,0:T(8,128)(2,1)}, bf16[18432,128]{1,0:T(8,128)(2,1)}) fusion(bf16[55424,128]{1,0:T(8,128)(2,1)} %bitcast.197), kind=kLoop, calls=%fused_computation.200 | loop fusion | bytes 18874368 | tf_op jit(solution)/shard_map/slice | solution.py:52
  87.9 7.6 %reshape.500 = bf16[768,2304]{1,0:T(8,128)(2,1)} reshape(bf16[13824,128]{1,0:T(8,128)(2,1)} %slice.108) | data formatting | bytes 7077888 | tf_op jit(solution)/shard_map/reshape | solution.py:52
  95.5 1.9 reshape.501
  98.6 5.0 fusion.25.q_ref.k_ref.v_ref
  103.6 25.3 %attend.1 = (bf16[2,12,208,208]{3,2,1,0:T(8,128)(2,1)}, bf16[416,768]{1,0:T(8,128)(2,1)}) custom-call(bf16[416,2304]{1,0:T(8,128)(2,1)} %fusion.25.q_ref.k_ref.v_ref, bf16[416,2304]{1,0:T(8,128)(2,1)} %fusion.25.q_ref.k_ref.v_ref, bf16[416,2304]{1,0:T(8,128)(2,1)} %fusion.25.q_ref.k_ref.v_ref, bf16[64,128]{1,0:T(8,128)(2,1)} %pad_maximum_fusion.table_ref, ...), custom_call_target="tpu_custom_call" | custom-call | tf_op jit(solution)/shard_map/attend/pallas_call | solution.py:169
  128.9 2.7 fusion.91
  131.9 8.4 %reshape.502 = bf16[768,3072]{1,0:T(8,128)(2,1)} reshape(bf16[18432,128]{1,0:T(8,128)(2,1)} %get-tuple-element.50) | data formatting | bytes 9437184 | tf_op jit(solution)/shard_map/reshape | solution.py:52
  140.2 9.2 %reshape.503 = bf16[3072,768]{1,0:T(8,128)(2,1)} reshape(bf16[18432,128]{1,0:T(8,128)(2,1)} %get-tuple-element.49) | data formatting | bytes 9437184 | tf_op jit(solution)/shard_map/reshape | solution.py:52
  149.8 15.1 %fusion.11 = (bf16[416,3072]{1,0:T(8,128)(2,1)}, f32[416,3072]{1,0:T(8,128)S(1)}) fusion(f32[3072]{0:T(1024)S(1)} %fusion.69, bf16[416,768]{1,0:T(8,128)(2,1)S(1)} %add_convert_fusion.1.n2_ref, bf16[768,3072]{1,0:T(8,128)(2,1)} %reshape.502), kind=kOutput, calls=%fused_computation.18 | convolution fusion | flops 2047279104 | bytes 13037568 | tf_op jit(solution)/shard_map/dot_general | solution.py:396
  164.9 3.6 fusion.17.dpre_ref
  168.5 2.6 multiply_reduce_fusion
  171.2 1.9 fusion.88
  173.1 1.5 convolution_convert_fusion.grad_ref
  174.6 24.8 %attend_back.1 = (bf16[416,768]{1,0:T(8,128)(2,1)}, bf16[416,768]{1,0:T(8,128)(2,1)}, bf16[416,768]{1,0:T(8,128)(2,1)}, f32[64,128]{1,0:T(8,128)}) custom-call(bf16[416,2304]{1,0:T(8,128)(2,1)} %fusion.25.q_ref.k_ref.v_ref, bf16[416,2304]{1,0:T(8,128)(2,1)} %fusion.25.q_ref.k_ref.v_ref, bf16[416,2304]{1,0:T(8,128)(2,1)} %fusion.25.q_ref.k_ref.v_ref, ...), custom_call_target="tpu_custom_call" | custom-call | tf_op jit(solution)/shard_map/attend_back/pallas_call | solution.py:191
  199.4 0.9 slice_bitcast_fusion
  200.8 6.0 %fusion.84 = (f32[768]{0:T(1024)S(1)}, f32[768]{0:T(1024)S(1)}, f32[416]{0:T(512)S(1)}, f32[416]{0:T(512)S(1)}, f32[416,768]{1,0:T(8,128)}) fusion(f32[416]{0:T(512)S(1)} %rsqrt.22, f32[416]{0:T(512)S(1)} %div.133, bf16[2,196,768]{2,1,0:T(8,128)(2,1)S(1)} %get-tuple-element.79, f32[416,768]{1,0:T(8,128)} %fusion.66, f32[768]{0:T(1024)S(1)} %get-tuple-element.48, ...), kind=kOutput, calls=%fused_computation.197 | convolution fusion | flops 1481463552 | bytes 8631424 | tf_op jit(solution)/shard_map/nf,df->nd/dot_general | solution.py:425
  207.5 3.0 multiply_convert_fusion
  210.4 32.9 %pack_grads.1 = bf16[55808,128]{1,0:T(8,128)(2,1)} custom-call(bf16[416,768]{1,0:T(8,128)(2,1)} %get-tuple-element.55.n1_ref, bf16[416,768]{1,0:T(8,128)(2,1)} %get-tuple-element.18.dq_ref, bf16[416,768]{1,0:T(8,128)(2,1)} %get-tuple-element.19.dk_ref, bf16[416,768]{1,0:T(8,128)(2,1)} %get-tuple-element.20.dv_ref, ...), custom_call_target="tpu_custom_call" | custom-call | tf_op jit(solution)/shard_map/pack_grads/pallas_call | solution.py:328
  243.4 161.6 %reduce-scatter.2.cloned.1.call-done = bf16[1744,128]{1,0:T(8,128)(2,1)} async-done(((bf16[55808,128]{1,0:T(8,128)(2,1)}), bf16[1744,128]{1,0:T(8,128)(2,1)}) %reduce-scatter.2.cloned.1.call-update) | async-done | bytes 446480 | tf_op jit(solution)/shard_map/reduce_scatter | solution.py:541
  405.2 1.3 copy.34
  406.4 5.3 fusion.65
  411.8 1.3 copy.35
  413.0 61.3 %all-gather.2.cloned.1.call-done = bf16[27904,128]{1,0:T(8,128)(2,1)} async-done(((bf16[1744,128]{1,0:T(8,128)(2,1)}), bf16[27904,128]{1,0:T(8,128)(2,1)}) %all-gather.2.cloned.1.call-update) | async-done | bytes 7143440 | tf_op jit(solution)/shard_map/all_gather | solution.py:542
  474.3 4.4 slice.124
  478.8 9.0 %fusion.56 = (bf16[3464,128]{1,0:T(8,128)(2,1)}, bf16[3464,128]{1,0:T(8,128)(2,1)S(1)}) fusion(f32[8,3464,128]{2,1,0:T(8,128)} %bitcast.205, s32[]{:T(128)S(6)} %select_n.202, f32[8,3464,128]{2,1,0:T(8,128)} %bitcast.192, f32[8,3464,128]{2,1,0:T(8,128)} %bitcast.189, bf16[8,3464,128]{2,1,0:T(8,128)(2,1)S(1)} %bitcast.200, s32[]{:T(128)S(6)} %select_n.198), kind=kLoop, calls=%fused_computation.82 | loop fusion | flops 15962112 | bytes 14188552 | tf_op jit(solution)/shard_map/convert_element_type | solution.py:563
  487.7 1.5 collective-permute-start.8
  489.8 16.0 %fusion = (f32[27712,128]{1,0:T(8,128)}, f32[27712,128]{1,0:T(8,128)}) fusion(f32[27712,128]{1,0:T(8,128)} %param.10, bf16[27904,128]{1,0:T(8,128)(2,1)S(1)} %bitcast.204), kind=kLoop, calls=%fused_computation.5 | loop fusion | flops 17735680 | bytes 49659904 | tf_op jit(solution)/shard_map/add | solution.py:495
  506.4 4.0 collective-permute-done.8
  510.4 30.3 %fusion.85 = (bf16[27712,128]{1,0:T(8,128)(2,1)}, f32[27712,128]{1,0:T(8,128)}, f32[27712,128]{1,0:T(8,128)}) fusion(f32[27712,128]{1,0:T(8,128)S(1)} %bitcast.191, bf16[27712,128]{1,0:T(8,128)(2,1)} %copy-done, f32[27712,128]{1,0:T(8,128)} %param.10, f32[27712,128]{1,0:T(8,128)} %param.11), kind=kLoop, calls=%fused_computation.198 | loop fusion | flops 63848448 | bytes 85131264 | tf_op jit(solution)/shard_map/convert_element_type | solution.py:559
  541.3 1.5 collective-permute-start.10
  542.9 6.4 %constant_dynamic-update-slice_fusion = bf16[2,8,3464,128]{3,2,1,0:T(8,128)(2,1)} fusion(bf16[2,8,3464,128]{3,2,1,0:T(8,128)(2,1)} %bitcast_dynamic-update-slice_fusion.8, bf16[1,8,3464,128]{3,2,1,0:T(8,128)(2,1)} %bitcast.202, s32[]{:T(128)S(6)} %select_n.197), kind=kLoop, calls=%fused_computation.142 | loop fusion | bytes 14188548 | tf_op jit(solution)/shard_map/dynamic_update_slice | solution.py:479
  549.8 2.1 bitcast_dynamic-update-slice_fusion.7
  551.9 9.3 %collective-permute-done.9 = bf16[3464,128]{1,0:T(8,128)(2,1)S(1)} collective-permute-done((bf16[3464,128]{1,0:T(8,128)(2,1)}, bf16[3464,128]{1,0:T(8,128)(2,1)S(1)}, u32[]{:S(2)}, u32[]{:S(2)}) %collective-permute-start.9) | collective-permute-done | bytes 886816 | tf_op jit(solution)/shard_map/ppermute | solution.py:452
  561.2 1.0 bitcast_dynamic-update-slice_fusion.6
  562.7 1.0 bitcast_dynamic-update-slice_fusion.5
  563.7 2.1 bitcast_dynamic-update-slice_fusion.4
  565.8 1.0 bitcast_dynamic-update-slice_fusion.3
  566.8 1.0 bitcast_dynamic-update-slice_fusion.2
  567.8 1.0 bitcast_dynamic-update-slice_fusion.1
  568.7 1.0 bitcast_dynamic-update-slice_fusion
  (117 shorter events, 10.4 us)
Async XLA Ops:
  7.2 397.9 %reduce-scatter.2.cloned.1.call-start = ((), (), s32[]{:S(2)}) async-start(), calls=%async_computation.1 | async-start | bytes 14733312 | tf_op jit(solution)/shard_map/reduce_scatter | solution.py:541
  10.7 30.9 %collective-permute-start = (bf16[3464,128]{1,0:T(8,128)(2,1)}, bf16[3464,128]{1,0:T(8,128)(2,1)S(1)}, u32[]{:S(2)}, u32[]{:S(2)}) collective-permute-start(bf16[3464,128]{1,0:T(8,128)(2,1)} %get-tuple-element.52), channel_id=1, source_target_pairs={{0,1},{1,0},{2,3},{3,2},{4,5},{5,4},{6,7},{7,6},{8,9},{9,8},{10,11... | collective-permute-start | bytes 2660360 | tf_op jit(solution)/shard_map/ppermute | solution.py:452
  13.7 38.9 %collective-permute-start.3 = (bf16[3464,128]{1,0:T(8,128)(2,1)}, bf16[3464,128]{1,0:T(8,128)(2,1)S(1)}, u32[]{:S(2)}, u32[]{:S(2)}) collective-permute-start(bf16[3464,128]{1,0:T(8,128)(2,1)} %get-tuple-element.51), channel_id=1, source_target_pairs={{0,1},{1,0},{2,3},{3,2},{4,5},{5,4},{6,7},{7,6},{8,9},{9,8},{10,11... | collective-permute-start | bytes 2660360 | tf_op jit(solution)/shard_map/ppermute | solution.py:452
  13.7 7.9 %copy-start.7 = (s32[2,1]{0,1:T(1,128)S(1)}, s32[2,1]{0,1:T(1,128)}, u32[]{:S(2)}) copy-start(s32[2,1]{0,1:T(1,128)} %param.8) | copy-start | bytes 28
  41.6 21.1 %collective-permute-start.1 = (bf16[3464,128]{1,0:T(8,128)(2,1)S(1)}, bf16[3464,128]{1,0:T(8,128)(2,1)S(1)}, u32[]{:S(2)}, u32[]{:S(2)}) collective-permute-start(bf16[3464,128]{1,0:T(8,128)(2,1)S(1)} %collective-permute-done), channel_id=1, source_target_pairs={{0,4},{2,6},{4,0},{6,2},{8,12},{10,14},{12,8},{14,10},{16,20},{18,... | collective-permute-start | bytes 2660360 | tf_op jit(solution)/shard_map/ppermute | solution.py:452
  43.5 20.6 %collective-permute-start.2 = (bf16[3464,128]{1,0:T(8,128)(2,1)S(1)}, bf16[3464,128]{1,0:T(8,128)(2,1)S(1)}, u32[]{:S(2)}, u32[]{:S(2)}) collective-permute-start(bf16[3464,128]{1,0:T(8,128)(2,1)S(1)} %collective-permute-done), channel_id=1, source_target_pairs={{0,8},{2,10},{4,12},{6,14},{8,0},{10,2},{12,4},{14,6},{16,24},{18,... | collective-permute-start | bytes 2660360 | tf_op jit(solution)/shard_map/ppermute | solution.py:452
  45.1 21.9 %collective-permute-start.4 = (bf16[3464,128]{1,0:T(8,128)(2,1)S(1)}, bf16[3464,128]{1,0:T(8,128)(2,1)S(1)}, u32[]{:S(2)}, u32[]{:S(2)}) collective-permute-start(bf16[3464,128]{1,0:T(8,128)(2,1)S(1)} %collective-permute-done), channel_id=1, source_target_pairs={{0,2},{2,0},{4,6},{6,4},{8,10},{10,8},{12,14},{14,12},{16,18},{18,... | collective-permute-start | bytes 2660360 | tf_op jit(solution)/shard_map/ppermute | solution.py:452
  52.6 17.4 %collective-permute-start.7 = (bf16[3464,128]{1,0:T(8,128)(2,1)S(1)}, bf16[3464,128]{1,0:T(8,128)(2,1)S(1)}, u32[]{:S(2)}, u32[]{:S(2)}) collective-permute-start(bf16[3464,128]{1,0:T(8,128)(2,1)S(1)} %collective-permute-done.3), channel_id=1, source_target_pairs={{0,2},{2,0},{4,6},{6,4},{8,10},{10,8},{12,14},{14,12},{16,18},{18,... | collective-permute-start | bytes 2660360 | tf_op jit(solution)/shard_map/ppermute | solution.py:452
  62.7 5.3 collective-permute-start.5
  64.1 4.9 collective-permute-start.6
  149.5 15.4 %slice-start.6 = ((s8[4718592]{0:T(1024)(128)(4,1)}), s8[4194304]{0:T(1024)(128)(4,1)S(1)}, s32[]{:S(2)}) async-start(s8[4718592]{0:T(1024)(128)(4,1)} %bitcast.207), calls=%async_computation.9 | async-start | bytes 8388608
  149.5 19.0 %slice-start.8 = ((s8[4718592]{0:T(1024)(128)(4,1)}), s8[4194304]{0:T(1024)(128)(4,1)S(1)}, s32[]{:S(2)}) async-start(s8[4718592]{0:T(1024)(128)(4,1)} %bitcast.209), calls=%async_computation.11 | async-start | bytes 8388608
  149.7 15.1 %copy-start.5 = (bf16[416,768]{1,0:T(8,128)(2,1)}, bf16[416,768]{1,0:T(8,128)(2,1)S(1)}, u32[]{:S(2)}) copy-start(bf16[416,768]{1,0:T(8,128)(2,1)S(1)} %add_convert_fusion.1.n2_ref) | copy-start | bytes 1916932
  149.7 15.1 %slice-start.7 = ((s8[4718592]{0:T(1024)(128)(4,1)}), s8[524288]{0:T(1024)(128)(4,1)S(1)}, s32[]{:S(2)}) async-start(s8[4718592]{0:T(1024)(128)(4,1)} %bitcast.207), calls=%async_computation.10 | async-start | bytes 1048576
  149.8 18.7 %slice-start.9 = ((s8[4718592]{0:T(1024)(128)(4,1)}), s8[524288]{0:T(1024)(128)(4,1)S(1)}, s32[]{:S(2)}) async-start(s8[4718592]{0:T(1024)(128)(4,1)} %bitcast.209), calls=%async_computation.12 | async-start | bytes 1048576
  168.5 2.6 copy-start.3
  171.1 1.9 copy-start.2
  173.1 1.6 copy-start.4
  200.8 6.7 %copy-start.1 = (f32[416,768]{1,0:T(8,128)S(1)}, f32[416,768]{1,0:T(8,128)}, u32[]{:S(2)}) copy-start(f32[416,768]{1,0:T(8,128)} %get-tuple-element.38) | copy-start | bytes 3833860
  243.4 161.7 %copy-start.6 = (bf16[416,768]{1,0:T(8,128)(2,1)S(1)}, bf16[416,768]{1,0:T(8,128)(2,1)}, u32[]{:S(2)}) copy-start(bf16[416,768]{1,0:T(8,128)(2,1)} %get-tuple-element.56) | copy-start | bytes 1916932
  243.4 230.9 %all-gather.2.cloned.1.call-start = ((), (), s32[]{:S(2)}) async-start(), calls=%async_computation.2 | async-start | bytes 7589888 | tf_op jit(solution)/shard_map/all_gather | solution.py:542
  474.3 15.4 %slice-start.4 = ((s8[7143424]{0:T(1024)(128)(4,1)}), s8[4194304]{0:T(1024)(128)(4,1)S(1)}, s32[]{:S(2)}) async-start(s8[7143424]{0:T(1024)(128)(4,1)} %bitcast.203), calls=%async_computation.7 | async-start | bytes 8388608
  478.7 9.0 %copy-start = (bf16[27712,128]{1,0:T(8,128)(2,1)}, bf16[27712,128]{1,0:T(8,128)(2,1)S(1)}, u32[]{:S(2)}) copy-start(bf16[27712,128]{1,0:T(8,128)(2,1)S(1)} %slice.124) | copy-start | bytes 21282820
  478.8 11.0 %slice-start.5 = ((s8[7143424]{0:T(1024)(128)(4,1)}), s8[2949120]{0:T(1024)(128)(4,1)S(1)}, s32[]{:S(2)}) async-start(s8[7143424]{0:T(1024)(128)(4,1)} %bitcast.203), calls=%async_computation.8 | async-start | bytes 5898240
  478.8 31.6 %slice-start = ((s8[14188544]{0:T(1024)(128)(4,1)}), s8[4194304]{0:T(1024)(128)(4,1)S(1)}, s32[]{:S(2)}) async-start(s8[14188544]{0:T(1024)(128)(4,1)} %bitcast.190), calls=%async_computation.3 | async-start | bytes 8388608
  487.7 22.7 %collective-permute-start.8 = (bf16[3464,128]{1,0:T(8,128)(2,1)S(1)}, bf16[3464,128]{1,0:T(8,128)(2,1)}, u32[]{:S(2)}, u32[]{:S(2)}) collective-permute-start(bf16[3464,128]{1,0:T(8,128)(2,1)S(1)} %get-tuple-element.40), channel_id=1, source_target_pairs={{0,1},{1,0},{2,3},{3,2},{4,5},{5,4},{6,7},{7,6},{8,9},{9,8},{10,11... | collective-permute-start | bytes 2660360 | tf_op jit(solution)/shard_map/ppermute | solution.py:452
  489.2 21.2 %slice-start.1 = ((s8[14188544]{0:T(1024)(128)(4,1)}), s8[4194304]{0:T(1024)(128)(4,1)S(1)}, s32[]{:S(2)}) async-start(s8[14188544]{0:T(1024)(128)(4,1)} %bitcast.190), calls=%async_computation.4 | async-start | bytes 8388608
  489.2 21.2 %slice-start.2 = ((s8[14188544]{0:T(1024)(128)(4,1)}), s8[4194304]{0:T(1024)(128)(4,1)S(1)}, s32[]{:S(2)}) async-start(s8[14188544]{0:T(1024)(128)(4,1)} %bitcast.190), calls=%async_computation.5 | async-start | bytes 8388608
  489.2 21.2 %slice-start.3 = ((s8[14188544]{0:T(1024)(128)(4,1)}), s8[1605632]{0:T(1024)(128)(4,1)S(1)}, s32[]{:S(2)}) async-start(s8[14188544]{0:T(1024)(128)(4,1)} %bitcast.190), calls=%async_computation.6 | async-start | bytes 3211264
  489.2 60.1 %collective-permute-start.11 = (bf16[3464,128]{1,0:T(8,128)(2,1)}, bf16[3464,128]{1,0:T(8,128)(2,1)}, u32[]{:S(2)}, u32[]{:S(2)}) collective-permute-start(bf16[3464,128]{1,0:T(8,128)(2,1)} %get-tuple-element.39), channel_id=1, source_target_pairs={{0,1},{1,0},{2,3},{3,2},{4,5},{5,4},{6,7},{7,6},{8,9},{9,8},{10,11... | collective-permute-start | bytes 2660360 | tf_op jit(solution)/shard_map/ppermute | solution.py:452
  540.8 20.4 %collective-permute-start.9 = (bf16[3464,128]{1,0:T(8,128)(2,1)}, bf16[3464,128]{1,0:T(8,128)(2,1)S(1)}, u32[]{:S(2)}, u32[]{:S(2)}) collective-permute-start(bf16[3464,128]{1,0:T(8,128)(2,1)} %collective-permute-done.8), channel_id=1, source_target_pairs={{0,4},{2,6},{4,0},{6,2},{8,12},{10,14},{12,8},{14,10},{16,20},{18,... | collective-permute-start | bytes 2660360 | tf_op jit(solution)/shard_map/ppermute | solution.py:452
  541.3 20.9 %collective-permute-start.10 = (bf16[3464,128]{1,0:T(8,128)(2,1)}, bf16[3464,128]{1,0:T(8,128)(2,1)S(1)}, u32[]{:S(2)}, u32[]{:S(2)}) collective-permute-start(bf16[3464,128]{1,0:T(8,128)(2,1)} %collective-permute-done.8), channel_id=1, source_target_pairs={{0,8},{2,10},{4,12},{6,14},{8,0},{10,2},{12,4},{14,6},{16,24},{18,... | collective-permute-start | bytes 2660360 | tf_op jit(solution)/shard_map/ppermute | solution.py:452
  542.9 23.0 %collective-permute-start.12 = (bf16[3464,128]{1,0:T(8,128)(2,1)}, bf16[3464,128]{1,0:T(8,128)(2,1)S(1)}, u32[]{:S(2)}, u32[]{:S(2)}) collective-permute-start(bf16[3464,128]{1,0:T(8,128)(2,1)} %collective-permute-done.8), channel_id=1, source_target_pairs={{0,2},{2,0},{4,6},{6,4},{8,10},{10,8},{12,14},{14,12},{16,18},{18,... | collective-permute-start | bytes 2660360 | tf_op jit(solution)/shard_map/ppermute | solution.py:452
  549.3 19.4 %collective-permute-start.15 = (bf16[3464,128]{1,0:T(8,128)(2,1)}, bf16[3464,128]{1,0:T(8,128)(2,1)S(1)}, u32[]{:S(2)}, u32[]{:S(2)}) collective-permute-start(bf16[3464,128]{1,0:T(8,128)(2,1)} %collective-permute-done.11), channel_id=1, source_target_pairs={{0,2},{2,0},{4,6},{6,4},{8,10},{10,8},{12,14},{14,12},{16,18},{18,... | collective-permute-start | bytes 2660360 | tf_op jit(solution)/shard_map/ppermute | solution.py:452
  561.2 5.6 collective-permute-start.13
  562.2 5.6 collective-permute-start.14
Sparse Core Ops, SparseCore 0:
  243.5 161.5 reduce-scatter.1
  407.2 67.0 all-gather.1

commit v4 on v3

--- a/solution.py
+++ b/solution.py
@@ -484,6 +484,42 @@
     return out.reshape(2 * own.shape[0], 128)
 
 
+def halve(values, names, name, exchange, bit):
+    axis = names.index(name)
+    sent = exchange(lax.dynamic_index_in_dim(values, 1 - bit, axis, keepdims=False))
+    kept = lax.dynamic_index_in_dim(values, bit, axis, keepdims=False)
+    total = (kept.astype(jnp.float32) + sent.astype(jnp.float32)).astype(values.dtype)
+    return total, [other for other in names if other != name]
+
+
+def reduce_shares(packed):
+    wide_size = lax.axis_size("wide")
+    group_size = lax.axis_size("grp")
+    if (wide_size, group_size) != (16, 2):
+        return lax.psum_scatter(packed, ("grp", "wide"), scatter_dimension=0, tiled=True)
+    share = packed.shape[0] // 32
+    core, cross, deep, far = wide_bits(4)
+    moves = {
+        "core": (lambda v: swap(v, "wide", 1), core),
+        "x": (lambda v: swap(v, "wide", 2), cross),
+        "near": (lambda v: swap(v, "wide", 4), deep),
+        "far": (lambda v: swap(v, "wide", 8), far),
+        "y": (lambda v: swap(v, "grp", 1), lax.axis_index("grp")),
+    }
+    blocks = packed.reshape(2, 2, 2, 2, 2, share, 128)
+    units = share // 16
+    cuts = [0, (units + 2) // 3 * 16, ((units + 2) // 3 + (units + 1) // 3) * 16, share]
+    orders = (("y", "x", "near"), ("x", "near", "y"), ("near", "y", "x"))
+    done = []
+    for low, high, order in zip(cuts, cuts[1:], orders):
+        part = blocks[..., low:high, :]
+        names = ["y", "far", "near", "x", "core"]
+        for name in ("core",) + order + ("far",):
+            part, names = halve(part, names, name, *moves[name])
+        done.append(part)
+    return jnp.concatenate(done, 0)
+
+
 def own_eighths(rows):
     core, cross, deep = wide_bits(3)
     parts = rows.reshape(8, -1, 128)
@@ -537,8 +573,8 @@
     tail = jnp.concatenate([member.reshape(-1) for member in tail])
     tail_rows = part_rows * group_size - filled
     tail = jnp.pad(tail, (0, tail_rows * 128 - tail.shape[0])).reshape(tail_rows, 128)
-    packed, share_rows = pack_shares(factors, tail, part_rows, group_size, wide_size)
-    owned = lax.psum_scatter(packed, ("grp", "wide"), scatter_dimension=0, tiled=True)
+    packed, _ = pack_shares(factors, tail, part_rows, group_size, wide_size)
+    owned = reduce_shares(packed)
     totals = lax.all_gather(owned, "wide", axis=0, tiled=True)
     factor = 1.0 / (micro_count * wide_size * group_size)
     bias_total = totals[part_rows : part_rows + feature // 128]

time: 588 us -> 531 us (0.903)
  waiting for transfers between devices: 254 us -> 135 us
  local copies, waits for them, and re-layouts: 94.8 us -> 122 us
  starting transfers between devices: 11.8 us -> 33.5 us
  other arithmetic: 76.6 us -> 90.3 us
    reduce_scatter x1 -> x0, waiting for transfers between devices: 162 us -> none  [body(): lax.psum_scatter(packed, ('grp', 'wide'), scatter_dimension=0, tiled=True)]
    ppermute x16 -> x31, waiting for transfers between devices: 31.3 us -> 76.6 us  [swap(): lax.ppermute(values, axis, [(i, i ^ bit) for i in range(lax.axis_size(axi...]
    ppermute x16 -> x31, starting transfers between devices: 11.7 us -> 33.5 us  [swap(): lax.ppermute(values, axis, [(i, i ^ bit) for i in range(lax.axis_size(axi...]
    convert_element_type x0 -> x15, other arithmetic: none -> 12.6 us  [halve(): (kept.astype(jnp.float32) + sent.astype(jnp.float32)).astype(values.dtype)]
    slice x0 -> x2, local copies, waits for them, and re-layouts: none -> 9.73 us  [reduce_shares(): part = blocks[..., low:high, :]]
    dynamic_slice x0 -> x3, local copies, waits for them, and re-layouts: none -> 7.53 us  [halve(): kept = lax.dynamic_index_in_dim(values, bit, axis, keepdims=False)]
    unnamed x40 -> x57, local copies, waits for them, and re-layouts: 2.86 us -> 9.22 us
  transfers between devices with their start and end apart: 18 -> 32, of which waited for: 7 -> 16; matrix products, arithmetic and copies ran while one was open for 18% -> 25% of each run, Pallas kernels for 0% -> 0%
where the time goes in v4:
time: 531 us; the launch traced here: 521 us
  waiting for transfers between devices  135 us (25%)
  local copies, waits for them, and re-layouts  122 us (23%)
  other arithmetic  90.3 us (17%)
  Pallas kernels  82.9 us (16%)
  matrix products  41.8 us (8%)
  starting transfers between devices  33.5 us (6%)
  between operations  15.1 us (3%)
    ppermute x31, waiting for transfers between devices, swap(): lax.ppermute(values, axis, [(i, i ^ bit) for i in range(lax.axis_size(axi...  76.6 us
    all_gather x1, waiting for transfers between devices, body(): totals = lax.all_gather(owned, 'wide', axis=0, tiled=True)  58.9 us
    ppermute x31, starting transfers between devices, swap(): lax.ppermute(values, axis, [(i, i ^ bit) for i in range(lax.axis_size(axi...  33.5 us
    pallas_call x1, Pallas kernels, pack_shares(): pl.pallas_call(functools.partial(pack_kernel, part_rows=part_rows, share_...  33 us
    convert_element_type x1, other arithmetic, finish(): return later[0].astype(jnp.bfloat16)  30.3 us
    reshape x4, local copies, waits for them, and re-layouts, unpack(): members.append(rows[row:row + length].reshape(dims_of))  27.1 us
    pallas_call x1, Pallas kernels, attend(): pl.pallas_call(attend_kernel, grid=(wins, pairs), in_specs=[column(0), co...  25.3 us
    pallas_call x1, Pallas kernels, attend_back(): pl.pallas_call(attend_back_kernel, grid=(wins, pairs), in_specs=[column(0...  24.6 us
  transfers between devices with their start and end apart: 32, of which 16 were waited for; matrix products, arithmetic and copies ran while one was open for 25% of the time, Pallas kernels for 0%

profile of v4, /device:TPU:0, one launch (start us, length us, event | category | flops | bytes accessed | tf_op | source)
XLA Modules:
  0.0 521.0 jit_solution(1394978564208096560)
XLA Ops:
  7.2 3.5 bitcast_convert_fusion
  10.7 3.0 collective-permute-start
  13.7 7.9 %convert_element_type.375 = bf16[27712,128]{1,0:T(8,128)(2,1)} convert(f32[27712,128]{1,0:T(8,128)} %param.9) | non-fusion elementwise | flops 3547136 | bytes 21282816 | tf_op jit(solution)/shard_map/convert_element_type | solution.py:556
  28.0 7.1 %reshape.529 = bf16[2,8,3464,128]{3,2,1,0:T(8,128)(2,1)} broadcast(bf16[]{:T(256)} %constant.274.clone.1), dimensions={} | broadcast | bytes 14188546 | tf_op jit(solution)/shard_map/reshape | solution.py:478
  35.1 6.4 %constant_dynamic-update-slice_fusion.1 = bf16[2,8,3464,128]{3,2,1,0:T(8,128)(2,1)} fusion(bf16[2,8,3464,128]{3,2,1,0:T(8,128)(2,1)} %reshape.529, bf16[1,8,3464,128]{3,2,1,0:T(8,128)(2,1)} %bitcast.288, s32[]{:T(128)S(6)} %select_n.256), kind=kLoop, calls=%fused_computation.198 | loop fusion | bytes 14188548 | tf_op jit(solution)/shard_map/dynamic_update_slice | solution.py:479
  41.5 2.0 collective-permute-start.1
  43.5 1.6 collective-permute-start.2
  45.1 7.5 %collective-permute-done.3 = bf16[3464,128]{1,0:T(8,128)(2,1)S(1)} collective-permute-done((bf16[3464,128]{1,0:T(8,128)(2,1)}, bf16[3464,128]{1,0:T(8,128)(2,1)S(1)}, u32[]{:S(2)}, u32[]{:S(2)}) %collective-permute-start.3) | collective-permute-done | bytes 886816 | tf_op jit(solution)/shard_map/ppermute | solution.py:452
  53.6 9.1 %collective-permute-done.1 = bf16[3464,128]{1,0:T(8,128)(2,1)S(1)} collective-permute-done((bf16[3464,128]{1,0:T(8,128)(2,1)S(1)}, bf16[3464,128]{1,0:T(8,128)(2,1)S(1)}, u32[]{:S(2)}, u32[]{:S(2)}) %collective-permute-start.1) | collective-permute-done | bytes 886816 | tf_op jit(solution)/shard_map/ppermute | solution.py:452
  72.4 3.4 slice.120
  75.8 1.6 slice.126
  77.4 9.3 %fusion.105 = (bf16[18432,128]{1,0:T(8,128)(2,1)}, bf16[18432,128]{1,0:T(8,128)(2,1)}) fusion(bf16[55424,128]{1,0:T(8,128)(2,1)} %bitcast.284), kind=kLoop, calls=%fused_computation.256 | loop fusion | bytes 18874368 | tf_op jit(solution)/shard_map/slice | solution.py:52
  87.9 7.6 %reshape.533 = bf16[768,2304]{1,0:T(8,128)(2,1)} reshape(bf16[13824,128]{1,0:T(8,128)(2,1)} %slice.120) | data formatting | bytes 7077888 | tf_op jit(solution)/shard_map/reshape | solution.py:52
  95.5 1.9 reshape.534
  98.6 5.0 fusion.28.q_ref.k_ref.v_ref
  103.6 25.3 %attend.1 = (bf16[2,12,208,208]{3,2,1,0:T(8,128)(2,1)}, bf16[416,768]{1,0:T(8,128)(2,1)}) custom-call(bf16[416,2304]{1,0:T(8,128)(2,1)} %fusion.28.q_ref.k_ref.v_ref, bf16[416,2304]{1,0:T(8,128)(2,1)} %fusion.28.q_ref.k_ref.v_ref, bf16[416,2304]{1,0:T(8,128)(2,1)} %fusion.28.q_ref.k_ref.v_ref, bf16[64,128]{1,0:T(8,128)(2,1)} %pad_maximum_fusion.1.table_ref, ...), custom_call_target="tpu_custom_call" | custom-call | tf_op jit(solution)/shard_map/attend/pallas_call | solution.py:169
  128.9 2.6 fusion.107
  131.8 8.4 %reshape.535 = bf16[768,3072]{1,0:T(8,128)(2,1)} reshape(bf16[18432,128]{1,0:T(8,128)(2,1)} %get-tuple-element.52) | data formatting | bytes 9437184 | tf_op jit(solution)/shard_map/reshape | solution.py:52
  140.2 9.2 %reshape.536 = bf16[3072,768]{1,0:T(8,128)(2,1)} reshape(bf16[18432,128]{1,0:T(8,128)(2,1)} %get-tuple-element.51) | data formatting | bytes 9437184 | tf_op jit(solution)/shard_map/reshape | solution.py:52
  149.8 15.2 %fusion.11 = (bf16[416,3072]{1,0:T(8,128)(2,1)}, f32[416,3072]{1,0:T(8,128)S(1)}) fusion(f32[3072]{0:T(1024)S(1)} %fusion.84, bf16[416,768]{1,0:T(8,128)(2,1)S(1)} %add_convert_fusion.1.n2_ref, bf16[768,3072]{1,0:T(8,128)(2,1)} %reshape.535), kind=kOutput, calls=%fused_computation.18 | convolution fusion | flops 2047279104 | bytes 13037568 | tf_op jit(solution)/shard_map/dot_general | solution.py:396
  165.0 3.6 fusion.17.dpre_ref
  168.6 2.6 multiply_reduce_fusion
  171.2 1.9 fusion.103
  174.7 24.6 %attend_back.1 = (bf16[416,768]{1,0:T(8,128)(2,1)}, bf16[416,768]{1,0:T(8,128)(2,1)}, bf16[416,768]{1,0:T(8,128)(2,1)}, f32[64,128]{1,0:T(8,128)}) custom-call(bf16[416,2304]{1,0:T(8,128)(2,1)} %fusion.28.q_ref.k_ref.v_ref, bf16[416,2304]{1,0:T(8,128)(2,1)} %fusion.28.q_ref.k_ref.v_ref, bf16[416,2304]{1,0:T(8,128)(2,1)} %fusion.28.q_ref.k_ref.v_ref, ...), custom_call_target="tpu_custom_call" | custom-call | tf_op jit(solution)/shard_map/attend_back/pallas_call | solution.py:191
  200.6 6.0 %fusion.99 = (f32[768]{0:T(1024)S(1)}, f32[768]{0:T(1024)S(1)}, f32[416]{0:T(512)S(1)}, f32[416]{0:T(512)S(1)}, f32[416,768]{1,0:T(8,128)}) fusion(f32[416]{0:T(512)S(1)} %rsqrt.22, f32[416]{0:T(512)S(1)} %div.133, bf16[2,196,768]{2,1,0:T(8,128)(2,1)S(1)} %get-tuple-element.87, f32[416,768]{1,0:T(8,128)} %fusion.72, f32[768]{0:T(1024)S(1)} %get-tuple-element.50, ...), kind=kOutput, calls=%fused_computation.252 | convolution fusion | flops 1481463552 | bytes 8631424 | tf_op jit(solution)/shard_map/nf,df->nd/dot_general | solution.py:425
  207.3 3.0 multiply_convert_fusion
  210.3 33.0 %pack_grads.1 = bf16[55808,128]{1,0:T(8,128)(2,1)} custom-call(bf16[416,768]{1,0:T(8,128)(2,1)} %get-tuple-element.63.n1_ref, bf16[416,768]{1,0:T(8,128)(2,1)} %get-tuple-element.18.dq_ref, bf16[416,768]{1,0:T(8,128)(2,1)} %get-tuple-element.19.dk_ref, bf16[416,768]{1,0:T(8,128)(2,1)} %get-tuple-element.20.dv_ref, ...), custom_call_target="tpu_custom_call" | custom-call | tf_op jit(solution)/shard_map/pack_grads/pallas_call | solution.py:328
  243.3 7.0 %fusion.104 = (bf16[2,2,2,2,2,576,128]{6,5,4,3,2,1,0:T(8,128)(2,1)}, bf16[2,2,2,2,2,576,128]{6,5,4,3,2,1,0:T(8,128)(2,1)S(1)}) fusion(bf16[2,2,2,2,2,1744,128]{6,5,4,3,2,1,0:T(8,128)(2,1)} %bitcast.278), kind=kLoop, calls=%fused_computation.255 | loop fusion | bytes 18874368 | tf_op jit(solution)/shard_map/slice | solution.py:515
  250.3 4.1 constant_dynamic-slice_fusion.3
  256.5 1.7 constant_dynamic-slice_fusion.1
  259.8 2.7 slice.136
  262.5 1.7 constant_dynamic-slice_fusion.5
  264.3 1.6 copy.61
  266.4 3.1 fusion.27
  271.3 2.4 fusion.26
  275.0 1.6 collective-permute-start.19
  276.6 2.4 fusion.25
  283.0 15.9 %collective-permute-done.14 = bf16[2,2,2,576,128]{4,3,1,0,2:T(8,128)(2,1)} collective-permute-done((bf16[2,2,2,576,128]{4,3,1,0,2:T(8,128)(2,1)}, bf16[2,2,2,576,128]{4,3,1,0,2:T(8,128)(2,1)}, u32[]{:S(2)}, u32[]{:S(2)}) %collective-permute-start.14) | collective-permute-done | bytes 1179680 | tf_op jit(solution)/shard_map/ppermute | solution.py:452
  298.9 1.9 fusion.31
  300.9 1.6 collective-permute-start.15
  303.5 1.6 fusion.30
  305.2 1.6 collective-permute-start.20
  306.7 4.5 collective-permute-done.9
  313.2 2.5 collective-permute-done.15
  315.9 1.6 collective-permute-start.16
  317.5 6.4 %collective-permute-done.20 = bf16[2,2,576,128]{3,2,0,1:T(8,128)(2,1)S(1)} collective-permute-done((bf16[2,2,576,128]{3,2,0,1:T(8,128)(2,1)S(1)}, bf16[2,2,576,128]{3,2,0,1:T(8,128)(2,1)S(1)}, u32[]{:S(2)}, u32[]{:S(2)}) %collective-permute-start.20) | collective-permute-done | bytes 589856 | tf_op jit(solution)/shard_map/ppermute | solution.py:452
  326.8 2.1 collective-permute-done.16
  329.1 2.7 collective-permute-start.17
  331.8 2.1 collective-permute-start.22
  334.6 3.6 collective-permute-start.12
  338.2 7.3 %collective-permute-done.17 = bf16[576,128]{1,0:T(8,128)(2,1)S(1)} collective-permute-done((bf16[576,128]{1,0:T(8,128)(2,1)S(1)}, bf16[576,128]{1,0:T(8,128)(2,1)S(1)}, u32[]{:S(2)}, u32[]{:S(2)}) %collective-permute-start.17) | collective-permute-done | bytes 147488 | tf_op jit(solution)/shard_map/ppermute | solution.py:452
  345.6 3.1 collective-permute-done.22
  348.7 1.9 collective-permute-done.12
  352.8 5.3 %fusion.71 = bf16[416,768]{1,0:T(8,128)(2,1)S(1)} fusion(f32[416,768]{1,0:T(8,128)S(1)} %get-tuple-element.75, bf16[416,3072]{1,0:T(8,128)(2,1)} %get-tuple-element.76.act_ref, bf16[3072,768]{1,0:T(8,128)(2,1)} %reshape.536, f32[768]{0:T(1024)S(1)} %get-tuple-element.43, f32[416]{0:T(512)S(1)} %mul.382), kind=kOutput, calls=%fused_computation.109 | convolution fusion | flops 1964212224 | bytes 9196160 | tf_op jit(solution)/shard_map/dot_general | solution.py:402
  359.4 58.9 %all-gather.2.cloned.1.call-done = bf16[27904,128]{1,0:T(8,128)(2,1)} async-done(((bf16[1744,128]{1,0:T(8,128)(2,1)}), bf16[27904,128]{1,0:T(8,128)(2,1)}) %all-gather.2.cloned.1.call-update) | async-done | bytes 7143440 | tf_op jit(solution)/shard_map/all_gather | solution.py:578
  418.3 4.1 slice.139
  422.5 9.3 %fusion.62 = (bf16[3464,128]{1,0:T(8,128)(2,1)}, bf16[3464,128]{1,0:T(8,128)(2,1)S(1)}) fusion(f32[8,3464,128]{2,1,0:T(8,128)} %bitcast.292, s32[]{:T(128)S(6)} %select_n.261, f32[8,3464,128]{2,1,0:T(8,128)} %bitcast.277, f32[8,3464,128]{2,1,0:T(8,128)} %bitcast.274, bf16[8,3464,128]{2,1,0:T(8,128)(2,1)S(1)} %bitcast.287, s32[]{:T(128)S(6)} %select_n.257), kind=kLoop, calls=%fused_computation.100 | loop fusion | flops 15962112 | bytes 14188552 | tf_op jit(solution)/shard_map/convert_element_type | solution.py:599
  433.8 16.0 %fusion = (f32[27712,128]{1,0:T(8,128)}, f32[27712,128]{1,0:T(8,128)}) fusion(f32[27712,128]{1,0:T(8,128)} %param.10, bf16[27904,128]{1,0:T(8,128)(2,1)S(1)} %bitcast.291), kind=kLoop, calls=%fused_computation.5 | loop fusion | flops 17735680 | bytes 49659904 | tf_op jit(solution)/shard_map/add | solution.py:531
  450.4 4.0 collective-permute-done.23
  454.5 30.3 %fusion.100 = (bf16[27712,128]{1,0:T(8,128)(2,1)}, f32[27712,128]{1,0:T(8,128)}, f32[27712,128]{1,0:T(8,128)}) fusion(f32[27712,128]{1,0:T(8,128)S(1)} %bitcast.276, bf16[27712,128]{1,0:T(8,128)(2,1)} %copy-done, f32[27712,128]{1,0:T(8,128)} %param.10, f32[27712,128]{1,0:T(8,128)} %param.11), kind=kLoop, calls=%fused_computation.253 | loop fusion | flops 63848448 | bytes 85131264 | tf_op jit(solution)/shard_map/convert_element_type | solution.py:595
  486.9 6.4 %constant_dynamic-update-slice_fusion = bf16[2,8,3464,128]{3,2,1,0:T(8,128)(2,1)} fusion(bf16[2,8,3464,128]{3,2,1,0:T(8,128)(2,1)} %bitcast_dynamic-update-slice_fusion.8, bf16[1,8,3464,128]{3,2,1,0:T(8,128)(2,1)} %bitcast.289, s32[]{:T(128)S(6)} %select_n.256), kind=kLoop, calls=%fused_computation.191 | loop fusion | bytes 14188548 | tf_op jit(solution)/shard_map/dynamic_update_slice | solution.py:479
  493.8 2.1 bitcast_dynamic-update-slice_fusion.7
  495.9 9.3 %collective-permute-done.24 = bf16[3464,128]{1,0:T(8,128)(2,1)S(1)} collective-permute-done((bf16[3464,128]{1,0:T(8,128)(2,1)}, bf16[3464,128]{1,0:T(8,128)(2,1)S(1)}, u32[]{:S(2)}, u32[]{:S(2)}) %collective-permute-start.24) | collective-permute-done | bytes 886816 | tf_op jit(solution)/shard_map/ppermute | solution.py:452
  507.7 2.1 bitcast_dynamic-update-slice_fusion.4
  (194 shorter events, 56.9 us)
Async XLA Ops:
  7.2 411.1 %all-gather.2.cloned.1.call-start = ((), (), s32[]{:S(2)}) async-start(), calls=%async_computation | async-start | bytes 7589888 | tf_op jit(solution)/shard_map/all_gather | solution.py:578
  10.7 30.8 %collective-permute-start = (bf16[3464,128]{1,0:T(8,128)(2,1)}, bf16[3464,128]{1,0:T(8,128)(2,1)S(1)}, u32[]{:S(2)}, u32[]{:S(2)}) collective-permute-start(bf16[3464,128]{1,0:T(8,128)(2,1)} %get-tuple-element.54), channel_id=1, source_target_pairs={{0,1},{1,0},{2,3},{3,2},{4,5},{5,4},{6,7},{7,6},{8,9},{9,8},{10,11... | collective-permute-start | bytes 2660360 | tf_op jit(solution)/shard_map/ppermute | solution.py:452
  13.7 38.9 %collective-permute-start.3 = (bf16[3464,128]{1,0:T(8,128)(2,1)}, bf16[3464,128]{1,0:T(8,128)(2,1)S(1)}, u32[]{:S(2)}, u32[]{:S(2)}) collective-permute-start(bf16[3464,128]{1,0:T(8,128)(2,1)} %get-tuple-element.53), channel_id=1, source_target_pairs={{0,1},{1,0},{2,3},{3,2},{4,5},{5,4},{6,7},{7,6},{8,9},{9,8},{10,11... | collective-permute-start | bytes 2660360 | tf_op jit(solution)/shard_map/ppermute | solution.py:452
  13.7 7.9 %copy-start.14 = (s32[2,1]{0,1:T(1,128)S(1)}, s32[2,1]{0,1:T(1,128)}, u32[]{:S(2)}) copy-start(s32[2,1]{0,1:T(1,128)} %param.8) | copy-start | bytes 28
  41.5 21.1 %collective-permute-start.1 = (bf16[3464,128]{1,0:T(8,128)(2,1)S(1)}, bf16[3464,128]{1,0:T(8,128)(2,1)S(1)}, u32[]{:S(2)}, u32[]{:S(2)}) collective-permute-start(bf16[3464,128]{1,0:T(8,128)(2,1)S(1)} %collective-permute-done), channel_id=1, source_target_pairs={{0,4},{2,6},{4,0},{6,2},{8,12},{10,14},{12,8},{14,10},{16,20},{18,... | collective-permute-start | bytes 2660360 | tf_op jit(solution)/shard_map/ppermute | solution.py:452
  43.5 20.6 %collective-permute-start.2 = (bf16[3464,128]{1,0:T(8,128)(2,1)S(1)}, bf16[3464,128]{1,0:T(8,128)(2,1)S(1)}, u32[]{:S(2)}, u32[]{:S(2)}) collective-permute-start(bf16[3464,128]{1,0:T(8,128)(2,1)S(1)} %collective-permute-done), channel_id=1, source_target_pairs={{0,8},{2,10},{4,12},{6,14},{8,0},{10,2},{12,4},{14,6},{16,24},{18,... | collective-permute-start | bytes 2660360 | tf_op jit(solution)/shard_map/ppermute | solution.py:452
  45.1 21.9 %collective-permute-start.4 = (bf16[3464,128]{1,0:T(8,128)(2,1)S(1)}, bf16[3464,128]{1,0:T(8,128)(2,1)S(1)}, u32[]{:S(2)}, u32[]{:S(2)}) collective-permute-start(bf16[3464,128]{1,0:T(8,128)(2,1)S(1)} %collective-permute-done), channel_id=1, source_target_pairs={{0,2},{2,0},{4,6},{6,4},{8,10},{10,8},{12,14},{14,12},{16,18},{18,... | collective-permute-start | bytes 2660360 | tf_op jit(solution)/shard_map/ppermute | solution.py:452
  52.6 17.4 %collective-permute-start.7 = (bf16[3464,128]{1,0:T(8,128)(2,1)S(1)}, bf16[3464,128]{1,0:T(8,128)(2,1)S(1)}, u32[]{:S(2)}, u32[]{:S(2)}) collective-permute-start(bf16[3464,128]{1,0:T(8,128)(2,1)S(1)} %collective-permute-done.3), channel_id=1, source_target_pairs={{0,2},{2,0},{4,6},{6,4},{8,10},{10,8},{12,14},{14,12},{16,18},{18,... | collective-permute-start | bytes 2660360 | tf_op jit(solution)/shard_map/ppermute | solution.py:452
  62.7 5.3 %collective-permute-start.5 = (bf16[3464,128]{1,0:T(8,128)(2,1)S(1)}, bf16[3464,128]{1,0:T(8,128)(2,1)S(1)}, u32[]{:S(2)}, u32[]{:S(2)}) collective-permute-start(bf16[3464,128]{1,0:T(8,128)(2,1)S(1)} %collective-permute-done.1), channel_id=1, source_target_pairs={{0,2},{2,0},{4,6},{6,4},{8,10},{10,8},{12,14},{14,12},{16,18},{18,... | collective-permute-start | bytes 2660360 | tf_op jit(solution)/shard_map/ppermute | solution.py:452
  64.1 4.9 collective-permute-start.6
  149.4 15.5 %slice-start.6 = ((s8[4718592]{0:T(1024)(128)(4,1)}), s8[4194304]{0:T(1024)(128)(4,1)S(1)}, s32[]{:S(2)}) async-start(s8[4718592]{0:T(1024)(128)(4,1)} %bitcast.294), calls=%async_computation.7 | async-start | bytes 8388608
  149.4 19.1 %slice-start.8 = ((s8[4718592]{0:T(1024)(128)(4,1)}), s8[4194304]{0:T(1024)(128)(4,1)S(1)}, s32[]{:S(2)}) async-start(s8[4718592]{0:T(1024)(128)(4,1)} %bitcast.296), calls=%async_computation.9 | async-start | bytes 8388608
  149.7 15.2 %copy-start.12 = (bf16[416,768]{1,0:T(8,128)(2,1)}, bf16[416,768]{1,0:T(8,128)(2,1)S(1)}, u32[]{:S(2)}) copy-start(bf16[416,768]{1,0:T(8,128)(2,1)S(1)} %add_convert_fusion.1.n2_ref) | copy-start | bytes 1916932
  149.7 15.2 %slice-start.7 = ((s8[4718592]{0:T(1024)(128)(4,1)}), s8[524288]{0:T(1024)(128)(4,1)S(1)}, s32[]{:S(2)}) async-start(s8[4718592]{0:T(1024)(128)(4,1)} %bitcast.294), calls=%async_computation.8 | async-start | bytes 1048576
  149.7 18.8 %slice-start.9 = ((s8[4718592]{0:T(1024)(128)(4,1)}), s8[524288]{0:T(1024)(128)(4,1)S(1)}, s32[]{:S(2)}) async-start(s8[4718592]{0:T(1024)(128)(4,1)} %bitcast.296), calls=%async_computation.10 | async-start | bytes 1048576
  168.6 2.6 copy-start.10
  171.2 1.9 copy-start.9
  173.1 1.6 copy-start.11
  200.6 6.7 %copy-start.8 = (f32[416,768]{1,0:T(8,128)S(1)}, f32[416,768]{1,0:T(8,128)}, u32[]{:S(2)}) copy-start(f32[416,768]{1,0:T(8,128)} %get-tuple-element.38) | copy-start | bytes 3833860
  256.0 10.4 %collective-permute-start.13 = (bf16[2,2,2,2,576,128]{5,4,1,0,2,3:T(8,128)(2,1)}, bf16[2,2,2,2,576,128]{5,4,1,0,2,3:T(8,128)(2,1)}, u32[]{:S(2)}, u32[]{:S(2)}) collective-permute-start(bf16[2,2,2,2,576,128]{5,4,1,0,2,3:T(8,128)(2,1)} %bitcast.270), channel_id=1, source_target_pairs={{0,2},{2,0},{4,6},{6,4},{8,10},{10,8},{12,14},{14,12},{16,18},{18,... | collective-permute-start | bytes 7077896 | tf_op jit(solution)/shard_map/ppermute | solution.py:452
  259.8 11.3 %collective-permute-start.18 = (bf16[2,2,2,2,576,128]{5,4,1,3,0,2:T(8,128)(2,1)}, bf16[2,2,2,2,576,128]{5,4,1,3,0,2:T(8,128)(2,1)}, u32[]{:S(2)}, u32[]{:S(2)}) collective-permute-start(bf16[2,2,2,2,576,128]{5,4,1,3,0,2:T(8,128)(2,1)} %bitcast.269), channel_id=1, source_target_pairs={{0,2},{2,0},{4,6},{6,4},{8,10},{10,8},{12,14},{14,12},{16,18},{18,... | collective-permute-start | bytes 7077896 | tf_op jit(solution)/shard_map/ppermute | solution.py:452
  265.8 10.7 %collective-permute-start.8 = (bf16[2,2,2,2,592,128]{5,4,1,2,3,0:T(8,128)(2,1)}, bf16[2,2,2,2,592,128]{5,4,1,2,3,0:T(8,128)(2,1)}, u32[]{:S(2)}, u32[]{:S(2)}) collective-permute-start(bf16[2,2,2,2,592,128]{5,4,1,2,3,0:T(8,128)(2,1)} %bitcast.268), channel_id=1, source_target_pairs={{0,2},{2,0},{4,6},{6,4},{8,10},{10,8},{12,14},{14,12},{16,18},{18,... | collective-permute-start | bytes 7274504 | tf_op jit(solution)/shard_map/ppermute | solution.py:452
  266.4 4.9 copy-start.4
  269.5 1.8 copy-start.5
  270.7 28.2 %collective-permute-start.14 = (bf16[2,2,2,576,128]{4,3,1,0,2:T(8,128)(2,1)}, bf16[2,2,2,576,128]{4,3,1,0,2:T(8,128)(2,1)}, u32[]{:S(2)}, u32[]{:S(2)}) collective-permute-start(bf16[2,2,2,576,128]{4,3,1,0,2:T(8,128)(2,1)} %dynamic-slice_bitcast_fusion.2), channel_id=1, source_target_pairs={{0,4},{2,6},{4,0},{6,2},{8,12},{10,14},{12,8},{14,10},{16,20},{18,... | collective-permute-start | bytes 3538952 | tf_op jit(solution)/shard_map/ppermute | solution.py:452
  271.3 5.3 %copy-start.1 = (bf16[2,2,2,2,1,592,128]{6,5,4,3,2,1,0:T(8,128)(2,1)S(1)}, bf16[2,2,2,2,1,592,128]{6,5,4,3,2,1,0:T(8,128)(2,1)}, u32[]{:S(2)}) copy-start(bf16[2,2,2,2,1,592,128]{6,5,4,3,2,1,0:T(8,128)(2,1)} %get-tuple-element.57) | copy-start | bytes 7274500
  273.7 2.8 copy-start.6
  275.0 28.5 %collective-permute-start.19 = (bf16[2,2,2,576,128]{4,3,1,2,0:T(8,128)(2,1)}, bf16[2,2,2,576,128]{4,3,1,2,0:T(8,128)(2,1)}, u32[]{:S(2)}, u32[]{:S(2)}) collective-permute-start(bf16[2,2,2,576,128]{4,3,1,2,0:T(8,128)(2,1)} %dynamic-slice_bitcast_fusion.1), channel_id=1, source_target_pairs={{0,8},{2,10},{4,12},{6,14},{8,0},{10,2},{12,4},{14,6},{16,24},{18,... | collective-permute-start | bytes 3538952 | tf_op jit(solution)/shard_map/ppermute | solution.py:452
  278.9 1.4 copy-start.2
  281.5 29.8 %collective-permute-start.9 = (bf16[2,2,2,592,128]{4,3,0,1,2:T(8,128)(2,1)}, bf16[2,2,2,592,128]{4,3,0,1,2:T(8,128)(2,1)S(1)}, u32[]{:S(2)}, u32[]{:S(2)}) collective-permute-start(bf16[2,2,2,592,128]{4,3,0,1,2:T(8,128)(2,1)} %dynamic-slice_bitcast_fusion), channel_id=1, source_target_pairs={{0,1},{1,0},{2,3},{3,2},{4,5},{5,4},{6,7},{7,6},{8,9},{9,8},{10,11... | collective-permute-start | bytes 3637256 | tf_op jit(solution)/shard_map/ppermute | solution.py:452
  283.0 20.5 %copy-start.7 = (bf16[2,2,2,2,576,128]{5,4,1,3,0,2:T(8,128)(2,1)S(1)}, bf16[2,2,2,2,576,128]{5,4,1,3,0,2:T(8,128)(2,1)}, u32[]{:S(2)}) copy-start(bf16[2,2,2,2,576,128]{5,4,1,3,0,2:T(8,128)(2,1)} %copy-done.6) | copy-start | bytes 7077892
  300.8 10.4 %copy-start.3 = (bf16[2,2,2,2,592,128]{5,4,1,2,3,0:T(8,128)(2,1)S(1)}, bf16[2,2,2,2,592,128]{5,4,1,2,3,0:T(8,128)(2,1)}, u32[]{:S(2)}) copy-start(bf16[2,2,2,2,592,128]{5,4,1,2,3,0:T(8,128)(2,1)} %copy-done.2) | copy-start | bytes 7274500
  300.9 14.8 %collective-permute-start.15 = (bf16[2,2,576,128]{3,2,1,0:T(8,128)(2,1)S(1)}, bf16[2,2,576,128]{3,2,1,0:T(8,128)(2,1)S(1)}, u32[]{:S(2)}, u32[]{:S(2)}) collective-permute-start(bf16[2,2,576,128]{3,2,1,0:T(8,128)(2,1)S(1)} %dynamic-slice_bitcast_fusion.5), channel_id=1, source_target_pairs={{0,8},{2,10},{4,12},{6,14},{8,0},{10,2},{12,4},{14,6},{16,24},{18,... | collective-permute-start | bytes 1769480 | tf_op jit(solution)/shard_map/ppermute | solution.py:452
  305.2 18.7 %collective-permute-start.20 = (bf16[2,2,576,128]{3,2,0,1:T(8,128)(2,1)S(1)}, bf16[2,2,576,128]{3,2,0,1:T(8,128)(2,1)S(1)}, u32[]{:S(2)}, u32[]{:S(2)}) collective-permute-start(bf16[2,2,576,128]{3,2,0,1:T(8,128)(2,1)S(1)} %dynamic-slice_bitcast_fusion.4), channel_id=1, source_target_pairs={{0,1},{1,0},{2,3},{3,2},{4,5},{5,4},{6,7},{7,6},{8,9},{9,8},{10,11... | collective-permute-start | bytes 1769480 | tf_op jit(solution)/shard_map/ppermute | solution.py:452
  311.6 14.0 %collective-permute-start.10 = (bf16[2,2,592,128]{3,2,0,1:T(8,128)(2,1)S(1)}, bf16[2,2,592,128]{3,2,0,1:T(8,128)(2,1)S(1)}, u32[]{:S(2)}, u32[]{:S(2)}) collective-permute-start(bf16[2,2,592,128]{3,2,0,1:T(8,128)(2,1)S(1)} %dynamic-slice_bitcast_fusion.3), channel_id=1, source_target_pairs={{0,4},{2,6},{4,0},{6,2},{8,12},{10,14},{12,8},{14,10},{16,20},{18,... | collective-permute-start | bytes 1818632 | tf_op jit(solution)/shard_map/ppermute | solution.py:452
  315.9 13.0 %collective-permute-start.16 = (bf16[2,576,128]{2,1,0:T(8,128)(2,1)S(1)}, bf16[2,576,128]{2,1,0:T(8,128)(2,1)S(1)}, u32[]{:S(2)}, u32[]{:S(2)}) collective-permute-start(bf16[2,576,128]{2,1,0:T(8,128)(2,1)S(1)} %dynamic-slice_bitcast_fusion.8), channel_id=1, source_target_pairs={{0,1},{1,0},{2,3},{3,2},{4,5},{5,4},{6,7},{7,6},{8,9},{9,8},{10,11... | collective-permute-start | bytes 884744 | tf_op jit(solution)/shard_map/ppermute | solution.py:452
  324.1 7.7 %collective-permute-start.21 = (bf16[2,576,128]{2,1,0:T(8,128)(2,1)S(1)}, bf16[2,576,128]{2,1,0:T(8,128)(2,1)S(1)}, u32[]{:S(2)}, u32[]{:S(2)}) collective-permute-start(bf16[2,576,128]{2,1,0:T(8,128)(2,1)S(1)} %dynamic-slice_bitcast_fusion.7), channel_id=1, source_target_pairs={{0,4},{2,6},{4,0},{6,2},{8,12},{10,14},{12,8},{14,10},{16,20},{18,... | collective-permute-start | bytes 884744 | tf_op jit(solution)/shard_map/ppermute | solution.py:452
  325.8 25.7 %copy-start.13 = (bf16[416,768]{1,0:T(8,128)(2,1)S(1)}, bf16[416,768]{1,0:T(8,128)(2,1)}, u32[]{:S(2)}) copy-start(bf16[416,768]{1,0:T(8,128)(2,1)} %get-tuple-element.64) | copy-start | bytes 1916932
  325.8 8.6 %collective-permute-start.11 = (bf16[2,592,128]{2,1,0:T(8,128)(2,1)S(1)}, bf16[2,592,128]{2,1,0:T(8,128)(2,1)S(1)}, u32[]{:S(2)}, u32[]{:S(2)}) collective-permute-start(bf16[2,592,128]{2,1,0:T(8,128)(2,1)S(1)} %dynamic-slice_bitcast_fusion.6), channel_id=1, source_target_pairs={{0,8},{2,10},{4,12},{6,14},{8,0},{10,2},{12,4},{14,6},{16,24},{18,... | collective-permute-start | bytes 909320 | tf_op jit(solution)/shard_map/ppermute | solution.py:452
  329.1 16.5 %collective-permute-start.17 = (bf16[576,128]{1,0:T(8,128)(2,1)S(1)}, bf16[576,128]{1,0:T(8,128)(2,1)S(1)}, u32[]{:S(2)}, u32[]{:S(2)}) collective-permute-start(bf16[576,128]{1,0:T(8,128)(2,1)S(1)} %dynamic-slice_bitcast_fusion.11), channel_id=1, source_target_pairs={{0,16},{2,18},{4,20},{6,22},{8,24},{10,26},{12,28},{14,30},{16,0},... | collective-permute-start | bytes 442376 | tf_op jit(solution)/shard_map/ppermute | solution.py:452
  331.8 16.9 %collective-permute-start.22 = (bf16[576,128]{1,0:T(8,128)(2,1)S(1)}, bf16[576,128]{1,0:T(8,128)(2,1)S(1)}, u32[]{:S(2)}, u32[]{:S(2)}) collective-permute-start(bf16[576,128]{1,0:T(8,128)(2,1)S(1)} %dynamic-slice_bitcast_fusion.10), channel_id=1, source_target_pairs={{0,16},{2,18},{4,20},{6,22},{8,24},{10,26},{12,28},{14,30},{16,0},... | collective-permute-start | bytes 442376 | tf_op jit(solution)/shard_map/ppermute | solution.py:452
  334.6 16.0 %collective-permute-start.12 = (bf16[592,128]{1,0:T(8,128)(2,1)S(1)}, bf16[592,128]{1,0:T(8,128)(2,1)S(1)}, u32[]{:S(2)}, u32[]{:S(2)}) collective-permute-start(bf16[592,128]{1,0:T(8,128)(2,1)S(1)} %dynamic-slice_bitcast_fusion.9), channel_id=1, source_target_pairs={{0,16},{2,18},{4,20},{6,22},{8,24},{10,26},{12,28},{14,30},{16,0},... | collective-permute-start | bytes 454664 | tf_op jit(solution)/shard_map/ppermute | solution.py:452
  418.3 15.5 %slice-start.4 = ((s8[7143424]{0:T(1024)(128)(4,1)}), s8[4194304]{0:T(1024)(128)(4,1)S(1)}, s32[]{:S(2)}) async-start(s8[7143424]{0:T(1024)(128)(4,1)} %bitcast.290), calls=%async_computation.5 | async-start | bytes 8388608
  422.4 9.3 %copy-start = (bf16[27712,128]{1,0:T(8,128)(2,1)}, bf16[27712,128]{1,0:T(8,128)(2,1)S(1)}, u32[]{:S(2)}) copy-start(bf16[27712,128]{1,0:T(8,128)(2,1)S(1)} %slice.139) | copy-start | bytes 21282820
  422.4 11.4 %slice-start.5 = ((s8[7143424]{0:T(1024)(128)(4,1)}), s8[2949120]{0:T(1024)(128)(4,1)S(1)}, s32[]{:S(2)}) async-start(s8[7143424]{0:T(1024)(128)(4,1)} %bitcast.290), calls=%async_computation.6 | async-start | bytes 5898240
  422.4 32.0 %slice-start = ((s8[14188544]{0:T(1024)(128)(4,1)}), s8[4194304]{0:T(1024)(128)(4,1)S(1)}, s32[]{:S(2)}) async-start(s8[14188544]{0:T(1024)(128)(4,1)} %bitcast.275), calls=%async_computation.1 | async-start | bytes 8388608
  431.8 22.7 %collective-permute-start.23 = (bf16[3464,128]{1,0:T(8,128)(2,1)S(1)}, bf16[3464,128]{1,0:T(8,128)(2,1)}, u32[]{:S(2)}, u32[]{:S(2)}) collective-permute-start(bf16[3464,128]{1,0:T(8,128)(2,1)S(1)} %get-tuple-element.40), channel_id=1, source_target_pairs={{0,1},{1,0},{2,3},{3,2},{4,5},{5,4},{6,7},{7,6},{8,9},{9,8},{10,11... | collective-permute-start | bytes 2660360 | tf_op jit(solution)/shard_map/ppermute | solution.py:452
  433.2 21.2 %slice-start.1 = ((s8[14188544]{0:T(1024)(128)(4,1)}), s8[4194304]{0:T(1024)(128)(4,1)S(1)}, s32[]{:S(2)}) async-start(s8[14188544]{0:T(1024)(128)(4,1)} %bitcast.275), calls=%async_computation.2 | async-start | bytes 8388608
  433.2 21.2 %slice-start.2 = ((s8[14188544]{0:T(1024)(128)(4,1)}), s8[4194304]{0:T(1024)(128)(4,1)S(1)}, s32[]{:S(2)}) async-start(s8[14188544]{0:T(1024)(128)(4,1)} %bitcast.275), calls=%async_computation.3 | async-start | bytes 8388608
  433.2 21.2 %slice-start.3 = ((s8[14188544]{0:T(1024)(128)(4,1)}), s8[1605632]{0:T(1024)(128)(4,1)S(1)}, s32[]{:S(2)}) async-start(s8[14188544]{0:T(1024)(128)(4,1)} %bitcast.275), calls=%async_computation.4 | async-start | bytes 3211264
  433.2 60.1 %collective-permute-start.26 = (bf16[3464,128]{1,0:T(8,128)(2,1)}, bf16[3464,128]{1,0:T(8,128)(2,1)}, u32[]{:S(2)}, u32[]{:S(2)}) collective-permute-start(bf16[3464,128]{1,0:T(8,128)(2,1)} %get-tuple-element.39), channel_id=1, source_target_pairs={{0,1},{1,0},{2,3},{3,2},{4,5},{5,4},{6,7},{7,6},{8,9},{9,8},{10,11... | collective-permute-start | bytes 2660360 | tf_op jit(solution)/shard_map/ppermute | solution.py:452
  484.8 20.4 %collective-permute-start.24 = (bf16[3464,128]{1,0:T(8,128)(2,1)}, bf16[3464,128]{1,0:T(8,128)(2,1)S(1)}, u32[]{:S(2)}, u32[]{:S(2)}) collective-permute-start(bf16[3464,128]{1,0:T(8,128)(2,1)} %collective-permute-done.23), channel_id=1, source_target_pairs={{0,4},{2,6},{4,0},{6,2},{8,12},{10,14},{12,8},{14,10},{16,20},{18,... | collective-permute-start | bytes 2660360 | tf_op jit(solution)/shard_map/ppermute | solution.py:452
  485.3 20.9 %collective-permute-start.25 = (bf16[3464,128]{1,0:T(8,128)(2,1)}, bf16[3464,128]{1,0:T(8,128)(2,1)S(1)}, u32[]{:S(2)}, u32[]{:S(2)}) collective-permute-start(bf16[3464,128]{1,0:T(8,128)(2,1)} %collective-permute-done.23), channel_id=1, source_target_pairs={{0,8},{2,10},{4,12},{6,14},{8,0},{10,2},{12,4},{14,6},{16,24},{18,... | collective-permute-start | bytes 2660360 | tf_op jit(solution)/shard_map/ppermute | solution.py:452
  486.9 23.0 %collective-permute-start.27 = (bf16[3464,128]{1,0:T(8,128)(2,1)}, bf16[3464,128]{1,0:T(8,128)(2,1)S(1)}, u32[]{:S(2)}, u32[]{:S(2)}) collective-permute-start(bf16[3464,128]{1,0:T(8,128)(2,1)} %collective-permute-done.23), channel_id=1, source_target_pairs={{0,2},{2,0},{4,6},{6,4},{8,10},{10,8},{12,14},{14,12},{16,18},{18,... | collective-permute-start | bytes 2660360 | tf_op jit(solution)/shard_map/ppermute | solution.py:452
  493.3 19.4 %collective-permute-start.30 = (bf16[3464,128]{1,0:T(8,128)(2,1)}, bf16[3464,128]{1,0:T(8,128)(2,1)S(1)}, u32[]{:S(2)}, u32[]{:S(2)}) collective-permute-start(bf16[3464,128]{1,0:T(8,128)(2,1)} %collective-permute-done.26), channel_id=1, source_target_pairs={{0,2},{2,0},{4,6},{6,4},{8,10},{10,8},{12,14},{14,12},{16,18},{18,... | collective-permute-start | bytes 2660360 | tf_op jit(solution)/shard_map/ppermute | solution.py:452
  505.2 5.6 %collective-permute-start.28 = (bf16[3464,128]{1,0:T(8,128)(2,1)S(1)}, bf16[3464,128]{1,0:T(8,128)(2,1)S(1)}, u32[]{:S(2)}, u32[]{:S(2)}) collective-permute-start(bf16[3464,128]{1,0:T(8,128)(2,1)S(1)} %collective-permute-done.24), channel_id=1, source_target_pairs={{0,2},{2,0},{4,6},{6,4},{8,10},{10,8},{12,14},{14,12},{16,18},{18,... | collective-permute-start | bytes 2660360 | tf_op jit(solution)/shard_map/ppermute | solution.py:452
  506.2 5.6 %collective-permute-start.29 = (bf16[3464,128]{1,0:T(8,128)(2,1)S(1)}, bf16[3464,128]{1,0:T(8,128)(2,1)S(1)}, u32[]{:S(2)}, u32[]{:S(2)}) collective-permute-start(bf16[3464,128]{1,0:T(8,128)(2,1)S(1)} %collective-permute-done.25), channel_id=1, source_target_pairs={{0,2},{2,0},{4,6},{6,4},{8,10},{10,8},{12,14},{14,12},{16,18},{18,... | collective-permute-start | bytes 2660360 | tf_op jit(solution)/shard_map/ppermute | solution.py:452
Sparse Core Ops, SparseCore 0:
  351.6 66.6 all-gather.1

commit v5 on v3

--- a/solution.py
+++ b/solution.py
@@ -211,11 +211,19 @@
     return lax.dot_general(left, right, (((0,), (0,)), ((), ())), preferred_element_type=jnp.float32)
 
 
+ORDERS = (("y", "x", "near"), ("x", "near", "y"), ("near", "y", "x"))
+
+
+def halves(wide_size, group_size):
+    return (wide_size, group_size) == (16, 2)
+
+
 def pack_kernel(
     n1_ref, dq_ref, dk_ref, dv_ref, att_ref, dproj_ref, n2_ref, dpre_ref, act_ref, dout_ref, tail_ref,
-    out_ref, rows_ref, stage_ref, bias_ref, stage_sems, bias_sems,
-    *, part_rows, share_rows, group_size,
+    *refs, part_rows, share_rows, group_size, wide_size, cuts, relative,
 ):
+    *out_refs, rows_ref, stage_ref, bias_ref, stage_sems = refs
+    kept_refs, sent_refs = out_refs[: len(cuts)], out_refs[len(cuts) :]
     count = n1_ref.shape[0]
     ones = jnp.ones((16, count), jnp.bfloat16)
 
@@ -243,24 +251,62 @@
             rows_ref[base + j : base + j + 1, :] = total[0:1, j * 128 : (j + 1) * 128]
         return base + ref.shape[1] // 128
 
-    limit = stage_ref.shape[1]
+    share = share_rows // wide_size
+    own_wide = lax.axis_index("wide")
+    own_group = lax.axis_index("grp")
     chunks = []
     for owner in range(group_size):
-        low = 0
-        while low < part_rows:
-            size = min(limit, part_rows - low)
-            chunks.append((owner * part_rows + low, owner * share_rows + low, size))
-            low += size
+        for place in range(wide_size):
+            low = place * share
+            size = max(0, min(share, part_rows - low))
+            chunks.append((owner, place, owner * part_rows + low, size))
     flying = {}
     sent = 0
+    bias_known = False
+
+    def pieces(slot, owner, place):
+        if not relative:
+            return [(stage_ref.at[slot], kept_refs[0].at[owner, place], None)]
+        flips = place ^ own_wide
+        flip = {
+            "y": owner ^ own_group,
+            "x": (flips >> 1) & 1,
+            "near": (flips >> 2) & 1,
+            "far": (flips >> 3) & 1,
+        }
+        found = []
+        for (low, high), order, kept_ref, sent_ref in zip(cuts, ORDERS, kept_refs, sent_refs):
+            spot = tuple(flip[name] for name in order + ("far",))
+            source = stage_ref.at[slot, pl.ds(low, high - low), :]
+            found.append((source, kept_ref.at[spot], sent_ref.at[spot]))
+        return found
+
+    def launch(slot, owner, place):
+        for source, kept, other in pieces(slot, owner, place):
+
+            def start(target, source=source):
+                pltpu.make_async_copy(source, target, stage_sems.at[slot]).start()
+
+            if other is None:
+                start(kept)
+            else:
+                other_core = ((place ^ own_wide) & 1) == 1
+                pl.when(other_core)(functools.partial(start, other))
+                pl.when(jnp.logical_not(other_core))(functools.partial(start, kept))
+
+    def finish(slot):
+        if slot in flying:
+            for source, kept, _ in pieces(slot, *flying.pop(slot)):
+                pltpu.make_async_copy(source, kept, stage_sems.at[slot]).wait()
 
     def emit(upto):
         nonlocal sent
-        while sent < len(chunks) and chunks[sent][0] + chunks[sent][2] <= upto:
-            source, target, size = chunks[sent]
+        while sent < len(chunks) and chunks[sent][2] + chunks[sent][3] <= upto:
+            if chunks[sent][3] < share and not bias_known:
+                break
+            owner, place, source, size = chunks[sent]
             slot = sent % 2
-            if slot in flying:
-                flying.pop(slot).wait()
+            finish(slot)
             step = next(s for s in (128, 64, 32, 16) if size % s == 0)
 
             def convert(i, carry, source=source, slot=slot, step=step):
@@ -271,13 +317,12 @@
                 return carry
 
             lax.fori_loop(0, size // step, convert, 0)
-            copy = pltpu.make_async_copy(
-                stage_ref.at[slot, pl.ds(0, size), :],
-                out_ref.at[pl.ds(target, size), :],
-                stage_sems.at[slot],
-            )
-            copy.start()
-            flying[slot] = copy
+            if size < share:
+                bias_place = part_rows - place * share
+                first = max(0, -bias_place)
+                stage_ref[slot, size:share, :] = bias_ref[first : first + share - size, :]
+            launch(slot, owner, place)
+            flying[slot] = (owner, place)
             sent += 1
 
     row = weight(0, n1_ref, [dq_ref, dk_ref, dv_ref])
@@ -287,7 +332,6 @@
     row = weight(row, att_ref, [dproj_ref])
     proj_bias = row
     row = bias(row, dproj_ref)
-    emit(row)
     bias_size = dproj_ref.shape[1] // 128
     spare = share_rows - part_rows
     bias_ref[...] = jnp.concatenate(
@@ -297,14 +341,8 @@
         ],
         0,
     ).astype(jnp.bfloat16)
-    bias_copies = [
-        pltpu.make_async_copy(
-            bias_ref, out_ref.at[pl.ds(owner * share_rows + part_rows, spare), :], bias_sems.at[owner]
-        )
-        for owner in range(group_size)
-    ]
-    for copy in bias_copies:
-        copy.start()
+    bias_known = True
+    emit(row)
     row = weight(row, n2_ref, [dpre_ref])
     row = bias(row, dpre_ref)
     emit(row)
@@ -313,10 +351,8 @@
     emit(row)
     rows_ref[row : row + tail_ref.shape[0], :] = tail_ref[...]
     emit(group_size * part_rows)
-    for slot in list(flying):
-        flying.pop(slot).wait()
-    for copy in bias_copies:
-        copy.wait()
+    for slot in range(2):
+        finish(slot)
 
 
 def pack_shares(factors, tail, part_rows, group_size, wide_size):
@@ -324,25 +360,39 @@
     grain = 16 * wide_size
     share_rows = -(-(part_rows + feature // 128) // grain) * grain
     spare = share_rows - part_rows
+    share = share_rows // wide_size
+    relative = halves(wide_size, group_size)
     whole = pl.BlockSpec(memory_space=pltpu.VMEM)
-    packed = pl.pallas_call(
+    if relative:
+        units = share // 16
+        ends = [0, (units + 2) // 3 * 16, ((units + 2) // 3 + (units + 1) // 3) * 16, share]
+        cuts = tuple(zip(ends, ends[1:]))
+        shapes = [(2, 2, 2, 2, high - low, 128) for low, high in cuts] * 2
+    else:
+        cuts = ((0, share),)
+        shapes = [(group_size, wide_size, share, 128)]
+    return pl.pallas_call(
         functools.partial(
-            pack_kernel, part_rows=part_rows, share_rows=share_rows, group_size=group_size
+            pack_kernel,
+            part_rows=part_rows,
+            share_rows=share_rows,
+            group_size=group_size,
+            wide_size=wide_size,
+            cuts=cuts,
+            relative=relative,
         ),
         in_specs=[whole] * (len(factors) + 1),
-        out_specs=pl.BlockSpec(memory_space=pl.ANY),
-        out_shape=jax.ShapeDtypeStruct((group_size * share_rows, 128), jnp.bfloat16),
+        out_specs=[pl.BlockSpec(memory_space=pl.ANY)] * len(shapes),
+        out_shape=[jax.ShapeDtypeStruct(shape, jnp.bfloat16) for shape in shapes],
         scratch_shapes=[
             pltpu.VMEM((group_size * part_rows, 128), jnp.float32),
-            pltpu.VMEM((2, 2048, 128), jnp.bfloat16),
+            pltpu.VMEM((2, share, 128), jnp.bfloat16),
             pltpu.VMEM((spare, 128), jnp.bfloat16),
             pltpu.SemaphoreType.DMA((2,)),
-            pltpu.SemaphoreType.DMA((group_size,)),
         ],
         compiler_params=pltpu.CompilerParams(vmem_limit_bytes=60 * 1024 * 1024),
         name="pack_grads",
     )(*factors, tail)
-    return packed, share_rows
 
 
 def gelu_slope(pre_act):
@@ -468,6 +518,7 @@
 def gather_groups(mine, diagonal, finish, base):
     core, cross, deep = wide_bits(3)
     first = swap(mine, "grp", 1)
+    diagonal, first = lax.optimization_barrier((diagonal, first))
     last = swap(diagonal, "grp", 1)
     side = swap(first, "wide", 2)
     back = swap(first, "wide", 4)
@@ -482,6 +533,31 @@
             at = eighth_index(which, cross ^ flip_cross, deep ^ flip_deep)
             out = lax.dynamic_update_slice(out, part[None, None], (1 - group, at, 0, 0))
     return out.reshape(2 * own.shape[0], 128)
+
+
+def joined(kept, sent):
+    return (kept.astype(jnp.float32) + sent.astype(jnp.float32)).astype(kept.dtype)
+
+
+def reduce_shares(packed):
+    if len(packed) == 1:
+        rows = packed[0].reshape(-1, 128)
+        return lax.psum_scatter(rows, ("grp", "wide"), scatter_dimension=0, tiled=True)
+    moves = {
+        "x": lambda v: swap(v, "wide", 2),
+        "near": lambda v: swap(v, "wide", 4),
+        "far": lambda v: swap(v, "wide", 8),
+        "y": lambda v: swap(v, "grp", 1),
+    }
+    done = []
+    for kept, sent, order in zip(packed[:3], packed[3:], ORDERS):
+        arrived = swap(sent, "wide", 1)
+        for name in order + ("far",):
+            leaving = joined(kept[1], arrived[1])
+            kept = joined(kept[0], arrived[0])
+            arrived = moves[name](leaving)
+        done.append(joined(kept, arrived))
+    return jnp.concatenate(done, 0)
 
 
 def own_eighths(rows):
@@ -537,8 +613,8 @@
     tail = jnp.concatenate([member.reshape(-1) for member in tail])
     tail_rows = part_rows * group_size - filled
     tail = jnp.pad(tail, (0, tail_rows * 128 - tail.shape[0])).reshape(tail_rows, 128)
-    packed, share_rows = pack_shares(factors, tail, part_rows, group_size, wide_size)
-    owned = lax.psum_scatter(packed, ("grp", "wide"), scatter_dimension=0, tiled=True)
+    packed = pack_shares(factors, tail, part_rows, group_size, wide_size)
+    owned = reduce_shares(packed)
     totals = lax.all_gather(owned, "wide", axis=0, tiled=True)
     factor = 1.0 / (micro_count * wide_size * group_size)
     bias_total = totals[part_rows : part_rows + feature // 128]

time: 588 us -> 526 us (0.89)
  waiting for transfers between devices: 254 us -> 155 us
  starting transfers between devices: 11.8 us -> 28.2 us
  Pallas kernels: 83 us -> 95.2 us
  other arithmetic: 76.6 us -> 84.4 us
    reduce_scatter x1 -> x0, waiting for transfers between devices: 162 us -> none  [body(): lax.psum_scatter(packed, ('grp', 'wide'), scatter_dimension=0, tiled=True)]
    ppermute x16 -> x31, waiting for transfers between devices: 31.3 us -> 97.9 us  [swap(): lax.ppermute(values, axis, [(i, i ^ bit) for i in range(lax.axis_size(axi...]
    ppermute x16 -> x31, starting transfers between devices: 11.7 us -> 28.1 us  [swap(): lax.ppermute(values, axis, [(i, i ^ bit) for i in range(lax.axis_size(axi...]
    pallas_call x1, Pallas kernels: 32.9 us -> 45.3 us  [pack_shares(): pl.pallas_call(functools.partial(pack_kernel, part_rows=part_rows, share_...]
  transfers between devices with their start and end apart: 18 -> 32, of which waited for: 7 -> 20; matrix products, arithmetic and copies ran while one was open for 18% -> 22% of each run, Pallas kernels for 0% -> 0%
where the time goes in v5:
time: 526 us; the launch traced here: 516 us
  waiting for transfers between devices  155 us (29%)
  local copies, waits for them, and re-layouts  96.3 us (18%)
  Pallas kernels  95.2 us (18%)
  other arithmetic  84.4 us (16%)
  matrix products  41.7 us (8%)
  starting transfers between devices  28.2 us (5%)
  between operations  15 us (3%)
    ppermute x31, waiting for transfers between devices, swap(): lax.ppermute(values, axis, [(i, i ^ bit) for i in range(lax.axis_size(axi...  97.9 us
    all_gather x1, waiting for transfers between devices, body(): totals = lax.all_gather(owned, 'wide', axis=0, tiled=True)  57 us
    pallas_call x1, Pallas kernels, pack_shares(): pl.pallas_call(functools.partial(pack_kernel, part_rows=part_rows, share_...  45.3 us
    convert_element_type x1, other arithmetic, finish(): return later[0].astype(jnp.bfloat16)  30.6 us
    ppermute x31, starting transfers between devices, swap(): lax.ppermute(values, axis, [(i, i ^ bit) for i in range(lax.axis_size(axi...  28.1 us
    reshape x4, local copies, waits for them, and re-layouts, unpack(): members.append(rows[row:row + length].reshape(dims_of))  27.1 us
    pallas_call x1, Pallas kernels, attend(): pl.pallas_call(attend_kernel, grid=(wins, pairs), in_specs=[column(0), co...  25.3 us
    pallas_call x1, Pallas kernels, attend_back(): pl.pallas_call(attend_back_kernel, grid=(wins, pairs), in_specs=[column(0...  24.6 us
  transfers between devices with their start and end apart: 32, of which 20 were waited for; matrix products, arithmetic and copies ran while one was open for 22% of the time, Pallas kernels for 0%

profile of v5, /device:TPU:0, one launch (start us, length us, event | category | flops | bytes accessed | tf_op | source)
XLA Modules:
  0.0 515.7 jit_solution(10323146672804094764)
XLA Ops:
  7.2 3.2 bitcast_convert_fusion
  10.4 3.0 collective-permute-start
  13.4 7.9 %convert_element_type.597 = bf16[27712,128]{1,0:T(8,128)(2,1)} convert(f32[27712,128]{1,0:T(8,128)} %param.9) | non-fusion elementwise | flops 3547136 | bytes 21282816 | tf_op jit(solution)/shard_map/convert_element_type | solution.py:596
  21.4 1.4 copy_bitcast_fusion
  24.7 1.3 fusion.66
  27.6 7.1 %reshape.652 = bf16[2,8,3464,128]{3,2,1,0:T(8,128)(2,1)} broadcast(bf16[]{:T(256)} %constant.104.clone.1), dimensions={} | broadcast | bytes 14188546 | tf_op jit(solution)/shard_map/reshape | solution.py:529
  34.8 6.4 %constant_dynamic-update-slice_fusion.1 = bf16[2,8,3464,128]{3,2,1,0:T(8,128)(2,1)} fusion(bf16[2,8,3464,128]{3,2,1,0:T(8,128)(2,1)} %reshape.652, bf16[1,8,3464,128]{3,2,1,0:T(8,128)(2,1)} %bitcast.330, s32[]{:T(128)S(6)} %select_n.197), kind=kLoop, calls=%fused_computation.225 | loop fusion | bytes 14188548 | tf_op jit(solution)/shard_map/dynamic_update_slice | solution.py:530
  41.2 1.5 collective-permute-start.1
  42.7 1.6 collective-permute-start.2
  45.8 16.6 %collective-permute-done.1 = bf16[3464,128]{1,0:T(8,128)(2,1)S(1)} collective-permute-done((bf16[3464,128]{1,0:T(8,128)(2,1)S(1)}, bf16[3464,128]{1,0:T(8,128)(2,1)S(1)}, u32[]{:S(2)}, u32[]{:S(2)}) %collective-permute-start.1) | collective-permute-done | bytes 886816 | tf_op jit(solution)/shard_map/ppermute | solution.py:502
  62.4 1.2 collective-permute-done.2
  63.6 2.8 collective-permute-done.3
  74.7 3.4 slice.318
  78.1 1.6 slice.324
  79.7 9.3 %fusion.125 = (bf16[18432,128]{1,0:T(8,128)(2,1)}, bf16[18432,128]{1,0:T(8,128)(2,1)}) fusion(bf16[55424,128]{1,0:T(8,128)(2,1)} %bitcast.326), kind=kLoop, calls=%fused_computation.282 | loop fusion | bytes 18874368 | tf_op jit(solution)/shard_map/slice | solution.py:52
  90.2 7.6 %reshape.656 = bf16[768,2304]{1,0:T(8,128)(2,1)} reshape(bf16[13824,128]{1,0:T(8,128)(2,1)} %slice.318) | data formatting | bytes 7077888 | tf_op jit(solution)/shard_map/reshape | solution.py:52
  97.8 1.9 reshape.657
  100.9 5.0 fusion.25.q_ref.k_ref.v_ref
  105.9 25.3 %attend.1 = (bf16[2,12,208,208]{3,2,1,0:T(8,128)(2,1)}, bf16[416,768]{1,0:T(8,128)(2,1)}) custom-call(bf16[416,2304]{1,0:T(8,128)(2,1)} %fusion.25.q_ref.k_ref.v_ref, bf16[416,2304]{1,0:T(8,128)(2,1)} %fusion.25.q_ref.k_ref.v_ref, bf16[416,2304]{1,0:T(8,128)(2,1)} %fusion.25.q_ref.k_ref.v_ref, bf16[64,128]{1,0:T(8,128)(2,1)} %pad_maximum_fusion.1.table_ref, ...), custom_call_target="tpu_custom_call" | custom-call | tf_op jit(solution)/shard_map/attend/pallas_call | solution.py:169
  131.2 2.7 fusion.127
  134.1 8.4 %reshape.658 = bf16[768,3072]{1,0:T(8,128)(2,1)} reshape(bf16[18432,128]{1,0:T(8,128)(2,1)} %get-tuple-element.70) | data formatting | bytes 9437184 | tf_op jit(solution)/shard_map/reshape | solution.py:52
  142.5 9.2 %reshape.659 = bf16[3072,768]{1,0:T(8,128)(2,1)} reshape(bf16[18432,128]{1,0:T(8,128)(2,1)} %get-tuple-element.69) | data formatting | bytes 9437184 | tf_op jit(solution)/shard_map/reshape | solution.py:52
  152.1 15.1 %fusion.11 = (bf16[416,3072]{1,0:T(8,128)(2,1)}, f32[416,3072]{1,0:T(8,128)S(1)}) fusion(f32[3072]{0:T(1024)S(1)} %fusion.105, bf16[416,768]{1,0:T(8,128)(2,1)S(1)} %add_convert_fusion.7.n2_ref, bf16[768,3072]{1,0:T(8,128)(2,1)} %reshape.658), kind=kOutput, calls=%fused_computation.18 | convolution fusion | flops 2047279104 | bytes 13037568 | tf_op jit(solution)/shard_map/dot_general | solution.py:446
  167.2 3.6 fusion.17.dpre_ref
  170.8 2.6 multiply_reduce_fusion
  173.5 1.9 fusion.124
  175.3 1.6 convolution_convert_fusion.grad_ref
  176.9 24.6 %attend_back.1 = (bf16[416,768]{1,0:T(8,128)(2,1)}, bf16[416,768]{1,0:T(8,128)(2,1)}, bf16[416,768]{1,0:T(8,128)(2,1)}, f32[64,128]{1,0:T(8,128)}) custom-call(bf16[416,2304]{1,0:T(8,128)(2,1)} %fusion.25.q_ref.k_ref.v_ref, bf16[416,2304]{1,0:T(8,128)(2,1)} %fusion.25.q_ref.k_ref.v_ref, bf16[416,2304]{1,0:T(8,128)(2,1)} %fusion.25.q_ref.k_ref.v_ref, ...), custom_call_target="tpu_custom_call" | custom-call | tf_op jit(solution)/shard_map/attend_back/pallas_call | solution.py:191
  202.9 6.0 %fusion.120 = (f32[768]{0:T(1024)S(1)}, f32[768]{0:T(1024)S(1)}, f32[416]{0:T(512)S(1)}, f32[416]{0:T(512)S(1)}, f32[416,768]{1,0:T(8,128)}) fusion(f32[416]{0:T(512)S(1)} %rsqrt.22, f32[416]{0:T(512)S(1)} %div.133, bf16[2,196,768]{2,1,0:T(8,128)(2,1)S(1)} %get-tuple-element.117, f32[416,768]{1,0:T(8,128)} %fusion.66, f32[768]{0:T(1024)S(1)} %get-tuple-element.68, ...), kind=kOutput, calls=%fused_computation.279 | convolution fusion | flops 1481463552 | bytes 8631424 | tf_op jit(solution)/shard_map/nf,df->nd/dot_general | solution.py:475
  209.6 3.0 multiply_convert_fusion
  212.5 45.3 %pack_grads.1 = (bf16[2,2,2,2,592,128]{5,4,3,2,1,0:T(8,128)(2,1)}, bf16[2,2,2,2,576,128]{5,4,3,2,1,0:T(8,128)(2,1)}, bf16[2,2,2,2,576,128]{5,4,3,2,1,0:T(8,128)(...) custom-call(bf16[416,768]{1,0:T(8,128)(2,1)} %get-tuple-element.93.n, ...), custom_call_target="tpu_custom_call" | custom-call | tf_op jit(solution)/shard_map/pack_grads/pallas_call | solution.py:374
  258.9 3.9 collective-permute-done.13
  262.7 2.4 add_convert_fusion.5
  267.3 2.3 collective-permute-done.8
  270.8 22.6 %collective-permute-done.14 = bf16[2,2,2,576,128]{4,3,2,1,0:T(8,128)(2,1)S(1)} collective-permute-done((bf16[2,2,2,576,128]{4,3,2,1,0:T(8,128)(2,1)S(1)}, bf16[2,2,2,576,128]{4,3,2,1,0:T(8,128)(2,1)S(1)}, u32[]{:S(2)}, u32[]{:S(2)}) %collective-permute-start.14) | collective-permute-done | bytes 1179680 | tf_op jit(solution)/shard_map/ppermute | solution.py:502
  295.9 3.8 collective-permute-done.9
  300.7 7.8 %collective-permute-done.15 = bf16[2,2,576,128]{3,2,1,0:T(8,128)(2,1)S(1)} collective-permute-done((bf16[2,2,576,128]{3,2,1,0:T(8,128)(2,1)S(1)}, bf16[2,2,576,128]{3,2,1,0:T(8,128)(2,1)S(1)}, u32[]{:S(2)}, u32[]{:S(2)}) %collective-permute-start.15) | collective-permute-done | bytes 589856 | tf_op jit(solution)/shard_map/ppermute | solution.py:502
  309.3 3.1 collective-permute-done.20
  313.2 2.0 collective-permute-done.10
  315.9 2.2 collective-permute-done.16
  318.2 2.6 collective-permute-start.17
  321.1 2.6 collective-permute-start.22
  323.8 4.3 collective-permute-start.12
  328.0 6.7 %collective-permute-done.17 = bf16[576,128]{1,0:T(8,128)(2,1)S(1)} collective-permute-done((bf16[576,128]{1,0:T(8,128)(2,1)S(1)}, bf16[576,128]{1,0:T(8,128)(2,1)S(1)}, u32[]{:S(2)}, u32[]{:S(2)}) %collective-permute-start.17) | collective-permute-done | bytes 147488 | tf_op jit(solution)/shard_map/ppermute | solution.py:502
  334.8 3.1 collective-permute-done.22
  337.9 2.5 collective-permute-done.12
  341.3 1.3 copy.34
  342.6 5.3 %fusion.65 = bf16[416,768]{1,0:T(8,128)(2,1)S(1)} fusion(f32[416,768]{1,0:T(8,128)S(1)} %get-tuple-element.105, bf16[416,3072]{1,0:T(8,128)(2,1)} %get-tuple-element.106.act_ref, bf16[3072,768]{1,0:T(8,128)(2,1)} %reshape.659, f32[768]{0:T(1024)S(1)} %get-tuple-element.61, f32[416]{0:T(512)S(1)} %mul.382), kind=kOutput, calls=%fused_computation.97 | convolution fusion | flops 1964212224 | bytes 9196160 | tf_op jit(solution)/shard_map/dot_general | solution.py:452
  347.9 1.3 copy.35
  349.2 57.0 %all-gather.2.cloned.1.call-done = bf16[27904,128]{1,0:T(8,128)(2,1)} async-done(((bf16[1744,128]{1,0:T(8,128)(2,1)}), bf16[27904,128]{1,0:T(8,128)(2,1)}) %all-gather.2.cloned.1.call-update) | async-done | bytes 7143440 | tf_op jit(solution)/shard_map/all_gather | solution.py:618
  406.2 3.9 slice.376
  410.1 9.0 %fusion.56 = (bf16[3464,128]{1,0:T(8,128)(2,1)S(1)}, bf16[3464,128]{1,0:T(8,128)(2,1)}) fusion(f32[8,3464,128]{2,1,0:T(8,128)} %bitcast.334, s32[]{:T(128)S(6)} %select_n.199, f32[8,3464,128]{2,1,0:T(8,128)} %bitcast.321, f32[8,3464,128]{2,1,0:T(8,128)} %bitcast.318, bf16[8,3464,128]{2,1,0:T(8,128)(2,1)S(1)} %bitcast.329, s32[]{:T(128)S(6)} %select_n.198), kind=kLoop, calls=%fused_computation.88 | loop fusion | flops 15962112 | bytes 14188552 | tf_op jit(solution)/shard_map/convert_element_type | solution.py:639
  419.1 1.5 collective-permute-start.23
  420.6 17.5 %fusion = (f32[27712,128]{1,0:T(8,128)}, f32[27712,128]{1,0:T(8,128)}) fusion(f32[27712,128]{1,0:T(8,128)} %param.10, bf16[27904,128]{1,0:T(8,128)(2,1)S(1)} %bitcast.333), kind=kLoop, calls=%fused_computation.5 | loop fusion | flops 17735680 | bytes 49659904 | tf_op jit(solution)/shard_map/add | solution.py:571
  438.7 2.4 collective-permute-done.23
  441.6 1.5 collective-permute-start.25
  443.2 30.6 %fusion.121 = (bf16[27712,128]{1,0:T(8,128)(2,1)}, f32[27712,128]{1,0:T(8,128)}, f32[27712,128]{1,0:T(8,128)}) fusion(f32[27712,128]{1,0:T(8,128)S(1)} %bitcast.320, bf16[27712,128]{1,0:T(8,128)(2,1)} %copy-done, f32[27712,128]{1,0:T(8,128)} %param.10, f32[27712,128]{1,0:T(8,128)} %param.11), kind=kLoop, calls=%fused_computation.280 | loop fusion | flops 63848448 | bytes 85131264 | tf_op jit(solution)/shard_map/convert_element_type | solution.py:635
  473.8 6.5 %constant_dynamic-update-slice_fusion = bf16[2,8,3464,128]{3,2,1,0:T(8,128)(2,1)} fusion(bf16[2,8,3464,128]{3,2,1,0:T(8,128)(2,1)} %bitcast_dynamic-update-slice_fusion.8, bf16[1,8,3464,128]{3,2,1,0:T(8,128)(2,1)} %bitcast.331, s32[]{:T(128)S(6)} %select_n.197), kind=kLoop, calls=%fused_computation.224 | loop fusion | bytes 14188548 | tf_op jit(solution)/shard_map/dynamic_update_slice | solution.py:530
  480.3 1.5 collective-permute-start.26
  481.8 2.1 bitcast_dynamic-update-slice_fusion.7
  484.1 2.1 bitcast_dynamic-update-slice_fusion.6
  486.6 2.1 bitcast_dynamic-update-slice_fusion.5
  488.7 13.7 %collective-permute-done.26 = bf16[3464,128]{1,0:T(8,128)(2,1)S(1)} collective-permute-done((bf16[3464,128]{1,0:T(8,128)(2,1)S(1)}, bf16[3464,128]{1,0:T(8,128)(2,1)S(1)}, u32[]{:S(2)}, u32[]{:S(2)}) %collective-permute-start.26) | collective-permute-done | bytes 886816 | tf_op jit(solution)/shard_map/ppermute | solution.py:502
  503.4 2.1 bitcast_dynamic-update-slice_fusion.3
  (166 shorter events, 35.6 us)
Async XLA Ops:
  7.2 399.0 %all-gather.2.cloned.1.call-start = ((), (), s32[]{:S(2)}) async-start(), calls=%async_computation | async-start | bytes 7589888 | tf_op jit(solution)/shard_map/all_gather | solution.py:618
  10.4 30.8 %collective-permute-start = (bf16[3464,128]{1,0:T(8,128)(2,1)}, bf16[3464,128]{1,0:T(8,128)(2,1)S(1)}, u32[]{:S(2)}, u32[]{:S(2)}) collective-permute-start(bf16[3464,128]{1,0:T(8,128)(2,1)} %get-tuple-element.71), channel_id=1, source_target_pairs={{0,1},{1,0},{2,3},{3,2},{4,5},{5,4},{6,7},{7,6},{8,9},{9,8},{10,11... | collective-permute-start | bytes 2660360 | tf_op jit(solution)/shard_map/ppermute | solution.py:502
  13.4 7.9 %copy-start.10 = (s32[2,1]{0,1:T(1,128)S(1)}, s32[2,1]{0,1:T(1,128)}, u32[]{:S(2)}) copy-start(s32[2,1]{0,1:T(1,128)} %param.8) | copy-start | bytes 28
  41.2 21.2 %collective-permute-start.1 = (bf16[3464,128]{1,0:T(8,128)(2,1)S(1)}, bf16[3464,128]{1,0:T(8,128)(2,1)S(1)}, u32[]{:S(2)}, u32[]{:S(2)}) collective-permute-start(bf16[3464,128]{1,0:T(8,128)(2,1)S(1)} %collective-permute-done), channel_id=1, source_target_pairs={{0,4},{2,6},{4,0},{6,2},{8,12},{10,14},{12,8},{14,10},{16,20},{18,... | collective-permute-start | bytes 2660360 | tf_op jit(solution)/shard_map/ppermute | solution.py:502
  42.7 20.9 %collective-permute-start.2 = (bf16[3464,128]{1,0:T(8,128)(2,1)S(1)}, bf16[3464,128]{1,0:T(8,128)(2,1)S(1)}, u32[]{:S(2)}, u32[]{:S(2)}) collective-permute-start(bf16[3464,128]{1,0:T(8,128)(2,1)S(1)} %collective-permute-done), channel_id=1, source_target_pairs={{0,8},{2,10},{4,12},{6,14},{8,0},{10,2},{12,4},{14,6},{16,24},{18,... | collective-permute-start | bytes 2660360 | tf_op jit(solution)/shard_map/ppermute | solution.py:502
  44.3 25.0 %collective-permute-start.4 = (bf16[3464,128]{1,0:T(8,128)(2,1)S(1)}, bf16[3464,128]{1,0:T(8,128)(2,1)S(1)}, u32[]{:S(2)}, u32[]{:S(2)}) collective-permute-start(bf16[3464,128]{1,0:T(8,128)(2,1)S(1)} %collective-permute-done), channel_id=1, source_target_pairs={{0,2},{2,0},{4,6},{6,4},{8,10},{10,8},{12,14},{14,12},{16,18},{18,... | collective-permute-start | bytes 2660360 | tf_op jit(solution)/shard_map/ppermute | solution.py:502
  44.3 22.1 %collective-permute-start.3 = (bf16[3464,128]{1,0:T(8,128)(2,1)S(1)}, bf16[3464,128]{1,0:T(8,128)(2,1)S(1)}, u32[]{:S(2)}, u32[]{:S(2)}) collective-permute-start(bf16[3464,128]{1,0:T(8,128)(2,1)S(1)} %get-tuple-element.27), channel_id=1, source_target_pairs={{0,1},{1,0},{2,3},{3,2},{4,5},{5,4},{6,7},{7,6},{8,9},{9,8},{10,11... | collective-permute-start | bytes 2660360 | tf_op jit(solution)/shard_map/ppermute | solution.py:502
  62.4 7.9 %collective-permute-start.5 = (bf16[3464,128]{1,0:T(8,128)(2,1)S(1)}, bf16[3464,128]{1,0:T(8,128)(2,1)S(1)}, u32[]{:S(2)}, u32[]{:S(2)}) collective-permute-start(bf16[3464,128]{1,0:T(8,128)(2,1)S(1)} %collective-permute-done.1), channel_id=1, source_target_pairs={{0,2},{2,0},{4,6},{6,4},{8,10},{10,8},{12,14},{14,12},{16,18},{18,... | collective-permute-start | bytes 2660360 | tf_op jit(solution)/shard_map/ppermute | solution.py:502
  63.6 7.7 %collective-permute-start.6 = (bf16[3464,128]{1,0:T(8,128)(2,1)S(1)}, bf16[3464,128]{1,0:T(8,128)(2,1)S(1)}, u32[]{:S(2)}, u32[]{:S(2)}) collective-permute-start(bf16[3464,128]{1,0:T(8,128)(2,1)S(1)} %collective-permute-done.2), channel_id=1, source_target_pairs={{0,2},{2,0},{4,6},{6,4},{8,10},{10,8},{12,14},{14,12},{16,18},{18,... | collective-permute-start | bytes 2660360 | tf_op jit(solution)/shard_map/ppermute | solution.py:502
  66.4 5.8 %collective-permute-start.7 = (bf16[3464,128]{1,0:T(8,128)(2,1)S(1)}, bf16[3464,128]{1,0:T(8,128)(2,1)S(1)}, u32[]{:S(2)}, u32[]{:S(2)}) collective-permute-start(bf16[3464,128]{1,0:T(8,128)(2,1)S(1)} %collective-permute-done.3), channel_id=1, source_target_pairs={{0,2},{2,0},{4,6},{6,4},{8,10},{10,8},{12,14},{14,12},{16,18},{18,... | collective-permute-start | bytes 2660360 | tf_op jit(solution)/shard_map/ppermute | solution.py:502
  151.7 15.4 %slice-start.6 = ((s8[4718592]{0:T(1024)(128)(4,1)}), s8[4194304]{0:T(1024)(128)(4,1)S(1)}, s32[]{:S(2)}) async-start(s8[4718592]{0:T(1024)(128)(4,1)} %bitcast.336), calls=%async_computation.7 | async-start | bytes 8388608
  151.7 19.0 %slice-start.8 = ((s8[4718592]{0:T(1024)(128)(4,1)}), s8[4194304]{0:T(1024)(128)(4,1)S(1)}, s32[]{:S(2)}) async-start(s8[4718592]{0:T(1024)(128)(4,1)} %bitcast.338), calls=%async_computation.9 | async-start | bytes 8388608
  152.0 15.1 %copy-start.4 = (bf16[416,768]{1,0:T(8,128)(2,1)}, bf16[416,768]{1,0:T(8,128)(2,1)S(1)}, u32[]{:S(2)}) copy-start(bf16[416,768]{1,0:T(8,128)(2,1)S(1)} %add_convert_fusion.7.n2_ref) | copy-start | bytes 1916932
  152.0 15.1 %slice-start.7 = ((s8[4718592]{0:T(1024)(128)(4,1)}), s8[524288]{0:T(1024)(128)(4,1)S(1)}, s32[]{:S(2)}) async-start(s8[4718592]{0:T(1024)(128)(4,1)} %bitcast.336), calls=%async_computation.8 | async-start | bytes 1048576
  152.0 18.7 %slice-start.9 = ((s8[4718592]{0:T(1024)(128)(4,1)}), s8[524288]{0:T(1024)(128)(4,1)S(1)}, s32[]{:S(2)}) async-start(s8[4718592]{0:T(1024)(128)(4,1)} %bitcast.338), calls=%async_computation.10 | async-start | bytes 1048576
  170.8 2.6 copy-start.5
  173.4 1.9 copy-start.2
  175.3 1.6 copy-start.3
  202.9 6.7 %copy-start.1 = (f32[416,768]{1,0:T(8,128)S(1)}, f32[416,768]{1,0:T(8,128)}, u32[]{:S(2)}) copy-start(f32[416,768]{1,0:T(8,128)} %get-tuple-element.58) | copy-start | bytes 3833860
  257.8 4.9 collective-permute-start.13
  258.3 7.7 %collective-permute-start.18 = (bf16[2,2,2,2,576,128]{5,4,3,2,1,0:T(8,128)(2,1)}, bf16[2,2,2,2,576,128]{5,4,3,2,1,0:T(8,128)(2,1)S(1)}, u32[]{:S(2)}, u32[]{:S(2)}) collective-permute-start(bf16[2,2,2,2,576,128]{5,4,3,2,1,0:T(8,128)(2,1)} %get-tuple-element.39), channel_id=1, source_target_pairs={{0,2},{2,0},{4,6},{6,4},{8,10},{10,8},{12,14},{14,12},{16,18},{18,... | collective-permute-start | bytes 7077896 | tf_op jit(solution)/shard_map/ppermute | solution.py:502
  258.4 11.1 %collective-permute-start.8 = (bf16[2,2,2,2,592,128]{5,4,3,2,1,0:T(8,128)(2,1)}, bf16[2,2,2,2,592,128]{5,4,3,2,1,0:T(8,128)(2,1)S(1)}, u32[]{:S(2)}, u32[]{:S(2)}) collective-permute-start(bf16[2,2,2,2,592,128]{5,4,3,2,1,0:T(8,128)(2,1)} %get-tuple-element.35), channel_id=1, source_target_pairs={{0,2},{2,0},{4,6},{6,4},{8,10},{10,8},{12,14},{14,12},{16,18},{18,... | collective-permute-start | bytes 7274504 | tf_op jit(solution)/shard_map/ppermute | solution.py:502
  262.7 3.4 copy-start.8
  265.1 28.3 %collective-permute-start.14 = (bf16[2,2,2,576,128]{4,3,2,1,0:T(8,128)(2,1)S(1)}, bf16[2,2,2,576,128]{4,3,2,1,0:T(8,128)(2,1)S(1)}, u32[]{:S(2)}, u32[]{:S(2)}) collective-permute-start(bf16[2,2,2,576,128]{4,3,2,1,0:T(8,128)(2,1)S(1)} %get-tuple-element.78), channel_id=1, source_target_pairs={{0,4},{2,6},{4,0},{6,2},{8,12},{10,14},{12,8},{14,10},{16,20},{18,... | collective-permute-start | bytes 3538952 | tf_op jit(solution)/shard_map/ppermute | solution.py:502
  266.1 3.5 copy-start.7
  266.7 28.3 %collective-permute-start.19 = (bf16[2,2,2,576,128]{4,3,2,1,0:T(8,128)(2,1)S(1)}, bf16[2,2,2,576,128]{4,3,2,1,0:T(8,128)(2,1)S(1)}, u32[]{:S(2)}, u32[]{:S(2)}) collective-permute-start(bf16[2,2,2,576,128]{4,3,2,1,0:T(8,128)(2,1)S(1)} %get-tuple-element.80), channel_id=1, source_target_pairs={{0,8},{2,10},{4,12},{6,14},{8,0},{10,2},{12,4},{14,6},{16,24},{18,... | collective-permute-start | bytes 3538952 | tf_op jit(solution)/shard_map/ppermute | solution.py:502
  270.2 29.6 %collective-permute-start.9 = (bf16[2,2,2,592,128]{4,3,2,1,0:T(8,128)(2,1)S(1)}, bf16[2,2,2,592,128]{4,3,2,1,0:T(8,128)(2,1)S(1)}, u32[]{:S(2)}, u32[]{:S(2)}) collective-permute-start(bf16[2,2,2,592,128]{4,3,2,1,0:T(8,128)(2,1)S(1)} %get-tuple-element.76), channel_id=1, source_target_pairs={{0,1},{1,0},{2,3},{3,2},{4,5},{5,4},{6,7},{7,6},{8,9},{9,8},{10,11... | collective-permute-start | bytes 3637256 | tf_op jit(solution)/shard_map/ppermute | solution.py:502
  293.7 14.8 %collective-permute-start.15 = (bf16[2,2,576,128]{3,2,1,0:T(8,128)(2,1)S(1)}, bf16[2,2,576,128]{3,2,1,0:T(8,128)(2,1)S(1)}, u32[]{:S(2)}, u32[]{:S(2)}) collective-permute-start(bf16[2,2,576,128]{3,2,1,0:T(8,128)(2,1)S(1)} %get-tuple-element.84), channel_id=1, source_target_pairs={{0,8},{2,10},{4,12},{6,14},{8,0},{10,2},{12,4},{14,6},{16,24},{18,... | collective-permute-start | bytes 1769480 | tf_op jit(solution)/shard_map/ppermute | solution.py:502
  295.3 17.1 %collective-permute-start.20 = (bf16[2,2,576,128]{3,2,1,0:T(8,128)(2,1)S(1)}, bf16[2,2,576,128]{3,2,1,0:T(8,128)(2,1)S(1)}, u32[]{:S(2)}, u32[]{:S(2)}) collective-permute-start(bf16[2,2,576,128]{3,2,1,0:T(8,128)(2,1)S(1)} %get-tuple-element.86), channel_id=1, source_target_pairs={{0,1},{1,0},{2,3},{3,2},{4,5},{5,4},{6,7},{7,6},{8,9},{9,8},{10,11... | collective-permute-start | bytes 1769480 | tf_op jit(solution)/shard_map/ppermute | solution.py:502
  300.1 15.1 %collective-permute-start.10 = (bf16[2,2,592,128]{3,2,1,0:T(8,128)(2,1)S(1)}, bf16[2,2,592,128]{3,2,1,0:T(8,128)(2,1)S(1)}, u32[]{:S(2)}, u32[]{:S(2)}) collective-permute-start(bf16[2,2,592,128]{3,2,1,0:T(8,128)(2,1)S(1)} %get-tuple-element.82), channel_id=1, source_target_pairs={{0,4},{2,6},{4,0},{6,2},{8,12},{10,14},{12,8},{14,10},{16,20},{18,... | collective-permute-start | bytes 1818632 | tf_op jit(solution)/shard_map/ppermute | solution.py:502
  308.7 9.4 %collective-permute-start.16 = (bf16[2,576,128]{2,1,0:T(8,128)(2,1)S(1)}, bf16[2,576,128]{2,1,0:T(8,128)(2,1)S(1)}, u32[]{:S(2)}, u32[]{:S(2)}) collective-permute-start(bf16[2,576,128]{2,1,0:T(8,128)(2,1)S(1)} %get-tuple-element.90), channel_id=1, source_target_pairs={{0,1},{1,0},{2,3},{3,2},{4,5},{5,4},{6,7},{7,6},{8,9},{9,8},{10,11... | collective-permute-start | bytes 884744 | tf_op jit(solution)/shard_map/ppermute | solution.py:502
  312.6 8.4 %collective-permute-start.21 = (bf16[2,576,128]{2,1,0:T(8,128)(2,1)S(1)}, bf16[2,576,128]{2,1,0:T(8,128)(2,1)S(1)}, u32[]{:S(2)}, u32[]{:S(2)}) collective-permute-start(bf16[2,576,128]{2,1,0:T(8,128)(2,1)S(1)} %get-tuple-element.92), channel_id=1, source_target_pairs={{0,4},{2,6},{4,0},{6,2},{8,12},{10,14},{12,8},{14,10},{16,20},{18,... | collective-permute-start | bytes 884744 | tf_op jit(solution)/shard_map/ppermute | solution.py:502
  315.4 25.9 %copy-start.6 = (bf16[416,768]{1,0:T(8,128)(2,1)S(1)}, bf16[416,768]{1,0:T(8,128)(2,1)}, u32[]{:S(2)}) copy-start(bf16[416,768]{1,0:T(8,128)(2,1)} %get-tuple-element.94) | copy-start | bytes 1916932
  315.4 8.3 %collective-permute-start.11 = (bf16[2,592,128]{2,1,0:T(8,128)(2,1)S(1)}, bf16[2,592,128]{2,1,0:T(8,128)(2,1)S(1)}, u32[]{:S(2)}, u32[]{:S(2)}) collective-permute-start(bf16[2,592,128]{2,1,0:T(8,128)(2,1)S(1)} %get-tuple-element.88), channel_id=1, source_target_pairs={{0,8},{2,10},{4,12},{6,14},{8,0},{10,2},{12,4},{14,6},{16,24},{18,... | collective-permute-start | bytes 909320 | tf_op jit(solution)/shard_map/ppermute | solution.py:502
  318.2 16.5 %collective-permute-start.17 = (bf16[576,128]{1,0:T(8,128)(2,1)S(1)}, bf16[576,128]{1,0:T(8,128)(2,1)S(1)}, u32[]{:S(2)}, u32[]{:S(2)}) collective-permute-start(bf16[576,128]{1,0:T(8,128)(2,1)S(1)} %fusion.101), channel_id=1, source_target_pairs={{0,16},{2,18},{4,20},{6,22},{8,24},{10,26},{12,28},{14,30},{16,0},... | collective-permute-start | bytes 442376 | tf_op jit(solution)/shard_map/ppermute | solution.py:502
  321.1 16.8 %collective-permute-start.22 = (bf16[576,128]{1,0:T(8,128)(2,1)S(1)}, bf16[576,128]{1,0:T(8,128)(2,1)S(1)}, u32[]{:S(2)}, u32[]{:S(2)}) collective-permute-start(bf16[576,128]{1,0:T(8,128)(2,1)S(1)} %fusion.103), channel_id=1, source_target_pairs={{0,16},{2,18},{4,20},{6,22},{8,24},{10,26},{12,28},{14,30},{16,0},... | collective-permute-start | bytes 442376 | tf_op jit(solution)/shard_map/ppermute | solution.py:502
  323.8 16.6 %collective-permute-start.12 = (bf16[592,128]{1,0:T(8,128)(2,1)S(1)}, bf16[592,128]{1,0:T(8,128)(2,1)S(1)}, u32[]{:S(2)}, u32[]{:S(2)}) collective-permute-start(bf16[592,128]{1,0:T(8,128)(2,1)S(1)} %fusion.99), channel_id=1, source_target_pairs={{0,16},{2,18},{4,20},{6,22},{8,24},{10,26},{12,28},{14,30},{16,0},... | collective-permute-start | bytes 454664 | tf_op jit(solution)/shard_map/ppermute | solution.py:502
  410.0 9.0 %copy-start = (bf16[27712,128]{1,0:T(8,128)(2,1)}, bf16[27712,128]{1,0:T(8,128)(2,1)S(1)}, u32[]{:S(2)}) copy-start(bf16[27712,128]{1,0:T(8,128)(2,1)S(1)} %slice.376) | copy-start | bytes 21282820
  410.1 10.6 %slice-start.4 = ((s8[7143424]{0:T(1024)(128)(4,1)}), s8[4194304]{0:T(1024)(128)(4,1)S(1)}, s32[]{:S(2)}) async-start(s8[7143424]{0:T(1024)(128)(4,1)} %bitcast.332), calls=%async_computation.5 | async-start | bytes 8388608
  410.1 10.6 %slice-start.5 = ((s8[7143424]{0:T(1024)(128)(4,1)}), s8[2949120]{0:T(1024)(128)(4,1)S(1)}, s32[]{:S(2)}) async-start(s8[7143424]{0:T(1024)(128)(4,1)} %bitcast.332), calls=%async_computation.6 | async-start | bytes 5898240
  419.0 24.1 %slice-start = ((s8[14188544]{0:T(1024)(128)(4,1)}), s8[4194304]{0:T(1024)(128)(4,1)S(1)}, s32[]{:S(2)}) async-start(s8[14188544]{0:T(1024)(128)(4,1)} %bitcast.319), calls=%async_computation.1 | async-start | bytes 8388608
  419.0 24.1 %slice-start.1 = ((s8[14188544]{0:T(1024)(128)(4,1)}), s8[4194304]{0:T(1024)(128)(4,1)S(1)}, s32[]{:S(2)}) async-start(s8[14188544]{0:T(1024)(128)(4,1)} %bitcast.319), calls=%async_computation.2 | async-start | bytes 8388608
  419.1 24.1 %slice-start.2 = ((s8[14188544]{0:T(1024)(128)(4,1)}), s8[4194304]{0:T(1024)(128)(4,1)S(1)}, s32[]{:S(2)}) async-start(s8[14188544]{0:T(1024)(128)(4,1)} %bitcast.319), calls=%async_computation.3 | async-start | bytes 8388608
  419.1 24.1 %slice-start.3 = ((s8[14188544]{0:T(1024)(128)(4,1)}), s8[1605632]{0:T(1024)(128)(4,1)S(1)}, s32[]{:S(2)}) async-start(s8[14188544]{0:T(1024)(128)(4,1)} %bitcast.319), calls=%async_computation.4 | async-start | bytes 3211264
  419.1 22.0 %collective-permute-start.23 = (bf16[3464,128]{1,0:T(8,128)(2,1)S(1)}, bf16[3464,128]{1,0:T(8,128)(2,1)}, u32[]{:S(2)}, u32[]{:S(2)}) collective-permute-start(bf16[3464,128]{1,0:T(8,128)(2,1)S(1)} %get-tuple-element.59), channel_id=1, source_target_pairs={{0,1},{1,0},{2,3},{3,2},{4,5},{5,4},{6,7},{7,6},{8,9},{9,8},{10,11... | collective-permute-start | bytes 2660360 | tf_op jit(solution)/shard_map/ppermute | solution.py:502
  441.1 42.8 %collective-permute-start.24 = (bf16[3464,128]{1,0:T(8,128)(2,1)}, bf16[3464,128]{1,0:T(8,128)(2,1)}, u32[]{:S(2)}, u32[]{:S(2)}) collective-permute-start(bf16[3464,128]{1,0:T(8,128)(2,1)} %collective-permute-done.23), channel_id=1, source_target_pairs={{0,4},{2,6},{4,0},{6,2},{8,12},{10,14},{12,8},{14,10},{16,20},{18,... | collective-permute-start | bytes 2660360 | tf_op jit(solution)/shard_map/ppermute | solution.py:502
  441.6 44.7 %collective-permute-start.25 = (bf16[3464,128]{1,0:T(8,128)(2,1)}, bf16[3464,128]{1,0:T(8,128)(2,1)}, u32[]{:S(2)}, u32[]{:S(2)}) collective-permute-start(bf16[3464,128]{1,0:T(8,128)(2,1)} %collective-permute-done.23), channel_id=1, source_target_pairs={{0,8},{2,10},{4,12},{6,14},{8,0},{10,2},{12,4},{14,6},{16,24},{18,... | collective-permute-start | bytes 2660360 | tf_op jit(solution)/shard_map/ppermute | solution.py:502
  443.2 60.2 %collective-permute-start.27 = (bf16[3464,128]{1,0:T(8,128)(2,1)}, bf16[3464,128]{1,0:T(8,128)(2,1)}, u32[]{:S(2)}, u32[]{:S(2)}) collective-permute-start(bf16[3464,128]{1,0:T(8,128)(2,1)} %collective-permute-done.23), channel_id=1, source_target_pairs={{0,2},{2,0},{4,6},{6,4},{8,10},{10,8},{12,14},{14,12},{16,18},{18,... | collective-permute-start | bytes 2660360 | tf_op jit(solution)/shard_map/ppermute | solution.py:502
  473.8 6.5 %copy-start.9 = (bf16[3464,128]{1,0:T(8,128)(2,1)S(1)}, bf16[3464,128]{1,0:T(8,128)(2,1)}, u32[]{:S(2)}) copy-start(bf16[3464,128]{1,0:T(8,128)(2,1)} %get-tuple-element.43) | copy-start | bytes 2660356
  480.3 22.1 %collective-permute-start.26 = (bf16[3464,128]{1,0:T(8,128)(2,1)S(1)}, bf16[3464,128]{1,0:T(8,128)(2,1)S(1)}, u32[]{:S(2)}, u32[]{:S(2)}) collective-permute-start(bf16[3464,128]{1,0:T(8,128)(2,1)S(1)} %copy-done.9), channel_id=1, source_target_pairs={{0,1},{1,0},{2,3},{3,2},{4,5},{5,4},{6,7},{7,6},{8,9},{9,8},{10,11... | collective-permute-start | bytes 2660360 | tf_op jit(solution)/shard_map/ppermute | solution.py:502
  483.9 21.6 %collective-permute-start.28 = (bf16[3464,128]{1,0:T(8,128)(2,1)}, bf16[3464,128]{1,0:T(8,128)(2,1)S(1)}, u32[]{:S(2)}, u32[]{:S(2)}) collective-permute-start(bf16[3464,128]{1,0:T(8,128)(2,1)} %collective-permute-done.24), channel_id=1, source_target_pairs={{0,2},{2,0},{4,6},{6,4},{8,10},{10,8},{12,14},{14,12},{16,18},{18,... | collective-permute-start | bytes 2660360 | tf_op jit(solution)/shard_map/ppermute | solution.py:502
  486.3 20.2 %collective-permute-start.29 = (bf16[3464,128]{1,0:T(8,128)(2,1)}, bf16[3464,128]{1,0:T(8,128)(2,1)S(1)}, u32[]{:S(2)}, u32[]{:S(2)}) collective-permute-start(bf16[3464,128]{1,0:T(8,128)(2,1)} %collective-permute-done.25), channel_id=1, source_target_pairs={{0,2},{2,0},{4,6},{6,4},{8,10},{10,8},{12,14},{14,12},{16,18},{18,... | collective-permute-start | bytes 2660360 | tf_op jit(solution)/shard_map/ppermute | solution.py:502
  502.4 5.1 collective-permute-start.30
Sparse Core Ops, SparseCore 0:
  341.4 64.7 all-gather.1

commit v6 on v5

--- a/solution.py
+++ b/solution.py
@@ -307,16 +307,19 @@
             owner, place, source, size = chunks[sent]
             slot = sent % 2
             finish(slot)
-            step = next(s for s in (128, 64, 32, 16) if size % s == 0)
-
-            def convert(i, carry, source=source, slot=slot, step=step):
-                at = pl.multiple_of(i * step, step)
-                stage_ref[slot, pl.ds(at, step), :] = rows_ref[
-                    pl.ds(pl.multiple_of(source + at, 16), step), :
+
+            def convert(at, count, source=source, slot=slot):
+                stage_ref[slot, pl.ds(at, count), :] = rows_ref[
+                    pl.ds(pl.multiple_of(source + at, 16), count), :
                 ].astype(jnp.bfloat16)
+
+            def convert_block(i, carry, convert=convert):
+                convert(pl.multiple_of(i * 128, 128), 128)
                 return carry
 
-            lax.fori_loop(0, size // step, convert, 0)
+            lax.fori_loop(0, size // 128, convert_block, 0)
+            if size % 128:
+                convert(size - size % 128, size % 128)
             if size < share:
                 bias_place = part_rows - place * share
                 first = max(0, -bias_place)

time: 526 us -> 515 us (0.979)
  Pallas kernels: 95.2 us -> 84.8 us
    pallas_call x1, Pallas kernels: 45.3 us -> 34.9 us  [pack_shares(): pl.pallas_call(functools.partial(pack_kernel, part_rows=part_rows, share_...]
  transfers between devices with their start and end apart: 32 -> 32, of which waited for: 20 -> 20; matrix products, arithmetic and copies ran while one was open for 22% -> 23% of each run, Pallas kernels for 0% -> 0%
where the time goes in v6:
time: 515 us; the launch traced here: 505 us
  waiting for transfers between devices  155 us (30%)
  local copies, waits for them, and re-layouts  96.3 us (19%)
  Pallas kernels  84.8 us (16%)
  other arithmetic  84.4 us (16%)
  matrix products  41.7 us (8%)
  starting transfers between devices  28.2 us (5%)
  between operations  15 us (3%)
    ppermute x31, waiting for transfers between devices, swap(): lax.ppermute(values, axis, [(i, i ^ bit) for i in range(lax.axis_size(axi...  97.8 us
    all_gather x1, waiting for transfers between devices, body(): totals = lax.all_gather(owned, 'wide', axis=0, tiled=True)  57 us
    pallas_call x1, Pallas kernels, pack_shares(): pl.pallas_call(functools.partial(pack_kernel, part_rows=part_rows, share_...  34.9 us
    convert_element_type x1, other arithmetic, finish(): return later[0].astype(jnp.bfloat16)  30.6 us
    ppermute x31, starting transfers between devices, swap(): lax.ppermute(values, axis, [(i, i ^ bit) for i in range(lax.axis_size(axi...  28.2 us
    reshape x4, local copies, waits for them, and re-layouts, unpack(): members.append(rows[row:row + length].reshape(dims_of))  27.1 us
    pallas_call x1, Pallas kernels, attend(): pl.pallas_call(attend_kernel, grid=(wins, pairs), in_specs=[column(0), co...  25.3 us
    pallas_call x1, Pallas kernels, attend_back(): pl.pallas_call(attend_back_kernel, grid=(wins, pairs), in_specs=[column(0...  24.6 us
  transfers between devices with their start and end apart: 32, of which 20 were waited for; matrix products, arithmetic and copies ran while one was open for 23% of the time, Pallas kernels for 0%

profile of v6, /device:TPU:0, one launch (start us, length us, event | category | flops | bytes accessed | tf_op | source)
XLA Modules:
  0.0 505.3 jit_solution(2363339320981811021)
XLA Ops:
  7.2 3.2 bitcast_convert_fusion
  10.4 3.0 collective-permute-start
  13.4 7.9 %convert_element_type.597 = bf16[27712,128]{1,0:T(8,128)(2,1)} convert(f32[27712,128]{1,0:T(8,128)} %param.9) | non-fusion elementwise | flops 3547136 | bytes 21282816 | tf_op jit(solution)/shard_map/convert_element_type | solution.py:599
  21.4 1.4 copy_bitcast_fusion
  24.7 1.3 fusion.66
  27.6 7.1 %reshape.652 = bf16[2,8,3464,128]{3,2,1,0:T(8,128)(2,1)} broadcast(bf16[]{:T(256)} %constant.104.clone.1), dimensions={} | broadcast | bytes 14188546 | tf_op jit(solution)/shard_map/reshape | solution.py:532
  34.8 6.4 %constant_dynamic-update-slice_fusion.1 = bf16[2,8,3464,128]{3,2,1,0:T(8,128)(2,1)} fusion(bf16[2,8,3464,128]{3,2,1,0:T(8,128)(2,1)} %reshape.652, bf16[1,8,3464,128]{3,2,1,0:T(8,128)(2,1)} %bitcast.330, s32[]{:T(128)S(6)} %select_n.197), kind=kLoop, calls=%fused_computation.225 | loop fusion | bytes 14188548 | tf_op jit(solution)/shard_map/dynamic_update_slice | solution.py:533
  41.2 1.5 collective-permute-start.1
  42.7 1.6 collective-permute-start.2
  45.8 16.6 %collective-permute-done.1 = bf16[3464,128]{1,0:T(8,128)(2,1)S(1)} collective-permute-done((bf16[3464,128]{1,0:T(8,128)(2,1)S(1)}, bf16[3464,128]{1,0:T(8,128)(2,1)S(1)}, u32[]{:S(2)}, u32[]{:S(2)}) %collective-permute-start.1) | collective-permute-done | bytes 886816 | tf_op jit(solution)/shard_map/ppermute | solution.py:505
  62.4 1.2 collective-permute-done.2
  63.6 2.8 collective-permute-done.3
  74.7 3.4 slice.318
  78.1 1.6 slice.324
  79.7 9.3 %fusion.125 = (bf16[18432,128]{1,0:T(8,128)(2,1)}, bf16[18432,128]{1,0:T(8,128)(2,1)}) fusion(bf16[55424,128]{1,0:T(8,128)(2,1)} %bitcast.326), kind=kLoop, calls=%fused_computation.282 | loop fusion | bytes 18874368 | tf_op jit(solution)/shard_map/slice | solution.py:52
  90.2 7.6 %reshape.656 = bf16[768,2304]{1,0:T(8,128)(2,1)} reshape(bf16[13824,128]{1,0:T(8,128)(2,1)} %slice.318) | data formatting | bytes 7077888 | tf_op jit(solution)/shard_map/reshape | solution.py:52
  97.8 1.9 reshape.657
  100.9 5.0 fusion.25.q_ref.k_ref.v_ref
  105.9 25.3 %attend.1 = (bf16[2,12,208,208]{3,2,1,0:T(8,128)(2,1)}, bf16[416,768]{1,0:T(8,128)(2,1)}) custom-call(bf16[416,2304]{1,0:T(8,128)(2,1)} %fusion.25.q_ref.k_ref.v_ref, bf16[416,2304]{1,0:T(8,128)(2,1)} %fusion.25.q_ref.k_ref.v_ref, bf16[416,2304]{1,0:T(8,128)(2,1)} %fusion.25.q_ref.k_ref.v_ref, bf16[64,128]{1,0:T(8,128)(2,1)} %pad_maximum_fusion.1.table_ref, ...), custom_call_target="tpu_custom_call" | custom-call | tf_op jit(solution)/shard_map/attend/pallas_call | solution.py:169
  131.2 2.7 fusion.127
  134.1 8.4 %reshape.658 = bf16[768,3072]{1,0:T(8,128)(2,1)} reshape(bf16[18432,128]{1,0:T(8,128)(2,1)} %get-tuple-element.70) | data formatting | bytes 9437184 | tf_op jit(solution)/shard_map/reshape | solution.py:52
  142.5 9.2 %reshape.659 = bf16[3072,768]{1,0:T(8,128)(2,1)} reshape(bf16[18432,128]{1,0:T(8,128)(2,1)} %get-tuple-element.69) | data formatting | bytes 9437184 | tf_op jit(solution)/shard_map/reshape | solution.py:52
  152.1 15.1 %fusion.11 = (bf16[416,3072]{1,0:T(8,128)(2,1)}, f32[416,3072]{1,0:T(8,128)S(1)}) fusion(f32[3072]{0:T(1024)S(1)} %fusion.105, bf16[416,768]{1,0:T(8,128)(2,1)S(1)} %add_convert_fusion.7.n2_ref, bf16[768,3072]{1,0:T(8,128)(2,1)} %reshape.658), kind=kOutput, calls=%fused_computation.18 | convolution fusion | flops 2047279104 | bytes 13037568 | tf_op jit(solution)/shard_map/dot_general | solution.py:449
  167.2 3.6 fusion.17.dpre_ref
  170.8 2.6 multiply_reduce_fusion
  173.5 1.9 fusion.124
  175.3 1.6 convolution_convert_fusion.grad_ref
  176.9 24.6 %attend_back.1 = (bf16[416,768]{1,0:T(8,128)(2,1)}, bf16[416,768]{1,0:T(8,128)(2,1)}, bf16[416,768]{1,0:T(8,128)(2,1)}, f32[64,128]{1,0:T(8,128)}) custom-call(bf16[416,2304]{1,0:T(8,128)(2,1)} %fusion.25.q_ref.k_ref.v_ref, bf16[416,2304]{1,0:T(8,128)(2,1)} %fusion.25.q_ref.k_ref.v_ref, bf16[416,2304]{1,0:T(8,128)(2,1)} %fusion.25.q_ref.k_ref.v_ref, ...), custom_call_target="tpu_custom_call" | custom-call | tf_op jit(solution)/shard_map/attend_back/pallas_call | solution.py:191
  202.9 6.0 %fusion.120 = (f32[768]{0:T(1024)S(1)}, f32[768]{0:T(1024)S(1)}, f32[416]{0:T(512)S(1)}, f32[416]{0:T(512)S(1)}, f32[416,768]{1,0:T(8,128)}) fusion(f32[416]{0:T(512)S(1)} %rsqrt.22, f32[416]{0:T(512)S(1)} %div.133, bf16[2,196,768]{2,1,0:T(8,128)(2,1)S(1)} %get-tuple-element.117, f32[416,768]{1,0:T(8,128)} %fusion.66, f32[768]{0:T(1024)S(1)} %get-tuple-element.68, ...), kind=kOutput, calls=%fused_computation.279 | convolution fusion | flops 1481463552 | bytes 8631424 | tf_op jit(solution)/shard_map/nf,df->nd/dot_general | solution.py:478
  209.6 3.0 multiply_convert_fusion
  212.5 34.9 %pack_grads.1 = (bf16[2,2,2,2,592,128]{5,4,3,2,1,0:T(8,128)(2,1)}, bf16[2,2,2,2,576,128]{5,4,3,2,1,0:T(8,128)(2,1)}, bf16[2,2,2,2,576,128]{5,4,3,2,1,0:T(8,128)(...) custom-call(bf16[416,768]{1,0:T(8,128)(2,1)} %get-tuple-element.93.n, ...), custom_call_target="tpu_custom_call" | custom-call | tf_op jit(solution)/shard_map/pack_grads/pallas_call | solution.py:377
  248.4 3.9 collective-permute-done.13
  252.3 2.4 add_convert_fusion.5
  256.8 2.3 collective-permute-done.8
  260.3 22.6 %collective-permute-done.14 = bf16[2,2,2,576,128]{4,3,2,1,0:T(8,128)(2,1)S(1)} collective-permute-done((bf16[2,2,2,576,128]{4,3,2,1,0:T(8,128)(2,1)S(1)}, bf16[2,2,2,576,128]{4,3,2,1,0:T(8,128)(2,1)S(1)}, u32[]{:S(2)}, u32[]{:S(2)}) %collective-permute-start.14) | collective-permute-done | bytes 1179680 | tf_op jit(solution)/shard_map/ppermute | solution.py:505
  285.5 3.9 collective-permute-done.9
  290.3 7.8 %collective-permute-done.15 = bf16[2,2,576,128]{3,2,1,0:T(8,128)(2,1)S(1)} collective-permute-done((bf16[2,2,576,128]{3,2,1,0:T(8,128)(2,1)S(1)}, bf16[2,2,576,128]{3,2,1,0:T(8,128)(2,1)S(1)}, u32[]{:S(2)}, u32[]{:S(2)}) %collective-permute-start.15) | collective-permute-done | bytes 589856 | tf_op jit(solution)/shard_map/ppermute | solution.py:505
  298.9 3.1 collective-permute-done.20
  302.8 1.9 collective-permute-done.10
  305.5 2.2 collective-permute-done.16
  307.8 2.7 collective-permute-start.17
  310.6 2.7 collective-permute-start.22
  313.3 4.3 collective-permute-start.12
  317.6 6.6 %collective-permute-done.17 = bf16[576,128]{1,0:T(8,128)(2,1)S(1)} collective-permute-done((bf16[576,128]{1,0:T(8,128)(2,1)S(1)}, bf16[576,128]{1,0:T(8,128)(2,1)S(1)}, u32[]{:S(2)}, u32[]{:S(2)}) %collective-permute-start.17) | collective-permute-done | bytes 147488 | tf_op jit(solution)/shard_map/ppermute | solution.py:505
  324.3 3.1 collective-permute-done.22
  327.5 2.5 collective-permute-done.12
  330.9 1.3 copy.34
  332.2 5.3 %fusion.65 = bf16[416,768]{1,0:T(8,128)(2,1)S(1)} fusion(f32[416,768]{1,0:T(8,128)S(1)} %get-tuple-element.105, bf16[416,3072]{1,0:T(8,128)(2,1)} %get-tuple-element.106.act_ref, bf16[3072,768]{1,0:T(8,128)(2,1)} %reshape.659, f32[768]{0:T(1024)S(1)} %get-tuple-element.61, f32[416]{0:T(512)S(1)} %mul.382), kind=kOutput, calls=%fused_computation.97 | convolution fusion | flops 1964212224 | bytes 9196160 | tf_op jit(solution)/shard_map/dot_general | solution.py:455
  337.5 1.3 copy.35
  338.8 57.0 %all-gather.2.cloned.1.call-done = bf16[27904,128]{1,0:T(8,128)(2,1)} async-done(((bf16[1744,128]{1,0:T(8,128)(2,1)}), bf16[27904,128]{1,0:T(8,128)(2,1)}) %all-gather.2.cloned.1.call-update) | async-done | bytes 7143440 | tf_op jit(solution)/shard_map/all_gather | solution.py:621
  395.8 3.9 slice.376
  399.7 9.0 %fusion.56 = (bf16[3464,128]{1,0:T(8,128)(2,1)S(1)}, bf16[3464,128]{1,0:T(8,128)(2,1)}) fusion(f32[8,3464,128]{2,1,0:T(8,128)} %bitcast.334, s32[]{:T(128)S(6)} %select_n.199, f32[8,3464,128]{2,1,0:T(8,128)} %bitcast.321, f32[8,3464,128]{2,1,0:T(8,128)} %bitcast.318, bf16[8,3464,128]{2,1,0:T(8,128)(2,1)S(1)} %bitcast.329, s32[]{:T(128)S(6)} %select_n.198), kind=kLoop, calls=%fused_computation.88 | loop fusion | flops 15962112 | bytes 14188552 | tf_op jit(solution)/shard_map/convert_element_type | solution.py:642
  408.7 1.5 collective-permute-start.23
  410.2 17.5 %fusion = (f32[27712,128]{1,0:T(8,128)}, f32[27712,128]{1,0:T(8,128)}) fusion(f32[27712,128]{1,0:T(8,128)} %param.10, bf16[27904,128]{1,0:T(8,128)(2,1)S(1)} %bitcast.333), kind=kLoop, calls=%fused_computation.5 | loop fusion | flops 17735680 | bytes 49659904 | tf_op jit(solution)/shard_map/add | solution.py:574
  428.3 2.4 collective-permute-done.23
  431.2 1.5 collective-permute-start.25
  432.8 30.6 %fusion.121 = (bf16[27712,128]{1,0:T(8,128)(2,1)}, f32[27712,128]{1,0:T(8,128)}, f32[27712,128]{1,0:T(8,128)}) fusion(f32[27712,128]{1,0:T(8,128)S(1)} %bitcast.320, bf16[27712,128]{1,0:T(8,128)(2,1)} %copy-done, f32[27712,128]{1,0:T(8,128)} %param.10, f32[27712,128]{1,0:T(8,128)} %param.11), kind=kLoop, calls=%fused_computation.280 | loop fusion | flops 63848448 | bytes 85131264 | tf_op jit(solution)/shard_map/convert_element_type | solution.py:638
  463.4 6.5 %constant_dynamic-update-slice_fusion = bf16[2,8,3464,128]{3,2,1,0:T(8,128)(2,1)} fusion(bf16[2,8,3464,128]{3,2,1,0:T(8,128)(2,1)} %bitcast_dynamic-update-slice_fusion.8, bf16[1,8,3464,128]{3,2,1,0:T(8,128)(2,1)} %bitcast.331, s32[]{:T(128)S(6)} %select_n.197), kind=kLoop, calls=%fused_computation.224 | loop fusion | bytes 14188548 | tf_op jit(solution)/shard_map/dynamic_update_slice | solution.py:533
  469.9 1.5 collective-permute-start.26
  471.4 2.1 bitcast_dynamic-update-slice_fusion.7
  473.7 2.1 bitcast_dynamic-update-slice_fusion.6
  476.2 2.1 bitcast_dynamic-update-slice_fusion.5
  478.3 13.7 %collective-permute-done.26 = bf16[3464,128]{1,0:T(8,128)(2,1)S(1)} collective-permute-done((bf16[3464,128]{1,0:T(8,128)(2,1)S(1)}, bf16[3464,128]{1,0:T(8,128)(2,1)S(1)}, u32[]{:S(2)}, u32[]{:S(2)}) %collective-permute-start.26) | collective-permute-done | bytes 886816 | tf_op jit(solution)/shard_map/ppermute | solution.py:505
  493.0 2.1 bitcast_dynamic-update-slice_fusion.3
  (166 shorter events, 35.5 us)
Async XLA Ops:
  7.2 388.6 %all-gather.2.cloned.1.call-start = ((), (), s32[]{:S(2)}) async-start(), calls=%async_computation | async-start | bytes 7589888 | tf_op jit(solution)/shard_map/all_gather | solution.py:621
  10.4 30.8 %collective-permute-start = (bf16[3464,128]{1,0:T(8,128)(2,1)}, bf16[3464,128]{1,0:T(8,128)(2,1)S(1)}, u32[]{:S(2)}, u32[]{:S(2)}) collective-permute-start(bf16[3464,128]{1,0:T(8,128)(2,1)} %get-tuple-element.71), channel_id=1, source_target_pairs={{0,1},{1,0},{2,3},{3,2},{4,5},{5,4},{6,7},{7,6},{8,9},{9,8},{10,11... | collective-permute-start | bytes 2660360 | tf_op jit(solution)/shard_map/ppermute | solution.py:505
  13.4 7.9 %copy-start.10 = (s32[2,1]{0,1:T(1,128)S(1)}, s32[2,1]{0,1:T(1,128)}, u32[]{:S(2)}) copy-start(s32[2,1]{0,1:T(1,128)} %param.8) | copy-start | bytes 28
  41.2 21.2 %collective-permute-start.1 = (bf16[3464,128]{1,0:T(8,128)(2,1)S(1)}, bf16[3464,128]{1,0:T(8,128)(2,1)S(1)}, u32[]{:S(2)}, u32[]{:S(2)}) collective-permute-start(bf16[3464,128]{1,0:T(8,128)(2,1)S(1)} %collective-permute-done), channel_id=1, source_target_pairs={{0,4},{2,6},{4,0},{6,2},{8,12},{10,14},{12,8},{14,10},{16,20},{18,... | collective-permute-start | bytes 2660360 | tf_op jit(solution)/shard_map/ppermute | solution.py:505
  42.7 20.9 %collective-permute-start.2 = (bf16[3464,128]{1,0:T(8,128)(2,1)S(1)}, bf16[3464,128]{1,0:T(8,128)(2,1)S(1)}, u32[]{:S(2)}, u32[]{:S(2)}) collective-permute-start(bf16[3464,128]{1,0:T(8,128)(2,1)S(1)} %collective-permute-done), channel_id=1, source_target_pairs={{0,8},{2,10},{4,12},{6,14},{8,0},{10,2},{12,4},{14,6},{16,24},{18,... | collective-permute-start | bytes 2660360 | tf_op jit(solution)/shard_map/ppermute | solution.py:505
  44.3 25.0 %collective-permute-start.4 = (bf16[3464,128]{1,0:T(8,128)(2,1)S(1)}, bf16[3464,128]{1,0:T(8,128)(2,1)S(1)}, u32[]{:S(2)}, u32[]{:S(2)}) collective-permute-start(bf16[3464,128]{1,0:T(8,128)(2,1)S(1)} %collective-permute-done), channel_id=1, source_target_pairs={{0,2},{2,0},{4,6},{6,4},{8,10},{10,8},{12,14},{14,12},{16,18},{18,... | collective-permute-start | bytes 2660360 | tf_op jit(solution)/shard_map/ppermute | solution.py:505
  44.3 22.1 %collective-permute-start.3 = (bf16[3464,128]{1,0:T(8,128)(2,1)S(1)}, bf16[3464,128]{1,0:T(8,128)(2,1)S(1)}, u32[]{:S(2)}, u32[]{:S(2)}) collective-permute-start(bf16[3464,128]{1,0:T(8,128)(2,1)S(1)} %get-tuple-element.27), channel_id=1, source_target_pairs={{0,1},{1,0},{2,3},{3,2},{4,5},{5,4},{6,7},{7,6},{8,9},{9,8},{10,11... | collective-permute-start | bytes 2660360 | tf_op jit(solution)/shard_map/ppermute | solution.py:505
  62.4 7.9 %collective-permute-start.5 = (bf16[3464,128]{1,0:T(8,128)(2,1)S(1)}, bf16[3464,128]{1,0:T(8,128)(2,1)S(1)}, u32[]{:S(2)}, u32[]{:S(2)}) collective-permute-start(bf16[3464,128]{1,0:T(8,128)(2,1)S(1)} %collective-permute-done.1), channel_id=1, source_target_pairs={{0,2},{2,0},{4,6},{6,4},{8,10},{10,8},{12,14},{14,12},{16,18},{18,... | collective-permute-start | bytes 2660360 | tf_op jit(solution)/shard_map/ppermute | solution.py:505
  63.6 7.7 %collective-permute-start.6 = (bf16[3464,128]{1,0:T(8,128)(2,1)S(1)}, bf16[3464,128]{1,0:T(8,128)(2,1)S(1)}, u32[]{:S(2)}, u32[]{:S(2)}) collective-permute-start(bf16[3464,128]{1,0:T(8,128)(2,1)S(1)} %collective-permute-done.2), channel_id=1, source_target_pairs={{0,2},{2,0},{4,6},{6,4},{8,10},{10,8},{12,14},{14,12},{16,18},{18,... | collective-permute-start | bytes 2660360 | tf_op jit(solution)/shard_map/ppermute | solution.py:505
  66.4 5.8 %collective-permute-start.7 = (bf16[3464,128]{1,0:T(8,128)(2,1)S(1)}, bf16[3464,128]{1,0:T(8,128)(2,1)S(1)}, u32[]{:S(2)}, u32[]{:S(2)}) collective-permute-start(bf16[3464,128]{1,0:T(8,128)(2,1)S(1)} %collective-permute-done.3), channel_id=1, source_target_pairs={{0,2},{2,0},{4,6},{6,4},{8,10},{10,8},{12,14},{14,12},{16,18},{18,... | collective-permute-start | bytes 2660360 | tf_op jit(solution)/shard_map/ppermute | solution.py:505
  151.7 15.4 %slice-start.6 = ((s8[4718592]{0:T(1024)(128)(4,1)}), s8[4194304]{0:T(1024)(128)(4,1)S(1)}, s32[]{:S(2)}) async-start(s8[4718592]{0:T(1024)(128)(4,1)} %bitcast.336), calls=%async_computation.7 | async-start | bytes 8388608
  151.7 19.0 %slice-start.8 = ((s8[4718592]{0:T(1024)(128)(4,1)}), s8[4194304]{0:T(1024)(128)(4,1)S(1)}, s32[]{:S(2)}) async-start(s8[4718592]{0:T(1024)(128)(4,1)} %bitcast.338), calls=%async_computation.9 | async-start | bytes 8388608
  152.0 15.1 %copy-start.4 = (bf16[416,768]{1,0:T(8,128)(2,1)}, bf16[416,768]{1,0:T(8,128)(2,1)S(1)}, u32[]{:S(2)}) copy-start(bf16[416,768]{1,0:T(8,128)(2,1)S(1)} %add_convert_fusion.7.n2_ref) | copy-start | bytes 1916932
  152.0 15.1 %slice-start.7 = ((s8[4718592]{0:T(1024)(128)(4,1)}), s8[524288]{0:T(1024)(128)(4,1)S(1)}, s32[]{:S(2)}) async-start(s8[4718592]{0:T(1024)(128)(4,1)} %bitcast.336), calls=%async_computation.8 | async-start | bytes 1048576
  152.0 18.7 %slice-start.9 = ((s8[4718592]{0:T(1024)(128)(4,1)}), s8[524288]{0:T(1024)(128)(4,1)S(1)}, s32[]{:S(2)}) async-start(s8[4718592]{0:T(1024)(128)(4,1)} %bitcast.338), calls=%async_computation.10 | async-start | bytes 1048576
  170.8 2.6 copy-start.5
  173.4 1.9 copy-start.2
  175.3 1.6 copy-start.3
  202.9 6.7 %copy-start.1 = (f32[416,768]{1,0:T(8,128)S(1)}, f32[416,768]{1,0:T(8,128)}, u32[]{:S(2)}) copy-start(f32[416,768]{1,0:T(8,128)} %get-tuple-element.58) | copy-start | bytes 3833860
  247.5 4.8 collective-permute-start.13
  247.9 7.8 %collective-permute-start.18 = (bf16[2,2,2,2,576,128]{5,4,3,2,1,0:T(8,128)(2,1)}, bf16[2,2,2,2,576,128]{5,4,3,2,1,0:T(8,128)(2,1)S(1)}, u32[]{:S(2)}, u32[]{:S(2)}) collective-permute-start(bf16[2,2,2,2,576,128]{5,4,3,2,1,0:T(8,128)(2,1)} %get-tuple-element.39), channel_id=1, source_target_pairs={{0,2},{2,0},{4,6},{6,4},{8,10},{10,8},{12,14},{14,12},{16,18},{18,... | collective-permute-start | bytes 7077896 | tf_op jit(solution)/shard_map/ppermute | solution.py:505
  248.0 11.1 %collective-permute-start.8 = (bf16[2,2,2,2,592,128]{5,4,3,2,1,0:T(8,128)(2,1)}, bf16[2,2,2,2,592,128]{5,4,3,2,1,0:T(8,128)(2,1)S(1)}, u32[]{:S(2)}, u32[]{:S(2)}) collective-permute-start(bf16[2,2,2,2,592,128]{5,4,3,2,1,0:T(8,128)(2,1)} %get-tuple-element.35), channel_id=1, source_target_pairs={{0,2},{2,0},{4,6},{6,4},{8,10},{10,8},{12,14},{14,12},{16,18},{18,... | collective-permute-start | bytes 7274504 | tf_op jit(solution)/shard_map/ppermute | solution.py:505
  252.3 3.4 copy-start.8
  254.7 28.3 %collective-permute-start.14 = (bf16[2,2,2,576,128]{4,3,2,1,0:T(8,128)(2,1)S(1)}, bf16[2,2,2,576,128]{4,3,2,1,0:T(8,128)(2,1)S(1)}, u32[]{:S(2)}, u32[]{:S(2)}) collective-permute-start(bf16[2,2,2,576,128]{4,3,2,1,0:T(8,128)(2,1)S(1)} %get-tuple-element.78), channel_id=1, source_target_pairs={{0,4},{2,6},{4,0},{6,2},{8,12},{10,14},{12,8},{14,10},{16,20},{18,... | collective-permute-start | bytes 3538952 | tf_op jit(solution)/shard_map/ppermute | solution.py:505
  255.6 3.5 copy-start.7
  256.3 28.3 %collective-permute-start.19 = (bf16[2,2,2,576,128]{4,3,2,1,0:T(8,128)(2,1)S(1)}, bf16[2,2,2,576,128]{4,3,2,1,0:T(8,128)(2,1)S(1)}, u32[]{:S(2)}, u32[]{:S(2)}) collective-permute-start(bf16[2,2,2,576,128]{4,3,2,1,0:T(8,128)(2,1)S(1)} %get-tuple-element.80), channel_id=1, source_target_pairs={{0,8},{2,10},{4,12},{6,14},{8,0},{10,2},{12,4},{14,6},{16,24},{18,... | collective-permute-start | bytes 3538952 | tf_op jit(solution)/shard_map/ppermute | solution.py:505
  259.7 29.6 %collective-permute-start.9 = (bf16[2,2,2,592,128]{4,3,2,1,0:T(8,128)(2,1)S(1)}, bf16[2,2,2,592,128]{4,3,2,1,0:T(8,128)(2,1)S(1)}, u32[]{:S(2)}, u32[]{:S(2)}) collective-permute-start(bf16[2,2,2,592,128]{4,3,2,1,0:T(8,128)(2,1)S(1)} %get-tuple-element.76), channel_id=1, source_target_pairs={{0,1},{1,0},{2,3},{3,2},{4,5},{5,4},{6,7},{7,6},{8,9},{9,8},{10,11... | collective-permute-start | bytes 3637256 | tf_op jit(solution)/shard_map/ppermute | solution.py:505
  283.3 14.8 %collective-permute-start.15 = (bf16[2,2,576,128]{3,2,1,0:T(8,128)(2,1)S(1)}, bf16[2,2,576,128]{3,2,1,0:T(8,128)(2,1)S(1)}, u32[]{:S(2)}, u32[]{:S(2)}) collective-permute-start(bf16[2,2,576,128]{3,2,1,0:T(8,128)(2,1)S(1)} %get-tuple-element.84), channel_id=1, source_target_pairs={{0,8},{2,10},{4,12},{6,14},{8,0},{10,2},{12,4},{14,6},{16,24},{18,... | collective-permute-start | bytes 1769480 | tf_op jit(solution)/shard_map/ppermute | solution.py:505
  284.9 17.1 %collective-permute-start.20 = (bf16[2,2,576,128]{3,2,1,0:T(8,128)(2,1)S(1)}, bf16[2,2,576,128]{3,2,1,0:T(8,128)(2,1)S(1)}, u32[]{:S(2)}, u32[]{:S(2)}) collective-permute-start(bf16[2,2,576,128]{3,2,1,0:T(8,128)(2,1)S(1)} %get-tuple-element.86), channel_id=1, source_target_pairs={{0,1},{1,0},{2,3},{3,2},{4,5},{5,4},{6,7},{7,6},{8,9},{9,8},{10,11... | collective-permute-start | bytes 1769480 | tf_op jit(solution)/shard_map/ppermute | solution.py:505
  289.7 15.0 %collective-permute-start.10 = (bf16[2,2,592,128]{3,2,1,0:T(8,128)(2,1)S(1)}, bf16[2,2,592,128]{3,2,1,0:T(8,128)(2,1)S(1)}, u32[]{:S(2)}, u32[]{:S(2)}) collective-permute-start(bf16[2,2,592,128]{3,2,1,0:T(8,128)(2,1)S(1)} %get-tuple-element.82), channel_id=1, source_target_pairs={{0,4},{2,6},{4,0},{6,2},{8,12},{10,14},{12,8},{14,10},{16,20},{18,... | collective-permute-start | bytes 1818632 | tf_op jit(solution)/shard_map/ppermute | solution.py:505
  298.2 9.5 %collective-permute-start.16 = (bf16[2,576,128]{2,1,0:T(8,128)(2,1)S(1)}, bf16[2,576,128]{2,1,0:T(8,128)(2,1)S(1)}, u32[]{:S(2)}, u32[]{:S(2)}) collective-permute-start(bf16[2,576,128]{2,1,0:T(8,128)(2,1)S(1)} %get-tuple-element.90), channel_id=1, source_target_pairs={{0,1},{1,0},{2,3},{3,2},{4,5},{5,4},{6,7},{7,6},{8,9},{9,8},{10,11... | collective-permute-start | bytes 884744 | tf_op jit(solution)/shard_map/ppermute | solution.py:505
  302.2 8.4 %collective-permute-start.21 = (bf16[2,576,128]{2,1,0:T(8,128)(2,1)S(1)}, bf16[2,576,128]{2,1,0:T(8,128)(2,1)S(1)}, u32[]{:S(2)}, u32[]{:S(2)}) collective-permute-start(bf16[2,576,128]{2,1,0:T(8,128)(2,1)S(1)} %get-tuple-element.92), channel_id=1, source_target_pairs={{0,4},{2,6},{4,0},{6,2},{8,12},{10,14},{12,8},{14,10},{16,20},{18,... | collective-permute-start | bytes 884744 | tf_op jit(solution)/shard_map/ppermute | solution.py:505
  304.9 25.9 %copy-start.6 = (bf16[416,768]{1,0:T(8,128)(2,1)S(1)}, bf16[416,768]{1,0:T(8,128)(2,1)}, u32[]{:S(2)}) copy-start(bf16[416,768]{1,0:T(8,128)(2,1)} %get-tuple-element.94) | copy-start | bytes 1916932
  304.9 8.4 %collective-permute-start.11 = (bf16[2,592,128]{2,1,0:T(8,128)(2,1)S(1)}, bf16[2,592,128]{2,1,0:T(8,128)(2,1)S(1)}, u32[]{:S(2)}, u32[]{:S(2)}) collective-permute-start(bf16[2,592,128]{2,1,0:T(8,128)(2,1)S(1)} %get-tuple-element.88), channel_id=1, source_target_pairs={{0,8},{2,10},{4,12},{6,14},{8,0},{10,2},{12,4},{14,6},{16,24},{18,... | collective-permute-start | bytes 909320 | tf_op jit(solution)/shard_map/ppermute | solution.py:505
  307.8 16.5 %collective-permute-start.17 = (bf16[576,128]{1,0:T(8,128)(2,1)S(1)}, bf16[576,128]{1,0:T(8,128)(2,1)S(1)}, u32[]{:S(2)}, u32[]{:S(2)}) collective-permute-start(bf16[576,128]{1,0:T(8,128)(2,1)S(1)} %fusion.101), channel_id=1, source_target_pairs={{0,16},{2,18},{4,20},{6,22},{8,24},{10,26},{12,28},{14,30},{16,0},... | collective-permute-start | bytes 442376 | tf_op jit(solution)/shard_map/ppermute | solution.py:505
  310.6 16.8 %collective-permute-start.22 = (bf16[576,128]{1,0:T(8,128)(2,1)S(1)}, bf16[576,128]{1,0:T(8,128)(2,1)S(1)}, u32[]{:S(2)}, u32[]{:S(2)}) collective-permute-start(bf16[576,128]{1,0:T(8,128)(2,1)S(1)} %fusion.103), channel_id=1, source_target_pairs={{0,16},{2,18},{4,20},{6,22},{8,24},{10,26},{12,28},{14,30},{16,0},... | collective-permute-start | bytes 442376 | tf_op jit(solution)/shard_map/ppermute | solution.py:505
  313.3 16.6 %collective-permute-start.12 = (bf16[592,128]{1,0:T(8,128)(2,1)S(1)}, bf16[592,128]{1,0:T(8,128)(2,1)S(1)}, u32[]{:S(2)}, u32[]{:S(2)}) collective-permute-start(bf16[592,128]{1,0:T(8,128)(2,1)S(1)} %fusion.99), channel_id=1, source_target_pairs={{0,16},{2,18},{4,20},{6,22},{8,24},{10,26},{12,28},{14,30},{16,0},... | collective-permute-start | bytes 454664 | tf_op jit(solution)/shard_map/ppermute | solution.py:505
  399.6 9.0 %copy-start = (bf16[27712,128]{1,0:T(8,128)(2,1)}, bf16[27712,128]{1,0:T(8,128)(2,1)S(1)}, u32[]{:S(2)}) copy-start(bf16[27712,128]{1,0:T(8,128)(2,1)S(1)} %slice.376) | copy-start | bytes 21282820
  399.6 10.6 %slice-start.4 = ((s8[7143424]{0:T(1024)(128)(4,1)}), s8[4194304]{0:T(1024)(128)(4,1)S(1)}, s32[]{:S(2)}) async-start(s8[7143424]{0:T(1024)(128)(4,1)} %bitcast.332), calls=%async_computation.5 | async-start | bytes 8388608
  399.7 10.6 %slice-start.5 = ((s8[7143424]{0:T(1024)(128)(4,1)}), s8[2949120]{0:T(1024)(128)(4,1)S(1)}, s32[]{:S(2)}) async-start(s8[7143424]{0:T(1024)(128)(4,1)} %bitcast.332), calls=%async_computation.6 | async-start | bytes 5898240
  408.6 24.1 %slice-start = ((s8[14188544]{0:T(1024)(128)(4,1)}), s8[4194304]{0:T(1024)(128)(4,1)S(1)}, s32[]{:S(2)}) async-start(s8[14188544]{0:T(1024)(128)(4,1)} %bitcast.319), calls=%async_computation.1 | async-start | bytes 8388608
  408.6 24.1 %slice-start.1 = ((s8[14188544]{0:T(1024)(128)(4,1)}), s8[4194304]{0:T(1024)(128)(4,1)S(1)}, s32[]{:S(2)}) async-start(s8[14188544]{0:T(1024)(128)(4,1)} %bitcast.319), calls=%async_computation.2 | async-start | bytes 8388608
  408.6 24.1 %slice-start.2 = ((s8[14188544]{0:T(1024)(128)(4,1)}), s8[4194304]{0:T(1024)(128)(4,1)S(1)}, s32[]{:S(2)}) async-start(s8[14188544]{0:T(1024)(128)(4,1)} %bitcast.319), calls=%async_computation.3 | async-start | bytes 8388608
  408.7 24.1 %slice-start.3 = ((s8[14188544]{0:T(1024)(128)(4,1)}), s8[1605632]{0:T(1024)(128)(4,1)S(1)}, s32[]{:S(2)}) async-start(s8[14188544]{0:T(1024)(128)(4,1)} %bitcast.319), calls=%async_computation.4 | async-start | bytes 3211264
  408.7 22.0 %collective-permute-start.23 = (bf16[3464,128]{1,0:T(8,128)(2,1)S(1)}, bf16[3464,128]{1,0:T(8,128)(2,1)}, u32[]{:S(2)}, u32[]{:S(2)}) collective-permute-start(bf16[3464,128]{1,0:T(8,128)(2,1)S(1)} %get-tuple-element.59), channel_id=1, source_target_pairs={{0,1},{1,0},{2,3},{3,2},{4,5},{5,4},{6,7},{7,6},{8,9},{9,8},{10,11... | collective-permute-start | bytes 2660360 | tf_op jit(solution)/shard_map/ppermute | solution.py:505
  430.7 42.8 %collective-permute-start.24 = (bf16[3464,128]{1,0:T(8,128)(2,1)}, bf16[3464,128]{1,0:T(8,128)(2,1)}, u32[]{:S(2)}, u32[]{:S(2)}) collective-permute-start(bf16[3464,128]{1,0:T(8,128)(2,1)} %collective-permute-done.23), channel_id=1, source_target_pairs={{0,4},{2,6},{4,0},{6,2},{8,12},{10,14},{12,8},{14,10},{16,20},{18,... | collective-permute-start | bytes 2660360 | tf_op jit(solution)/shard_map/ppermute | solution.py:505
  431.2 44.7 %collective-permute-start.25 = (bf16[3464,128]{1,0:T(8,128)(2,1)}, bf16[3464,128]{1,0:T(8,128)(2,1)}, u32[]{:S(2)}, u32[]{:S(2)}) collective-permute-start(bf16[3464,128]{1,0:T(8,128)(2,1)} %collective-permute-done.23), channel_id=1, source_target_pairs={{0,8},{2,10},{4,12},{6,14},{8,0},{10,2},{12,4},{14,6},{16,24},{18,... | collective-permute-start | bytes 2660360 | tf_op jit(solution)/shard_map/ppermute | solution.py:505
  432.8 60.2 %collective-permute-start.27 = (bf16[3464,128]{1,0:T(8,128)(2,1)}, bf16[3464,128]{1,0:T(8,128)(2,1)}, u32[]{:S(2)}, u32[]{:S(2)}) collective-permute-start(bf16[3464,128]{1,0:T(8,128)(2,1)} %collective-permute-done.23), channel_id=1, source_target_pairs={{0,2},{2,0},{4,6},{6,4},{8,10},{10,8},{12,14},{14,12},{16,18},{18,... | collective-permute-start | bytes 2660360 | tf_op jit(solution)/shard_map/ppermute | solution.py:505
  463.4 6.5 %copy-start.9 = (bf16[3464,128]{1,0:T(8,128)(2,1)S(1)}, bf16[3464,128]{1,0:T(8,128)(2,1)}, u32[]{:S(2)}) copy-start(bf16[3464,128]{1,0:T(8,128)(2,1)} %get-tuple-element.43) | copy-start | bytes 2660356
  469.9 22.1 %collective-permute-start.26 = (bf16[3464,128]{1,0:T(8,128)(2,1)S(1)}, bf16[3464,128]{1,0:T(8,128)(2,1)S(1)}, u32[]{:S(2)}, u32[]{:S(2)}) collective-permute-start(bf16[3464,128]{1,0:T(8,128)(2,1)S(1)} %copy-done.9), channel_id=1, source_target_pairs={{0,1},{1,0},{2,3},{3,2},{4,5},{5,4},{6,7},{7,6},{8,9},{9,8},{10,11... | collective-permute-start | bytes 2660360 | tf_op jit(solution)/shard_map/ppermute | solution.py:505
  473.5 21.6 %collective-permute-start.28 = (bf16[3464,128]{1,0:T(8,128)(2,1)}, bf16[3464,128]{1,0:T(8,128)(2,1)S(1)}, u32[]{:S(2)}, u32[]{:S(2)}) collective-permute-start(bf16[3464,128]{1,0:T(8,128)(2,1)} %collective-permute-done.24), channel_id=1, source_target_pairs={{0,2},{2,0},{4,6},{6,4},{8,10},{10,8},{12,14},{14,12},{16,18},{18,... | collective-permute-start | bytes 2660360 | tf_op jit(solution)/shard_map/ppermute | solution.py:505
  475.9 20.2 %collective-permute-start.29 = (bf16[3464,128]{1,0:T(8,128)(2,1)}, bf16[3464,128]{1,0:T(8,128)(2,1)S(1)}, u32[]{:S(2)}, u32[]{:S(2)}) collective-permute-start(bf16[3464,128]{1,0:T(8,128)(2,1)} %collective-permute-done.25), channel_id=1, source_target_pairs={{0,2},{2,0},{4,6},{6,4},{8,10},{10,8},{12,14},{14,12},{16,18},{18,... | collective-permute-start | bytes 2660360 | tf_op jit(solution)/shard_map/ppermute | solution.py:505
  492.0 5.1 %collective-permute-start.30 = (bf16[3464,128]{1,0:T(8,128)(2,1)S(1)}, bf16[3464,128]{1,0:T(8,128)(2,1)S(1)}, u32[]{:S(2)}, u32[]{:S(2)}) collective-permute-start(bf16[3464,128]{1,0:T(8,128)(2,1)S(1)} %collective-permute-done.26), channel_id=1, source_target_pairs={{0,2},{2,0},{4,6},{6,4},{8,10},{10,8},{12,14},{14,12},{16,18},{18,... | collective-permute-start | bytes 2660360 | tf_op jit(solution)/shard_map/ppermute | solution.py:505
Sparse Core Ops, SparseCore 0:
  330.9 64.7 all-gather.1
